TPU v7x, 512 devices: a whole 4x4x16 slice. The times are simulated.
512 devices in a mesh: seq: 32 (over y, x, core), tp: 16 (over z).
Axes of the slice: x: 4, y: 4, z: 16, core: 2. Of those that a mesh axis runs over, the one named last changes fastest.
Arguments:
- tokens: bfloat16 [4096, 4096], P('seq', 'tp'), may hold values from -6 to 6
- in_weight: bfloat16 [4096, 8192], P(None, 'tp'), may hold values from -0.09375 to 0.09375
- conv_weight: float32 [4, 8192], P(None, 'tp'), may hold values from -3 to 3
- conv_bias: float32 [8192], P('tp'), may hold values from -0.5 to 0.5
- proj_weight: bfloat16 [8192, 288], P('tp'), may hold values from -0.0625 to 0.0625
- dt_weight: bfloat16 [256, 8192], P(None, 'tp'), may hold values from -0.375 to 0.375
- dt_bias: float32 [8192], P('tp'), may hold values from -7 to -2
- a_log: float32 [16, 8192], P(None, 'tp'), may hold values from -3 to 1.5
- skip_gain: float32 [8192], P('tp'), may hold values from 0.5 to 1.5
- threshold: float32 [8192], P('tp'), may hold values from -0.5 to 0.5
Outputs:
- gated: bfloat16 [4096, 8192], P('seq', 'tp')
All inputs are finite; a program needn't handle non-finite values.
Results may differ from a plain program's by a relative error of at most 0.0085.
Values may be sent and summed in bfloat16 or wider, within the bound.
No kernel may reach another device: no remote copies, remote signals or barrier semaphores. Data moves between devices by JAX's collectives and lax.ppermute only.
A program may use at most 64 MiB of HBM per device.

v0:
```python
import math

import jax
import jax.numpy as jnp
from jax import lax
from jax.sharding import PartitionSpec as P


def shifted(x, axis, by):
    peers = lax.axis_size(axis)
    pairs = [(i, i + by) for i in range(peers) if 0 <= i + by < peers]
    return lax.ppermute(x, axis, pairs)


def carried_in(value, axis, join, neutral):
    count, mine = (lax.axis_size(axis), lax.axis_index(axis))
    pieces = jax.tree.map(lambda part: lax.all_gather(part, axis), value)
    total = jax.tree.map(
        lambda part, zero: jnp.full_like(part, 0) + jnp.asarray(zero, part.dtype), value, neutral
    )

    def turn(position, total):
        longer = join(total, jax.tree.map(lambda part: part[position], pieces))
        return jax.tree.map(lambda new, old: jnp.where(position < mine, new, old), longer, total)

    return lax.fori_loop(0, count - 1, turn, total)


def combine_pair(earlier, later):
    return (earlier[0] * later[0], later[0] * earlier[1] + later[1])


def lower_table(rows):
    row_ids = lax.broadcasted_iota(jnp.int32, (rows, rows), 0)
    col_ids = lax.broadcasted_iota(jnp.int32, (rows, rows), 1)
    return row_ids >= col_ids


def local_pass(step_size, inflow_rows, b_coef, c_coef, rate, start_state, block):
    rows, width = step_size.shape
    count = rows // block
    lower = lower_table(block)
    lower_float = lower.astype(jnp.float32)

    def run(carry, items):
        state, decay_all = carry
        step_block, flow_block, b_block, c_block = items
        summed = jnp.dot(
            lower_float,
            step_block,
            precision=lax.Precision.HIGHEST,
            preferred_element_type=jnp.float32,
        )
        diff = jnp.where(lower[:, :, None], summed[:, None, :] - summed[None, :, :], 0.0)
        weights = jnp.where(
            lower[:, :, None, None], jnp.exp(diff[:, :, None, :] * rate[None, None]), 0.0
        )
        inflow = flow_block[:, None, :] * b_block[:, :, None]
        states = jnp.einsum("tsnc,snc->tnc", weights, inflow, precision=lax.Precision.HIGHEST)
        states = states + jnp.exp(summed[:, None, :] * rate[None]) * state[None]
        outputs = jnp.einsum("tn,tnc->tc", c_block, states, precision=lax.Precision.HIGHEST)
        block_decay = jnp.exp(summed[-1][None, :] * rate)
        return ((states[-1], block_decay * decay_all), outputs)

    items = (
        step_size.reshape(count, block, width),
        inflow_rows.reshape(count, block, width),
        b_coef.reshape(count, block, -1),
        c_coef.reshape(count, block, -1),
    )
    (end_state, decay_all), outputs = lax.scan(
        run, (start_state, jnp.ones_like(start_state)), items
    )
    return (end_state, decay_all, outputs.reshape(rows, width))


def per_device(
    tokens,
    in_weight,
    conv_weight,
    conv_bias,
    proj_weight,
    dt_weight,
    dt_bias,
    a_log,
    skip_gain,
    threshold,
):
    tok_rows = tokens.shape[0]
    width = in_weight.shape[1]
    taps = conv_weight.shape[0]
    rank = dt_weight.shape[0]
    states_n = a_log.shape[0]
    projected = jnp.dot(
        lax.all_gather(tokens, "tp", axis=1, tiled=True),
        in_weight,
        preferred_element_type=jnp.float32,
    ).astype(jnp.bfloat16)
    rim_inner = shifted(projected[tok_rows - taps + 1 :], "seq", 1)
    padded = jnp.concatenate([rim_inner, projected], axis=0)
    pre = conv_bias[None, :] + jnp.zeros((tok_rows, width), jnp.float32)
    for k in range(taps):
        pre = pre + conv_weight[k][None, :] * padded[k : k + tok_rows].astype(jnp.float32)
    u_half = jax.nn.silu(pre).astype(jnp.bfloat16)
    partial_sums = jnp.dot(u_half, proj_weight, preferred_element_type=jnp.float32)
    total = lax.psum(partial_sums, "tp")
    dt_low = total[:, :rank].astype(jnp.bfloat16)
    b_coef = total[:, rank : rank + states_n]
    c_coef = total[:, rank + states_n :]
    step_size = jax.nn.softplus(
        jnp.dot(dt_low, dt_weight, preferred_element_type=jnp.float32) + dt_bias[None, :]
    )
    rate = -jnp.exp(a_log)
    u_float = u_half.astype(jnp.float32)
    inflow_rows = step_size * u_float
    block = math.gcd(tok_rows, 16)
    zero_state = jnp.zeros((states_n, width), jnp.float32)
    end_state, decay_all, local_out = local_pass(
        step_size, inflow_rows, b_coef, c_coef, rate, zero_state, block
    )
    incoming = carried_in(
        (decay_all, end_state), "seq", combine_pair, (jnp.ones_like(decay_all), zero_state)
    )
    entry_state = incoming[1]
    whole_lower = lower_table(tok_rows).astype(jnp.float32)
    summed = jnp.dot(
        whole_lower, step_size, precision=lax.Precision.HIGHEST, preferred_element_type=jnp.float32
    )
    growth = jnp.exp(summed[:, None, :] * rate[None])
    scan_out = local_out + jnp.einsum(
        "tn,tnc->tc", c_coef, growth * entry_state[None], precision=lax.Precision.HIGHEST
    )
    y_full = scan_out + skip_gain[None, :] * u_float
    return (y_full * jax.nn.sigmoid(4.0 * (y_full - threshold[None, :]))).astype(jnp.bfloat16)


def solution(mesh):
    return jax.shard_map(
        per_device,
        mesh=mesh,
        in_specs=(
            P("seq", "tp"),
            P(None, "tp"),
            P(None, "tp"),
            P("tp"),
            P("tp", None),
            P(None, "tp"),
            P("tp"),
            P(None, "tp"),
            P("tp"),
            P("tp"),
        ),
        out_specs=P("seq", "tp"),
        check_vma=False,
    )
```

profile of v0, /device:TPU:1, one launch (start us, length us, event | category | flops | bytes accessed | tf_op | source)
XLA Modules:
  0.0 405.8 jit_solution(9924214870880622098)
XLA Ops:
  7.3 68.5 %all-gather.6.cloned.1.call-done = bf16[128,4096]{1,0:T(8,128)(2,1)} async-done(((bf16[128,256]{1,0:T(8,128)(2,1)}), bf16[128,4096]{1,0:T(8,128)(2,1)}) %all-gather.6.cloned.1.call-update) | async-done | bytes 1048592 | tf_op jit(solution)/shard_map/all_gather | solution.py:95
  75.8 3.2 convolution_convert_fusion
  79.1 14.8 %collective-permute-start = (bf16[3,512]{1,0:T(4,128)(2,1)S(1)}, bf16[3,512]{1,0:T(4,128)(2,1)S(1)}, u32[]{:S(2)}, u32[]{:S(2)}) collective-permute-start(bf16[3,512]{1,0:T(4,128)(2,1)S(1)} %slice.57), channel_id=1, source_target_pairs={{0,16},{16,32},{32,48},{48,64},{64,80},{80,96},{96,112},{112,128},... | collective-permute-start | bytes 9224 | tf_op jit(solution)/shard_map/ppermute | solution.py:12
  94.9 0.9 fusion.23
  95.9 121.1 %all-reduce.2.cloned.1.call-done = f32[128,288]{0,1:T(8,128)} async-done(((f32[128,288]{0,1:T(8,128)}), f32[128,288]{0,1:T(8,128)}) %all-reduce.2.cloned.1.call-update) | async-done | bytes 147472 | tf_op jit(solution)/shard_map/psum | solution.py:106
  217.9 1.3 convert_multiply_fusion.1
  219.1 25.1 %while.31 = (s32[]{:T(128)}, f32[16,512]{1,0:T(8,128)S(1)}, f32[16,512]{1,0:T(8,128)S(1)}, f32[8,16,512]{2,1,0:T(8,128)S(1)}, f32[8,16,512]{2,1,0:T(8,128)S(1)},...) while((s32[]{:T(128)}, f32[16,512]{1,0:T(8,128)S(1)}, ...), condition=%wide.region_2.3_spmd.clone.clone, body=%wide.region_1.2_spmd.clone.clone.sunk | while | flops 12215043 | bytes 4797323 | solution.py:71
  219.5 2.2 multiply_reduce_fusion.2
  222.7 2.2 multiply_reduce_fusion.2
  225.8 2.2 multiply_reduce_fusion.2
  228.9 2.2 multiply_reduce_fusion.2
  232.1 2.2 multiply_reduce_fusion.2
  235.2 2.2 multiply_reduce_fusion.2
  238.3 2.2 multiply_reduce_fusion.2
  241.5 2.2 multiply_reduce_fusion.2
  245.9 63.7 %all-gather.8.cloned.1.call-done = f32[512,512]{1,0:T(8,128)} async-done(((f32[16,512]{1,0:T(8,128)}), f32[512,512]{1,0:T(8,128)}) %all-gather.8.cloned.1.call-update) | async-done | bytes 1048592 | tf_op jit(solution)/shard_map/all_gather | solution.py:17
  309.6 61.0 %all-gather.10.cloned.1.call-done = f32[512,512]{1,0:T(8,128)} async-done(((f32[16,512]{1,0:T(8,128)}), f32[512,512]{1,0:T(8,128)}) %all-gather.10.cloned.1.call-update) | async-done | bytes 1048592 | tf_op jit(solution)/shard_map/all_gather | solution.py:17
  370.6 25.2 %while.30 = (s32[]{:T(128)}, f32[16,512]{1,0:T(8,128)S(1)}, s32[]{:T(128)}, f32[32,16,512]{2,1,0:T(8,128)}, f32[32,16,512]{2,1,0:T(8,128)}, /*index=5*/s32[]{:T(128)}, s32[]{:T(128)}) while((s32[]{:T(128)}, f32[16,512]{1,0:T(8,128)S(1)}, s32[]{:T(128)}, f32[32,16,512]{2,1,0:T(8,128)}, f32[32,16,512]{2,1,0:T(8,128)}, ...), condition=%wide.region_4.5_spmd.clone, body=%wide.region_3.4_spmd.clone.sunk | while | flops 32772 | bytes 131173 | solution.py:26
  371.4 0.8 fusion.39
  372.2 0.8 fusion.39
  373.1 0.8 fusion.39
  373.9 0.8 fusion.39
  374.7 0.8 fusion.39
  375.5 0.8 fusion.39
  376.3 0.8 fusion.39
  377.1 0.8 fusion.39
  377.9 0.8 fusion.39
  378.7 0.8 fusion.39
  379.6 0.8 fusion.39
  380.4 0.8 fusion.39
  381.2 0.8 fusion.39
  382.0 0.8 fusion.39
  382.8 0.8 fusion.39
  383.6 0.8 fusion.39
  384.4 0.8 fusion.39
  385.3 0.8 fusion.39
  386.1 0.8 fusion.39
  386.9 0.8 fusion.39
  387.7 0.8 fusion.39
  388.5 0.8 fusion.39
  389.3 0.8 fusion.39
  390.1 0.8 fusion.39
  390.9 0.8 fusion.39
  391.8 0.8 fusion.39
  392.6 0.8 fusion.39
  393.4 0.8 fusion.39
  394.2 0.8 fusion.39
  395.8 2.7 fusion.9
  (141 shorter events, 13.4 us)
Async XLA Ops:
  6.5 88.3 %copy-start = (bf16[512,288]{0,1:T(8,128)(2,1)S(1)}, bf16[512,288]{0,1:T(8,128)(2,1)}, u32[]{:S(2)}) copy-start(bf16[512,288]{0,1:T(8,128)(2,1)} %param.18) | copy-start | bytes 884740
  6.5 87.4 %copy-start.5 = (f32[4,512]{1,0:T(4,128)S(1)}, f32[4,512]{1,0:T(4,128)}, u32[]{:S(2)}) copy-start(f32[4,512]{1,0:T(4,128)} %param.16) | copy-start | bytes 24580
  6.5 88.1 %copy-start.6 = (f32[512]{0:T(512)S(1)}, f32[512]{0:T(512)}, u32[]{:S(2)}) copy-start(f32[512]{0:T(512)} %param.17) | copy-start | bytes 6148
  6.5 89.3 %copy-start.4 = (f32[16,512]{1,0:T(8,128)S(1)}, f32[16,512]{1,0:T(8,128)}, u32[]{:S(2)}) copy-start(f32[16,512]{1,0:T(8,128)} %param.21) | copy-start | bytes 98308
  6.5 211.3 %copy-start.3 = (bf16[256,512]{1,0:T(8,128)(2,1)S(1)}, bf16[256,512]{1,0:T(8,128)(2,1)}, u32[]{:S(2)}) copy-start(bf16[256,512]{1,0:T(8,128)(2,1)} %param.19) | copy-start | bytes 786436
  6.5 211.3 %copy-start.7 = (f32[512]{0:T(512)S(1)}, f32[512]{0:T(512)}, u32[]{:S(2)}) copy-start(f32[512]{0:T(512)} %param.20) | copy-start | bytes 6148
  6.6 69.3 %all-gather.6.cloned.1.call-start = ((), (), s32[]{:S(2)}) async-start(), calls=%async_computation | async-start | bytes 1114112 | tf_op jit(solution)/shard_map/all_gather | solution.py:95
  7.3 209.6 %all-reduce.2.cloned.1.call-start = ((), (), s32[]{:S(2)}) async-start(), calls=%async_computation.1 | async-start | bytes 294912 | tf_op jit(solution)/shard_map/psum | solution.py:106
  79.1 15.6 %collective-permute-start = (bf16[3,512]{1,0:T(4,128)(2,1)S(1)}, bf16[3,512]{1,0:T(4,128)(2,1)S(1)}, u32[]{:S(2)}, u32[]{:S(2)}) collective-permute-start(bf16[3,512]{1,0:T(4,128)(2,1)S(1)} %slice.57), channel_id=1, source_target_pairs={{0,16},{16,32},{32,48},{48,64},{64,80},{80,96},{96,112},{112,128},... | collective-permute-start | bytes 9224 | tf_op jit(solution)/shard_map/ppermute | solution.py:12
  95.8 213.8 %all-gather.8.cloned.1.call-start = ((), (), s32[]{:S(2)}) async-start(), calls=%async_computation.2 | async-start | bytes 1081344 | tf_op jit(solution)/shard_map/all_gather | solution.py:17
  244.2 0.6 copy-start.2
  244.2 0.7 copy-start.1
  244.2 154.3 %copy-start.8 = (f32[512]{0:T(512)S(1)}, f32[512]{0:T(512)}, u32[]{:S(2)}) copy-start(f32[512]{0:T(512)} %param.23) | copy-start | bytes 6148
  244.3 154.3 %copy-start.9 = (f32[512]{0:T(512)S(1)}, f32[512]{0:T(512)}, u32[]{:S(2)}) copy-start(f32[512]{0:T(512)} %param.22) | copy-start | bytes 6148
  244.9 125.8 %all-gather.10.cloned.1.call-start = ((), (), s32[]{:S(2)}) async-start(), calls=%async_computation.3 | async-start | bytes 1081344 | tf_op jit(solution)/shard_map/all_gather | solution.py:17
Sparse Core Ops, SparseCore 0:
  9.4 66.3 all-gather.5
  95.9 120.9 all-reduce.1
  245.0 64.5 all-gather.7
  313.1 57.5 all-gather.9
where the time goes:
time: 408 us; the launch traced here: 406 us
  waiting for transfers between devices  316 us (77%)
  other arithmetic  44.8 us (11%)
  starting transfers between devices  15 us (4%)
  between operations  13.4 us (3%)
  matrix products  12.7 us (3%)
    all_gather x2, waiting for transfers between devices, carried_in(): pieces = jax.tree.map(lambda part: lax.all_gather(part, axis), value)  125 us
    psum x1, waiting for transfers between devices, per_device(): total = lax.psum(partial_sums, 'tp')  121 us
    all_gather x1, waiting for transfers between devices, per_device(): lax.all_gather(tokens, 'tp', axis=1, tiled=True)  68.5 us
    select_n x31, other arithmetic, turn(): jnp.where(position < mine, new, old)  24.5 us
    dot_general x8, other arithmetic, run(): jnp.einsum('tsnc,snc->tnc', weights, inflow, precision=lax.Precision.HIGH...  17.3 us
    ppermute x1, starting transfers between devices, shifted(): return lax.ppermute(x, axis, pairs)  14.8 us
  transfers between devices with their start and end apart: 5, of which 5 were waited for; matrix products, arithmetic and copies ran while one was open for 0% of the time, Pallas kernels for 0%

commit v1 on v0

v1 whole, which is shorter than its diff:
```python
import math

import jax
import jax.numpy as jnp
from jax import lax
from jax.experimental import pallas as pl
from jax.experimental.pallas import tpu as pltpu
from jax.sharding import PartitionSpec as P

LOG2E = math.log2(math.e)
F32 = jnp.float32
BF16 = jnp.bfloat16
VMEM = pl.BlockSpec(memory_space=pltpu.VMEM)
SMEM = pl.BlockSpec(memory_space=pltpu.SMEM)


def struct(shape, dtype):
    return jax.ShapeDtypeStruct(shape, dtype)


def to_all(block, axis):
    peers = lax.axis_size(axis)
    return lax.all_to_all(jnp.broadcast_to(block[None], (peers,) + block.shape), axis, 0, 0)


def project_kernel(main_ref, tail_ref, weight_ref, inner_ref):
    shards, rows, depth = main_ref.shape
    tail_rows = tail_ref.shape[1]
    width = weight_ref.shape[1]
    acc = jnp.zeros((rows, width), F32)
    acc_tail = jnp.zeros((tail_rows, width), F32)
    for z in range(shards):
        w = weight_ref[z * depth : (z + 1) * depth, :]
        acc = acc + jnp.dot(main_ref[z], w, preferred_element_type=F32)
        acc_tail = acc_tail + jnp.dot(tail_ref[z], w, preferred_element_type=F32)
    inner_ref[:rows, :] = acc.astype(BF16)
    inner_ref[rows:, :] = acc_tail.astype(BF16)


def conv_kernel(inner_ref, rim_ref, taps_ref, bias_ref, proj_ref, u_ref, part_ref, pad_ref):
    rows, width = inner_ref.shape
    rim = rim_ref.shape[0]
    taps = taps_ref.shape[0]
    pad_ref[:rim, :] = rim_ref[...].astype(F32)
    pad_ref[rim:, :] = inner_ref[...].astype(F32)
    pre = jnp.broadcast_to(bias_ref[...], (rows, width))
    for k in range(taps):
        first = rim - taps + 1 + k
        pre = pre + taps_ref[k : k + 1, :] * pad_ref[first : first + rows, :]
    u = (pre / (1.0 + jnp.exp(-pre))).astype(BF16)
    u_ref[...] = u
    part_ref[...] = jnp.dot(u, proj_ref[...], preferred_element_type=F32).astype(BF16)


def split3(x):
    a = x.astype(BF16)
    r = x - a.astype(F32)
    b = r.astype(BF16)
    c = (r - b.astype(F32)).astype(BF16)
    return a, b, c


def state_kernel(
    mix_ref, dtw_ref, dtb_ref, alog_ref, u_ref, step_ref, cum_ref, pay_ref, left_ref, flow_ref, bx_ref
):
    rows, width = u_ref.shape
    rank = dtw_ref.shape[0]
    n = alog_ref.shape[0]
    tiles = rows // 8
    v = jnp.dot(mix_ref[:, :rank], dtw_ref[...], preferred_element_type=F32) + dtb_ref[...]
    step = jnp.maximum(v, 0.0) + jnp.log1p(jnp.exp(-jnp.abs(v)))
    step_ref[...] = step
    row_ids = lax.broadcasted_iota(jnp.int32, (rows, rows), 0)
    col_ids = lax.broadcasted_iota(jnp.int32, (rows, rows), 1)
    lower = (row_ids >= col_ids).astype(F32).astype(BF16)
    cum = sum(jnp.dot(lower, p, preferred_element_type=F32) for p in split3(step)[::-1])
    cum_ref[...] = cum
    whole = cum[rows - 1 : rows, :]
    left_ref[...] = (whole - cum).reshape(tiles, 8, width)
    flow_ref[...] = (step * u_ref[...].astype(F32)).reshape(tiles, 8, width)
    b = mix_ref[:, rank : rank + n].astype(F32) + mix_ref[:, rank + 2 * n : rank + 3 * n].astype(F32)
    for i in range(n):
        bx_ref[:, i] = jnp.broadcast_to(b[:, i : i + 1], (rows, 128)).reshape(tiles, 8, 128)
    rate2 = -jnp.exp(alog_ref[...]) * LOG2E
    for g in range(width // 128):
        lanes = slice(g * 128, (g + 1) * 128)
        rate_g = jnp.broadcast_to(rate2[:, None, lanes], (n, 8, 128))

        def turn(i, acc):
            grow = jnp.exp2(rate_g * left_ref[i, :, lanes][None])
            return acc + grow * (flow_ref[i, :, lanes][None] * bx_ref[i])

        acc = lax.fori_loop(0, tiles, turn, jnp.zeros((n, 8, 128), F32), unroll=2)
        pay_ref[:n, lanes] = jnp.sum(acc, axis=1).astype(BF16)
    hi, lo, _ = split3(whole)
    pay_ref[n : n + 1, :] = hi
    pay_ref[n + 1 : n + 2, :] = lo


def local_kernel(mix_ref, alog_ref, u_ref, step_ref, cum_ref, skip_ref, y_ref, grow_ref, bt_ref, ct_ref, flow_ref, cx_ref):
    rows, width = u_ref.shape
    n = alog_ref.shape[0]
    tiles = rows // 8
    rank = mix_ref.shape[1] - 4 * n
    b = mix_ref[:, rank : rank + n].astype(F32) + mix_ref[:, rank + 2 * n : rank + 3 * n].astype(F32)
    c = mix_ref[:, rank + n : rank + 2 * n].astype(F32) + mix_ref[:, rank + 3 * n :].astype(F32)
    rate2 = -jnp.exp(alog_ref[...]) * LOG2E
    for i in range(n):
        cx_ref[:, i] = jnp.broadcast_to(c[:, i : i + 1], (rows, 128)).reshape(tiles, 8, 128)
    b_t, c_t = b.T, c.T
    for t in range(rows):
        bt_ref[t] = jnp.broadcast_to(b_t[:, t : t + 1], (n, 128))
        ct_ref[t] = jnp.broadcast_to(c_t[:, t : t + 1], (n, 128))
    u_float = u_ref[...].astype(F32)
    flow_ref[...] = step_ref[...] * u_float
    groups = width // 128

    def turn(t, state):
        d = step_ref[pl.ds(t, 1), :]
        f = flow_ref[pl.ds(t, 1), :]
        bt = jnp.concatenate([bt_ref[t]] * groups, axis=1)
        ct = jnp.concatenate([ct_ref[t]] * groups, axis=1)
        state = jnp.exp2(rate2 * d) * state + bt * f
        y_ref[pl.ds(t, 1), :] = jnp.sum(ct * state, axis=0, keepdims=True)
        return state

    lax.fori_loop(0, rows, turn, jnp.zeros((n, width), F32), unroll=4)
    y_ref[...] = y_ref[...] + skip_ref[...] * u_float

    for g in range(groups):
        lanes = slice(g * 128, (g + 1) * 128)
        rate_g = jnp.broadcast_to(rate2[:, None, lanes], (n, 8, 128))

        def fill(i, _):
            cum = cum_ref[pl.ds(pl.multiple_of(i * 8, 8), 8), lanes]
            grow_ref[i, :, :, lanes] = cx_ref[i] * jnp.exp2(rate_g * cum[None])
            return 0

        lax.fori_loop(0, tiles, fill, 0, unroll=2)


def final_kernel(mine_ref, all_ref, alog_ref, y_ref, grow_ref, thr_ref, out_ref):
    rows, width = y_ref.shape
    n = alog_ref.shape[0]
    tiles = rows // 8
    peers = all_ref.shape[0]
    mine = mine_ref[0]
    rate2 = -jnp.exp(alog_ref[...]) * LOG2E

    def join(p, state):
        block = all_ref[p].astype(F32)
        whole = block[n : n + 1, :] + block[n + 1 : n + 2, :]
        longer = jnp.exp2(rate2 * whole) * state + block[:n, :]
        return jnp.where(p < mine, longer, state)

    entry = lax.fori_loop(0, peers - 1, join, jnp.zeros((n, width), F32), unroll=2)
    for g in range(width // 128):
        lanes = slice(g * 128, (g + 1) * 128)
        entry_g = jnp.broadcast_to(entry[:, None, lanes], (n, 8, 128))
        thr = thr_ref[:, lanes]

        def turn(i, _):
            at = pl.ds(pl.multiple_of(i * 8, 8), 8)
            y = y_ref[at, lanes] + jnp.sum(grow_ref[i, :, :, lanes] * entry_g, axis=0)
            y_ref[at, lanes] = y / (1.0 + jnp.exp(-4.0 * (y - thr)))
            return 0

        lax.fori_loop(0, tiles, turn, 0, unroll=2)
    out_ref[...] = y_ref[...].astype(BF16)


def call(kernel, outs, ins, scratch=(), flops=0, specs=None):
    return pl.pallas_call(
        kernel,
        out_shape=outs,
        in_specs=specs or [VMEM] * len(ins),
        out_specs=jax.tree.map(lambda _: VMEM, outs),
        scratch_shapes=scratch,
        cost_estimate=pl.CostEstimate(flops=flops, bytes_accessed=flops // 64, transcendentals=0),
        compiler_params=pltpu.CompilerParams(vmem_limit_bytes=48 << 20),
    )(*ins)


def per_device(
    tokens, in_weight, conv_weight, conv_bias, proj_weight, dt_weight, dt_bias, a_log, skip_gain, threshold
):
    rows = tokens.shape[0]
    width = in_weight.shape[1]
    taps = conv_weight.shape[0]
    rank = dt_weight.shape[0]
    n = a_log.shape[0]
    shards = lax.axis_size("tp")
    peers = lax.axis_size("seq")
    each = rows // shards
    cut = rows - 8

    tail = to_all(tokens[cut:], "tp")
    main = lax.all_gather(tokens[:cut], "tp")
    inner = call(project_kernel, struct((rows, width), BF16), (main, tail, in_weight), flops=1 << 29)
    rim = lax.ppermute(inner[rows - 8 :], "seq", [(i, i + 1) for i in range(peers - 1)])
    u, part = call(
        conv_kernel,
        (struct((rows, width), BF16), struct((rows, rank + 2 * n), BF16)),
        (inner, rim, conv_weight, conv_bias[None], proj_weight),
        (pltpu.VMEM((rows + 8, width), F32),),
        flops=1 << 26,
    )
    parts = lax.all_to_all(part.reshape(shards, each, rank + 2 * n), "tp", 0, 0)
    total = jnp.sum(parts.astype(F32), axis=0)
    high = lax.reduce_precision(total, 8, 7)
    low = total[:, rank:] - high[:, rank:]
    mix = to_all(jnp.concatenate([high, low], axis=1).astype(BF16), "tp").reshape(rows, rank + 4 * n)
    step, cum, pay = call(
        state_kernel,
        (struct((rows, width), F32), struct((rows, width), F32), struct((n + 2, width), BF16)),
        (mix, dt_weight, dt_bias[None], a_log, u),
        (
            pltpu.VMEM((rows // 8, 8, width), F32),
            pltpu.VMEM((rows // 8, 8, width), F32),
            pltpu.VMEM((rows // 8, n, 8, 128), F32),
        ),
        flops=1 << 26,
    )
    everyone = to_all(pay, "seq")
    y_local, grow = call(
        local_kernel,
        (struct((rows, width), F32), struct((rows // 8, n, 8, width), F32)),
        (mix, a_log, u, step, cum, skip_gain[None]),
        (
            pltpu.VMEM((rows, n, 128), F32),
            pltpu.VMEM((rows, n, 128), F32),
            pltpu.VMEM((rows, width), F32),
            pltpu.VMEM((rows // 8, n, 8, 128), F32),
        ),
        flops=1 << 28,
    )
    mine = lax.axis_index("seq").astype(jnp.int32)[None]
    return call(
        final_kernel,
        struct((rows, width), BF16),
        (mine, everyone, a_log, y_local, grow, threshold[None]),
        flops=1 << 26,
        specs=[SMEM] + [VMEM] * 5,
    )


def solution(mesh):
    return jax.shard_map(
        per_device,
        mesh=mesh,
        in_specs=(
            P("seq", "tp"),
            P(None, "tp"),
            P(None, "tp"),
            P("tp"),
            P("tp", None),
            P(None, "tp"),
            P("tp"),
            P(None, "tp"),
            P("tp"),
            P("tp"),
        ),
        out_specs=P("seq", "tp"),
        check_vma=False,
    )
```

time: 408 us -> 131 us (0.32)
  waiting for transfers between devices: 316 us -> 8.79 us
  blocking collectives: 0 us -> 65.2 us
  other arithmetic: 44.8 us -> 0.11 us
  starting transfers between devices: 15 us -> 36.3 us
  between operations: 13.4 us -> 0.14 us
  matrix products: 12.7 us -> 0 us
  Pallas kernels: 0 us -> 10.4 us
  local copies, waits for them, and re-layouts: 2.05 us -> 9.74 us
    all_gather x3 -> x0, waiting for transfers between devices: 193 us -> none  [the longest x2 125 us: carried_in(): pieces = jax.tree.map(lambda part: lax.all_gather(part, axis), value)]
    psum x1 -> x0, waiting for transfers between devices: 121 us -> none  [per_device(): total = lax.psum(partial_sums, 'tp')]
    all_to_all x0 -> x2, blocking collectives: none -> 35.7 us  [the longest x1 20.2 us: per_device(): parts = lax.all_to_all(part.reshape(shards, each, rank + 2 * n), 'tp', 0, 0)]
    all_gather x0 -> x1, blocking collectives: none -> 29.4 us  [per_device(): main = lax.all_gather(tokens[:cut], 'tp')]
    select_n x39 -> x0, other arithmetic: 25.6 us -> none  [the longest x31 24.5 us: turn(): jnp.where(position < mine, new, old)]
    all_to_all x0 -> x2, starting transfers between devices: none -> 25.5 us  [to_all(): lax.all_to_all(jnp.broadcast_to(block[None], (peers,) + block.shape), axi...]
    dot_general x8 -> x0, other arithmetic: 17.3 us -> none  [run(): jnp.einsum('tsnc,snc->tnc', weights, inflow, precision=lax.Precision.HIGH...]
    dot_general x21 -> x0, matrix products: 12.7 us -> none  [the longest x1 3.23 us: per_device(): jnp.dot(lax.all_gather(tokens, 'tp', axis=1, tiled=True), in_weight, pref...]
  transfers between devices with their start and end apart: 5 -> 3, of which waited for: 5 -> 2; matrix products, arithmetic and copies ran while one was open for 0% -> 1% of each run, Pallas kernels for 0% -> 3%
where the time goes in v1:
time: 131 us
  blocking collectives  65.2 us (50%)
  starting transfers between devices  36.3 us (28%)
  Pallas kernels  10.4 us (8%)
  local copies, waits for them, and re-layouts  9.74 us (7%)
  waiting for transfers between devices  8.79 us (7%)
    all_gather x1, blocking collectives, per_device(): main = lax.all_gather(tokens[:cut], 'tp')  29.4 us
    all_to_all x2, starting transfers between devices, to_all(): lax.all_to_all(jnp.broadcast_to(block[None], (peers,) + block.shape), axi...  25.5 us
    all_to_all x1, blocking collectives, per_device(): parts = lax.all_to_all(part.reshape(shards, each, rank + 2 * n), 'tp', 0, 0)  20.2 us
    all_to_all x1, blocking collectives, to_all(): lax.all_to_all(jnp.broadcast_to(block[None], (peers,) + block.shape), axi...  15.5 us
    ppermute x1, starting transfers between devices, per_device(): lax.ppermute(inner[rows - 8:], 'seq', [(i, i + 1) for i in range(peers -...  10.8 us
    pallas_call x5, Pallas kernels, call(): pl.pallas_call(kernel, out_shape=outs, in_specs=specs or [VMEM] * len(ins...  10.4 us
    all_to_all x2, waiting for transfers between devices, to_all(): lax.all_to_all(jnp.broadcast_to(block[None], (peers,) + block.shape), axi...  8.25 us
    unnamed x23, local copies, waits for them, and re-layouts  6.58 us
  transfers between devices with their start and end apart: 3, of which 2 were waited for; matrix products, arithmetic and copies ran while one was open for 1% of the time, Pallas kernels for 3%

profile of v1, /device:TPU:1, one launch (start us, length us, event | category | flops | bytes accessed | tf_op | source)
XLA Modules:
  0.0 130.6 jit_solution(2206170185181982323)
XLA Ops:
  0.0 0.0 copy-start.10
  0.0 0.0 copy-start.6
  0.0 0.0 copy-start.5
  0.0 0.7 slice.16
  0.7 0.6 broadcast_in_dim.34
  1.4 15.7 %all-to-all-start = ((bf16[16,8,256]{2,1,0:T(8,128)(2,1)}), bf16[16,8,256]{2,1,0:T(8,128)(2,1)S(1)}, u32[]{:S(2)}, u32[]{:S(2)}) async-start(bf16[16,8,256]{2,1,0:T(8,128)(2,1)} %broadcast_in_dim.34), calls=%async_computation | async-start | bytes 131072 | tf_op jit(solution)/shard_map/all_to_all | solution.py:23
  17.1 0.8 slice.15
  18.0 0.0 copy-start.3
  18.0 0.0 copy-start.4
  18.0 0.0 copy-start.7
  18.0 29.4 %all-gather = bf16[1920,256]{1,0:T(8,128)(2,1)S(1)} all-gather(bf16[120,256]{1,0:T(8,128)(2,1)S(1)} %slice.15), channel_id=2, replica_groups=mesh['seq'=32,'tp'=16] {'tp'}, dimensions={0}, use_global_device_ids=true | all-gather | bytes 1044480 | tf_op jit(solution)/shard_map/all_gather | solution.py:198
  47.4 0.0 all-to-all-done.tail_ref
  47.4 0.0 copy-start
  47.4 2.2 %copy-done = bf16[4096,512]{1,0:T(8,128)(2,1)S(1)} copy-done((bf16[4096,512]{1,0:T(8,128)(2,1)S(1)}, bf16[4096,512]{1,0:T(8,128)(2,1)}, u32[]{:S(2)}) %copy-start) | copy-done | bytes 4194328
  49.6 0.0 copy-start.9
  49.6 1.5 %shard_map.100.inner_ref = bf16[128,512]{1,0:T(8,128)(2,1)S(1)} custom-call(bf16[16,120,256]{2,1,0:T(8,128)(2,1)S(1)} %bitcast.8, bf16[16,8,256]{2,1,0:T(8,128)(2,1)S(1)} %all-to-all-done.tail_ref, bf16[4096,512]{1,0:T(8,128)(2,1)S(1)} %copy-done), custom_call_target="tpu_custom_call" | custom-call | flops 536870912 | bytes 8388608 | tf_op jit(solution)/shard_map/pallas_call | solution.py:173
  51.1 0.0 copy-start.8
  51.1 10.8 %collective-permute-start = (bf16[8,512]{1,0:T(8,128)(2,1)S(1)}, bf16[8,512]{1,0:T(8,128)(2,1)S(1)}, u32[]{:S(2)}, u32[]{:S(2)}) collective-permute-start(bf16[8,512]{1,0:T(8,128)(2,1)S(1)} %slice.20), channel_id=1, source_target_pairs={{0,16},{16,32},{32,48},{48,64},{64,80},{80,96},{96,112},{112,128},... | collective-permute-start | bytes 24584 | tf_op jit(solution)/shard_map/ppermute | solution.py:200
  61.9 0.0 copy-done.10
  61.9 0.2 copy.11.proj_ref
  62.1 0.5 collective-permute-done.rim_ref
  62.7 0.0 copy-done.6
  62.7 0.0 copy-done.5
  62.7 0.4 shard_map.101
  63.1 20.2 %all_to_all.20 = bf16[16,8,288]{2,1,0:T(8,128)(2,1)S(1)} all-to-all(bf16[16,8,288]{2,1,0:T(8,128)(2,1)S(1)} %bitcast.11), channel_id=1, replica_groups=mesh['seq'=32,'tp'=16] {'tp'}, dimensions={0} | all-to-all | bytes 147456 | tf_op jit(solution)/shard_map/all_to_all | solution.py:208
  83.4 0.1 pad_maximum_fusion
  83.5 15.5 %all_to_all.21 = bf16[16,8,320]{2,1,0:T(8,128)(2,1)S(1)} all-to-all(bf16[16,8,320]{2,1,0:T(8,128)(2,1)S(1)} %broadcast_in_dim.36), channel_id=1, replica_groups=mesh['seq'=32,'tp'=16] {'tp'}, dimensions={0} | all-to-all | bytes 163840 | tf_op jit(solution)/shard_map/all_to_all | solution.py:23
  99.0 0.0 copy-done.3
  99.0 0.0 copy-done.4
  99.0 0.0 copy-done.7
  99.0 1.7 %shard_map.102 = (f32[128,512]{1,0:T(8,128)S(1)}, f32[128,512]{1,0:T(8,128)S(1)}, bf16[18,512]{1,0:T(8,128)(2,1)S(1)}) custom-call(bf16[128,320]{1,0:T(8,128)(2,1)S(1)} %bitcast.9, bf16[256,512]{1,0:T(8,128)(2,1)S(1)} %copy-done.3, f32[1,512]{1,0:T(1,128)S(1)} %bitcast.13, f32[16,512]{1,0:T(8,128)S(1)} %copy-done.4, bf16[128,512]{1,0:T(8,128)(2,1)S(1)} %get-tuple-element.13.u_ref), custom_call_target="tpu_custom_call" | custom-call | flops 67108864 | bytes 1048576 | tf_op jit(solution)/shard_map/pallas_call | solution.py:173
  100.7 0.9 broadcast_in_dim.38
  101.6 9.7 %all-to-all-start.3 = ((bf16[32,18,512]{2,1,0:T(8,128)(2,1)}), bf16[32,18,512]{2,1,0:T(8,128)(2,1)S(1)}, u32[]{:S(2)}, u32[]{:S(2)}) async-start(bf16[32,18,512]{2,1,0:T(8,128)(2,1)} %broadcast_in_dim.38), calls=%async_computation.3 | async-start | bytes 1572864 | tf_op jit(solution)/shard_map/all_to_all | solution.py:23
  111.4 0.0 copy-done.9
  111.4 4.0 %shard_map.103 = (f32[128,512]{1,0:T(8,128)S(1)}, f32[16,16,8,512]{3,2,1,0:T(8,128)S(1)}) custom-call(bf16[128,320]{1,0:T(8,128)(2,1)S(1)} %bitcast.10, f32[16,512]{1,0:T(8,128)S(1)} %copy-done.4, bf16[128,512]{1,0:T(8,128)(2,1)S(1)} %get-tuple-element.13.u_ref, f32[128,512]{1,0:T(8,128)S(1)} %get-tuple-element.15.step_ref, ...), custom_call_target="tpu_custom_call" | custom-call | flops 268435456 | bytes 4194304 | tf_op jit(solution)/shard_map/pallas_call | solution.py:173
  115.4 0.0 copy-start.1
  115.4 2.0 %copy-done.1 = f32[16,16,8,512]{3,2,1,0:T(8,128)} copy-done((f32[16,16,8,512]{3,2,1,0:T(8,128)}, f32[16,16,8,512]{3,2,1,0:T(8,128)S(1)}, u32[]{:S(2)}) %copy-start.1) | copy-done | bytes 4194328
  117.4 8.2 %all-to-all-done.3.all_ref = bf16[32,18,512]{2,1,0:T(8,128)(2,1)S(1)} async-done(((bf16[32,18,512]{2,1,0:T(8,128)(2,1)}), bf16[32,18,512]{2,1,0:T(8,128)(2,1)S(1)}, u32[]{:S(2)}, u32[]{:S(2)}) %all-to-all-start.3) | async-done | bytes 589856 | tf_op jit(solution)/shard_map/all_to_all | solution.py:23
  125.6 0.0 copy-done.8
  125.6 0.0 copy-start.2
  125.6 2.2 %copy-done.2 = f32[16,16,8,512]{3,2,1,0:T(8,128)S(1)} copy-done((f32[16,16,8,512]{3,2,1,0:T(8,128)S(1)}, f32[16,16,8,512]{3,2,1,0:T(8,128)}, u32[]{:S(2)}) %copy-start.2) | copy-done | bytes 4194328
  127.8 2.8 %shard_map.104 = bf16[128,512]{1,0:T(8,128)(2,1)} custom-call(s32[1]{0:T(128)} %bitcast.mine_ref, bf16[32,18,512]{2,1,0:T(8,128)(2,1)S(1)} %all-to-all-done.3.all_ref, f32[16,512]{1,0:T(8,128)S(1)} %copy-done.4, f32[128,512]{1,0:T(8,128)S(1)} %get-tuple-element.17.y_ref, f32[16,16,8,512]{3,2,1,0:T(8,128)S(1)} %copy-done.2, f32[1,512]{1,0:T(1,128)S(1)} %bitcast.14), custom_call_target="tpu_custom_call" | custom-call | flops 67108864 | bytes 1048576 | tf_op jit(solution)/shard_map/pallas_call | solution.py:173
  (5 shorter events, 0.0 us)
Async XLA Ops:
  0.0 61.9 %copy-start.10 = (bf16[512,288]{0,1:T(8,128)(2,1)S(1)}, bf16[512,288]{0,1:T(8,128)(2,1)}, u32[]{:S(2)}) copy-start(bf16[512,288]{0,1:T(8,128)(2,1)} %param.14) | copy-start | bytes 884740
  0.0 62.7 %copy-start.6 = (f32[512]{0:T(512)S(1)}, f32[512]{0:T(512)}, u32[]{:S(2)}) copy-start(f32[512]{0:T(512)} %param.13) | copy-start | bytes 6148
  0.0 62.7 %copy-start.5 = (f32[4,512]{1,0:T(4,128)S(1)}, f32[4,512]{1,0:T(4,128)}, u32[]{:S(2)}) copy-start(f32[4,512]{1,0:T(4,128)} %taps_ref.1) | copy-start | bytes 24580
  1.4 46.1 %all-to-all-start = ((bf16[16,8,256]{2,1,0:T(8,128)(2,1)}), bf16[16,8,256]{2,1,0:T(8,128)(2,1)S(1)}, u32[]{:S(2)}, u32[]{:S(2)}) async-start(bf16[16,8,256]{2,1,0:T(8,128)(2,1)} %broadcast_in_dim.34), calls=%async_computation | async-start | bytes 131072 | tf_op jit(solution)/shard_map/all_to_all | solution.py:23
  18.0 81.0 %copy-start.3 = (bf16[256,512]{1,0:T(8,128)(2,1)S(1)}, bf16[256,512]{1,0:T(8,128)(2,1)}, u32[]{:S(2)}) copy-start(bf16[256,512]{1,0:T(8,128)(2,1)} %dtw_ref.1) | copy-start | bytes 786436
  18.0 81.0 %copy-start.4 = (f32[16,512]{1,0:T(8,128)S(1)}, f32[16,512]{1,0:T(8,128)}, u32[]{:S(2)}) copy-start(f32[16,512]{1,0:T(8,128)} %alog_ref.5) | copy-start | bytes 98308
  18.0 81.0 %copy-start.7 = (f32[512]{0:T(512)S(1)}, f32[512]{0:T(512)}, u32[]{:S(2)}) copy-start(f32[512]{0:T(512)} %param.16) | copy-start | bytes 6148
  47.4 2.2 %copy-start = (bf16[4096,512]{1,0:T(8,128)(2,1)S(1)}, bf16[4096,512]{1,0:T(8,128)(2,1)}, u32[]{:S(2)}) copy-start(bf16[4096,512]{1,0:T(8,128)(2,1)} %weight_ref.1) | copy-start | bytes 12582916
  49.6 61.8 %copy-start.9 = (f32[512]{0:T(512)S(1)}, f32[512]{0:T(512)}, u32[]{:S(2)}) copy-start(f32[512]{0:T(512)} %param.18) | copy-start | bytes 6148
  51.1 74.5 %copy-start.8 = (f32[512]{0:T(512)S(1)}, f32[512]{0:T(512)}, u32[]{:S(2)}) copy-start(f32[512]{0:T(512)} %param.19) | copy-start | bytes 6148
  51.1 11.6 %collective-permute-start = (bf16[8,512]{1,0:T(8,128)(2,1)S(1)}, bf16[8,512]{1,0:T(8,128)(2,1)S(1)}, u32[]{:S(2)}, u32[]{:S(2)}) collective-permute-start(bf16[8,512]{1,0:T(8,128)(2,1)S(1)} %slice.20), channel_id=1, source_target_pairs={{0,16},{16,32},{32,48},{48,64},{64,80},{80,96},{96,112},{112,128},... | collective-permute-start | bytes 24584 | tf_op jit(solution)/shard_map/ppermute | solution.py:200
  101.6 24.0 %all-to-all-start.3 = ((bf16[32,18,512]{2,1,0:T(8,128)(2,1)}), bf16[32,18,512]{2,1,0:T(8,128)(2,1)S(1)}, u32[]{:S(2)}, u32[]{:S(2)}) async-start(bf16[32,18,512]{2,1,0:T(8,128)(2,1)} %broadcast_in_dim.38), calls=%async_computation.3 | async-start | bytes 1572864 | tf_op jit(solution)/shard_map/all_to_all | solution.py:23
  115.4 2.0 %copy-start.1 = (f32[16,16,8,512]{3,2,1,0:T(8,128)}, f32[16,16,8,512]{3,2,1,0:T(8,128)S(1)}, u32[]{:S(2)}) copy-start(f32[16,16,8,512]{3,2,1,0:T(8,128)S(1)} %get-tuple-element.18.grow_ref) | copy-start | bytes 12582916
  125.6 2.2 %copy-start.2 = (f32[16,16,8,512]{3,2,1,0:T(8,128)S(1)}, f32[16,16,8,512]{3,2,1,0:T(8,128)}, u32[]{:S(2)}) copy-start(f32[16,16,8,512]{3,2,1,0:T(8,128)} %copy-done.1) | copy-start | bytes 12582916

commit v2 on v1

v2 whole, which is shorter than its diff:
```python
import math

import jax
import jax.numpy as jnp
from jax import lax
from jax.experimental import pallas as pl
from jax.experimental.pallas import tpu as pltpu
from jax.sharding import PartitionSpec as P

LOG2E = math.log2(math.e)
F32 = jnp.float32
BF16 = jnp.bfloat16
VMEM = pl.BlockSpec(memory_space=pltpu.VMEM)
SMEM = pl.BlockSpec(memory_space=pltpu.SMEM)


def struct(shape, dtype):
    return jax.ShapeDtypeStruct(shape, dtype)


def silu(v):
    return v / (1.0 + jnp.exp(-v))


def convolve(taps_ref, bias_ref, pad_ref, rows, width):
    taps = taps_ref.shape[0]
    pre = jnp.broadcast_to(bias_ref[...], (rows, width))
    for k in range(taps):
        first = 9 - taps + k
        pre = pre + taps_ref[k : k + 1, :] * pad_ref[first : first + rows, :]
    return silu(pre).astype(BF16)


def pieces(depth, room):
    return [(at, min(room, depth - at)) for at in range(0, depth, room)]


def project_kernel(
    main_ref, tokens_ref, weight_ref, taps_ref, bias_ref, proj_ref,
    send_ref, edge_ref, u_ref, pad_ref, wide_ref,
):
    shards, held, depth = main_ref.shape
    rows, width = u_ref.shape
    sums = proj_ref.shape[1]
    acc = jnp.zeros((held, width), F32)
    for z in range(shards):
        w = weight_ref[z * depth : (z + 1) * depth, :]
        acc = acc + jnp.dot(main_ref[z], w, preferred_element_type=F32)
    pad_ref[:16, :] = jnp.zeros((16, width), F32)
    pad_ref[8 + rows - held :, :] = acc.astype(BF16).astype(F32)
    edge_ref[:8, :] = pad_ref[rows : rows + 8, :].astype(BF16)
    edge_ref[8:, :] = pad_ref[8:16, :].astype(BF16)
    u = convolve(taps_ref, bias_ref, pad_ref, rows, width)
    u_ref[...] = u
    part = jnp.dot(u, proj_ref[...], preferred_element_type=F32)
    wide_ref[:, :, :sums] = part.reshape(shards, 8, sums)
    late = tokens_ref[0:8, :].astype(F32)[0:1, :]
    room = wide_ref.shape[2] - sums
    row_ids = lax.broadcasted_iota(jnp.int32, (8, room), 0)
    block = jnp.zeros((8, room), F32)
    for p, (at, size) in enumerate(pieces(depth, room)):
        piece = late[:, at : at + size]
        if size < room:
            piece = jnp.concatenate([piece, jnp.zeros((1, room - size), F32)], axis=1)
        block = jnp.where(row_ids == p, jnp.broadcast_to(piece, (8, room)), block)
    wide_ref[:, :, sums:] = jnp.broadcast_to(block[None], (shards, 8, room))
    send_ref[...] = wide_ref[...].astype(BF16)


def late_kernel(
    got_ref, rim_ref, edge_ref, weight_ref, taps_ref, bias_ref, proj_ref,
    mix_ref, u_ref, wide_ref, first_ref, pad_ref, pay_ref,
):
    shards, _, lanes = got_ref.shape
    depth = weight_ref.shape[0] // shards
    width = weight_ref.shape[1]
    sums = proj_ref.shape[1]
    room = lanes - sums
    wide_ref[...] = got_ref[...].astype(F32)
    total = jnp.sum(wide_ref[:, :, :sums], axis=0)
    for p, (at, size) in enumerate(pieces(depth, room)):
        first_ref[:, at : at + size] = wide_ref[:, p, sums : sums + size]
    first = first_ref[...].astype(BF16)
    row_ids = lax.broadcasted_iota(jnp.int32, (shards, width), 0)
    acc = jnp.zeros((shards, width), F32)
    for z in range(shards):
        d = jnp.dot(first, weight_ref[z * depth : (z + 1) * depth, :], preferred_element_type=F32)
        acc = acc + jnp.where(row_ids == z, d, 0.0)
    pad_ref[:8, :] = rim_ref[...].astype(F32)
    pad_ref[8:, :] = edge_ref[8:, :].astype(F32)
    pad_ref[8:9, :] = jnp.sum(acc, axis=0, keepdims=True).astype(BF16).astype(F32)
    u = convolve(taps_ref, bias_ref, pad_ref, 8, width)
    u_ref[...] = u
    part = jnp.dot(u, proj_ref[...], preferred_element_type=F32)
    high = total.astype(BF16).astype(F32)
    rank = mix_ref.shape[2] - 256
    coefs = sums - rank
    half = sums // 2
    late = taps_ref.shape[0]
    pay_ref[...] = jnp.zeros_like(pay_ref)
    pay_ref[:, :sums] = high
    pay_ref[:, sums : sums + coefs] = total[:, rank:] - high[:, rank:]
    at = sums + coefs
    pay_ref[:late, at : at + half] = part[:late, :half]
    pay_ref[late : 2 * late, at : at + half] = part[:late, half:]
    pay = pay_ref[...].astype(BF16)
    for z in range(shards):
        mix_ref[z] = pay


def split3(x):
    a = x.astype(BF16)
    r = x - a.astype(F32)
    b = r.astype(BF16)
    c = (r - b.astype(F32)).astype(BF16)
    return a, b, c


def running_sum(x):
    rows = x.shape[0]
    row_ids = lax.broadcasted_iota(jnp.int32, (rows, rows), 0)
    col_ids = lax.broadcasted_iota(jnp.int32, (rows, rows), 1)
    lower = (row_ids >= col_ids).astype(F32).astype(BF16)
    return sum(jnp.dot(lower, p, preferred_element_type=F32) for p in split3(x)[::-1])


def state_kernel(
    mix_ref, dtw_ref, dtb_ref, alog_ref, u_ref, late_u_ref,
    step_ref, coef_ref, pay_ref,
    uf_ref, flow_ref, left_ref, bx_ref, end_ref, low_ref,
):
    shards, each, _ = mix_ref.shape
    rows, width = u_ref.shape
    rank = dtw_ref.shape[0]
    n = alog_ref.shape[0]
    sums = rank + 2 * n
    half = sums // 2
    at = sums + 2 * n
    late = each // 2
    tiles = rows // 8
    low_ref[...] = mix_ref[:, :, :rank].astype(F32).reshape(rows, rank)
    coef = mix_ref[:, :, rank:sums].astype(F32) + mix_ref[:, :, sums:at].astype(F32)
    coef_ref[...] = coef.reshape(rows, 2 * n)
    pairs = jnp.sum(mix_ref[:, :, at : at + half].astype(F32), axis=0)
    early = jnp.concatenate([pairs[:late], pairs[late:]], axis=1)
    low_ref[:late, :] = early[:, :rank]
    coef_ref[:late, :] = early[:, rank:]
    v = jnp.dot(low_ref[...].astype(BF16), dtw_ref[...], preferred_element_type=F32) + dtb_ref[...]
    step = jnp.maximum(v, 0.0) + jnp.log1p(jnp.exp(-jnp.abs(v)))
    step_ref[...] = step
    cum = running_sum(step)
    whole = cum[rows - 1 : rows, :]
    left_ref[...] = (whole - cum).reshape(tiles, 8, width)
    uf_ref[...] = u_ref[...].astype(F32)
    uf_ref[:8, :] = late_u_ref[...].astype(F32)
    flow_ref[...] = (step * uf_ref[...]).reshape(tiles, 8, width)
    b = coef_ref[:, :n]
    for i in range(n):
        bx_ref[:, i] = jnp.broadcast_to(b[:, i : i + 1], (rows, 128)).reshape(tiles, 8, 128)
    rate2 = -jnp.exp(alog_ref[...]) * LOG2E
    groups = width // 128
    for g in range(groups):
        lanes = slice(g * 128, (g + 1) * 128)
        rate_g = jnp.broadcast_to(rate2[:, None, lanes], (n, 8, 128))

        def turn(i, acc):
            grow = jnp.exp2(rate_g * left_ref[i, :, lanes][None])
            return acc + grow * (flow_ref[i, :, lanes][None] * bx_ref[i])

        acc = lax.fori_loop(0, tiles, turn, jnp.zeros((n, 8, 128), F32), unroll=2)
        hi, lo, _ = split3(whole[:, lanes])
        end_ref[g * n : (g + 1) * n, :] = jnp.sum(acc, axis=1)
        end_ref[groups * n + g : groups * n + g + 1, :] = hi.astype(F32)
        end_ref[groups * n + groups + g : groups * n + groups + g + 1, :] = lo.astype(F32)
    end = end_ref[...].astype(BF16)
    for p in range(pay_ref.shape[0]):
        pay_ref[p] = end


def local_kernel(
    coef_ref, alog_ref, u_ref, late_u_ref, step_ref, skip_ref,
    y_ref, grow_ref, bt_ref, ct_ref, cx_ref, uf_ref, flow_ref, cum_ref,
):
    rows, width = u_ref.shape
    uf_ref[...] = u_ref[...].astype(F32)
    uf_ref[:8, :] = late_u_ref[...].astype(F32)
    flow_ref[...] = (step_ref[...] * uf_ref[...]).reshape(rows // 8, 8, width)
    cum_ref[...] = running_sum(step_ref[...])
    n = alog_ref.shape[0]
    blocks = rows // 16
    b, c = coef_ref[:, :n], coef_ref[:, n:]
    rate2 = -jnp.exp(alog_ref[...]) * LOG2E
    for i in range(n):
        cx_ref[:, i] = jnp.broadcast_to(c[:, i : i + 1], (rows, 128)).reshape(blocks, 16, 128)
    b_t, c_t = b.T, c.T
    for t in range(rows):
        bt_ref[t] = jnp.broadcast_to(b_t[:, t : t + 1], (n, 128))
        ct_ref[t] = jnp.broadcast_to(c_t[:, t : t + 1], (n, 128))
    groups = width // 128

    def block_turn(i, state):
        for r in range(8):
            t = i * 8 + r
            d = step_ref[pl.ds(t, 1), :]
            f = flow_ref[i, r : r + 1, :]
            bt = jnp.concatenate([bt_ref[t]] * groups, axis=1)
            ct = jnp.concatenate([ct_ref[t]] * groups, axis=1)
            state = jnp.exp2(rate2 * d) * state + bt * f
            y_ref[pl.ds(t, 1), :] = jnp.sum(ct * state, axis=0, keepdims=True)
        return state

    lax.fori_loop(0, rows // 8, block_turn, jnp.zeros((n, width), F32))
    y_ref[...] = y_ref[...] + skip_ref[...] * uf_ref[...]

    for g in range(groups):
        lanes = slice(g * 128, (g + 1) * 128)
        rate_g = jnp.broadcast_to(rate2[:, None, lanes], (n, 16, 128))

        def fill(i, _):
            cum = cum_ref[pl.ds(pl.multiple_of(i * 16, 16), 16), lanes]
            grow_ref[i, :, :, lanes] = (cx_ref[i] * jnp.exp2(rate_g * cum[None])).astype(BF16)
            return 0

        lax.fori_loop(0, blocks, fill, 0)


def final_kernel(mine_ref, all_ref, alog_ref, y_ref, grow_ref, thr_ref, out_ref):
    rows, width = y_ref.shape
    n = alog_ref.shape[0]
    blocks = rows // 16
    peers = all_ref.shape[0]
    mine = mine_ref[0]
    rate2 = -jnp.exp(alog_ref[...]) * LOG2E

    groups = width // 128
    for g in range(groups):
        lanes = slice(g * 128, (g + 1) * 128)
        rate_g = rate2[:, lanes]

        def join(p, state):
            block = all_ref[p].astype(F32)
            at = groups * n + g
            whole = block[at : at + 1, :] + block[at + groups : at + groups + 1, :]
            longer = jnp.exp2(rate_g * whole) * state + block[g * n : (g + 1) * n, :]
            return jnp.where(p < mine, longer, state)

        entry = jnp.zeros((n, 128), F32)
        for p in range(peers - 1):
            entry = join(p, entry)
        entry_g = jnp.broadcast_to(entry[:, None, :], (n, 16, 128))
        thr = thr_ref[:, lanes]

        def turn(i, _):
            at = pl.ds(pl.multiple_of(i * 16, 16), 16)
            y = y_ref[at, lanes] + jnp.sum(grow_ref[i, :, :, lanes].astype(F32) * entry_g, axis=0)
            y_ref[at, lanes] = y / (1.0 + jnp.exp(-4.0 * (y - thr)))
            return 0

        lax.fori_loop(0, blocks, turn, 0)
    out_ref[...] = y_ref[...].astype(BF16)


def call(kernel, outs, ins, scratch=(), flops=0, specs=None):
    return pl.pallas_call(
        kernel,
        out_shape=outs,
        in_specs=specs or [VMEM] * len(ins),
        out_specs=jax.tree.map(lambda _: VMEM, outs),
        scratch_shapes=scratch,
        cost_estimate=pl.CostEstimate(flops=flops, bytes_accessed=flops // 64, transcendentals=0),
        compiler_params=pltpu.CompilerParams(vmem_limit_bytes=12 << 20),
    )(*ins)


def per_device(
    tokens, in_weight, conv_weight, conv_bias, proj_weight, dt_weight, dt_bias, a_log, skip_gain, threshold
):
    rows = tokens.shape[0]
    width = in_weight.shape[1]
    taps = conv_weight.shape[0]
    rank = dt_weight.shape[0]
    n = a_log.shape[0]
    shards = lax.axis_size("tp")
    peers = lax.axis_size("seq")
    sums = rank + 2 * n
    lanes = -(-sums // 128) * 128
    bias = conv_bias[None]

    main = lax.all_gather(tokens[1:], "tp")
    send, edge, u = call(
        project_kernel,
        (struct((shards, 8, lanes), BF16), struct((16, width), BF16), struct((rows, width), BF16)),
        (main, tokens, in_weight, conv_weight, bias, proj_weight),
        (pltpu.VMEM((rows + 8, width), F32), pltpu.VMEM((shards, 8, lanes), F32)),
        flops=1 << 29,
    )
    rim = lax.ppermute(edge[:8], "seq", [(i, i + 1) for i in range(peers - 1)])
    got = lax.all_to_all(send, "tp", 0, 0)
    mix, late_u = call(
        late_kernel,
        (struct((shards, 8, rank + 256), BF16), struct((8, width), BF16)),
        (got, rim, edge, in_weight, conv_weight, bias, proj_weight),
        (
            pltpu.VMEM((shards, 8, lanes), F32),
            pltpu.VMEM((shards, tokens.shape[1]), F32),
            pltpu.VMEM((16, width), F32),
            pltpu.VMEM((8, rank + 256), F32),
        ),
        flops=1 << 28,
    )
    mix = lax.all_to_all(mix, "tp", 0, 0)
    whole = struct((rows, width), F32)
    step, coef, pay = call(
        state_kernel,
        (whole, struct((rows, 2 * n), F32), struct((peers, (n + 2) * width // 128, 128), BF16)),
        (mix, dt_weight, dt_bias[None], a_log, u, late_u),
        (
            pltpu.VMEM((rows, width), F32),
            pltpu.VMEM((rows // 8, 8, width), F32),
            pltpu.VMEM((rows // 8, 8, width), F32),
            pltpu.VMEM((rows // 8, n, 8, 128), F32),
            pltpu.VMEM(((n + 2) * width // 128, 128), F32),
            pltpu.VMEM((rows, rank), F32),
        ),
        flops=1 << 26,
    )
    everyone = lax.all_to_all(pay, "seq", 0, 0)
    y_local, grow = call(
        local_kernel,
        (whole, struct((rows // 16, n, 16, width), BF16)),
        (coef, a_log, u, late_u, step, skip_gain[None]),
        (
            pltpu.VMEM((rows, n, 128), F32),
            pltpu.VMEM((rows, n, 128), F32),
            pltpu.VMEM((rows // 16, n, 16, 128), F32),
            pltpu.VMEM((rows, width), F32),
            pltpu.VMEM((rows // 8, 8, width), F32),
            pltpu.VMEM((rows, width), F32),
        ),
        flops=1 << 28,
    )
    mine = lax.axis_index("seq").astype(jnp.int32)[None]
    return call(
        final_kernel,
        struct((rows, width), BF16),
        (mine, everyone, a_log, y_local, grow, threshold[None]),
        flops=1 << 26,
        specs=[SMEM] + [VMEM] * 5,
    )


def solution(mesh):
    return jax.shard_map(
        per_device,
        mesh=mesh,
        in_specs=(
            P("seq", "tp"),
            P(None, "tp"),
            P(None, "tp"),
            P("tp"),
            P("tp", None),
            P(None, "tp"),
            P("tp"),
            P(None, "tp"),
            P("tp"),
            P("tp"),
        ),
        out_specs=P("seq", "tp"),
        check_vma=False,
    )
```

time: 131 us -> 117 us (0.89)
  starting transfers between devices: 36.3 us -> 28 us
  blocking collectives: 65.2 us -> 58.9 us
    all_to_all x2 -> x1, blocking collectives: 35.7 us -> 23.4 us  [per_device(): mix = lax.all_to_all(mix, 'tp', 0, 0)]
    all_to_all x2, starting transfers between devices: 25.5 us -> 17 us  [the longest x1 10.5 us: per_device(): everyone = lax.all_to_all(pay, 'seq', 0, 0)]
    all_gather x1, blocking collectives: 29.4 us -> 35.4 us  [per_device(): main = lax.all_gather(tokens[1:], 'tp')]
    unnamed x23 -> x26, local copies, waits for them, and re-layouts: 6.58 us -> 8.68 us
    broadcast_in_dim x3 -> x0, local copies, waits for them, and re-layouts: 1.59 us -> none  [to_all(): jnp.broadcast_to(block[None], (peers,) + block.shape)]
    slice x3 -> x1, local copies, waits for them, and re-layouts: 1.57 us -> 0.01 us  [per_device(): rim = lax.ppermute(edge[:8], 'seq', [(i, i + 1) for i in range(peers - 1)])]
  transfers between devices with their start and end apart: 3 -> 3, of which waited for: 2 -> 3; matrix products, arithmetic and copies ran while one was open for 1% -> 0% of each run, Pallas kernels for 3% -> 3%
where the time goes in v2:
time: 117 us; the launch traced here: 116 us
  blocking collectives  58.9 us (50%)
  starting transfers between devices  28 us (24%)
  Pallas kernels  11.5 us (10%)
  waiting for transfers between devices  9.27 us (8%)
  local copies, waits for them, and re-layouts  8.68 us (7%)
    all_gather x1, blocking collectives, per_device(): main = lax.all_gather(tokens[1:], 'tp')  35.4 us
    all_to_all x1, blocking collectives, per_device(): mix = lax.all_to_all(mix, 'tp', 0, 0)  23.4 us
    pallas_call x5, Pallas kernels, call(): pl.pallas_call(kernel, out_shape=outs, in_specs=specs or [VMEM] * len(ins...  11.5 us
    ppermute x1, starting transfers between devices, per_device(): rim = lax.ppermute(edge[:8], 'seq', [(i, i + 1) for i in range(peers - 1)])  10.9 us
    all_to_all x1, starting transfers between devices, per_device(): everyone = lax.all_to_all(pay, 'seq', 0, 0)  10.5 us
    unnamed x26, local copies, waits for them, and re-layouts  8.68 us
    all_to_all x1, waiting for transfers between devices, per_device(): everyone = lax.all_to_all(pay, 'seq', 0, 0)  8.39 us
    all_to_all x1, starting transfers between devices, per_device(): got = lax.all_to_all(send, 'tp', 0, 0)  6.53 us
  transfers between devices with their start and end apart: 3, of which 3 were waited for; matrix products, arithmetic and copies ran while one was open for 0% of the time, Pallas kernels for 3%

profile of v2, /device:TPU:1, one launch (start us, length us, event | category | flops | bytes accessed | tf_op | source)
XLA Modules:
  0.0 116.4 jit_solution(6126900243290589795)
XLA Ops:
  0.0 0.0 copy-start.6
  0.0 0.0 copy-start.8
  0.0 0.9 slice_bitcast_fusion
  0.9 1.2 %copy.13.proj_ref = bf16[512,288]{1,0:T(8,128)(2,1)S(1)} copy(bf16[512,288]{0,1:T(8,128)(2,1)} %param.14) | data formatting | bytes 589824 | tf_op args[4]
  2.1 35.4 %all-gather.1.main_ref = bf16[16,127,256]{2,1,0:T(8,128)(2,1)S(1)} all-gather(bf16[1,127,256]{2,1,0:T(8,128)(2,1)S(1)} %slice_bitcast_fusion), channel_id=2, replica_groups=mesh['seq'=32,'tp'=16] {'tp'}, dimensions={0}, use_global_device_ids=true | all-gather | bytes 1105408 | tf_op jit(solution)/shard_map/all_gather | solution.py:289
  37.5 0.0 copy-start
  37.5 2.2 %copy-done = bf16[4096,512]{1,0:T(8,128)(2,1)S(1)} copy-done((bf16[4096,512]{1,0:T(8,128)(2,1)S(1)}, bf16[4096,512]{1,0:T(8,128)(2,1)}, u32[]{:S(2)}) %copy-start) | copy-done | bytes 4194328
  39.7 0.0 copy-start.3
  39.7 0.8 copy-done.3
  40.5 0.0 copy-start.5
  40.5 0.7 copy-done.5
  41.2 0.0 copy-start.7
  41.2 0.7 copy-done.7
  41.9 0.0 copy-start.2
  41.9 0.0 copy-start.4
  41.9 0.0 copy-start.9
  41.9 1.8 %shard_map.100 = (bf16[16,8,384]{2,1,0:T(8,128)(2,1)}, bf16[16,512]{1,0:T(8,128)(2,1)S(1)}, bf16[128,512]{1,0:T(8,128)(2,1)S(1)}) custom-call(bf16[16,127,256]{2,1,0:T(8,128)(2,1)S(1)} %all-gather.1.main_ref, bf16[128,256]{1,0:T(8,128)(2,1)S(1)} %copy-done.3, bf16[4096,512]{1,0:T(8,128)(2,1)S(1)} %copy-done, f32[4,512]{1,0:T(4,128)S(1)} %copy-done.5, ...), custom_call_target="tpu_custom_call" | custom-call | flops 536870912 | bytes 8388608 | tf_op jit(solution)/shard_map/pallas_call | solution.py:264
  43.7 0.0 copy-start.11
  43.7 0.0 copy-start.10
  43.7 6.5 %all-to-all-start = ((bf16[16,8,384]{2,1,0:T(8,128)(2,1)}), bf16[16,8,384]{2,1,0:T(8,128)(2,1)S(1)}, u32[]{:S(2)}, u32[]{:S(2)}) async-start(bf16[16,8,384]{2,1,0:T(8,128)(2,1)} %get-tuple-element.15), calls=%async_computation | async-start | bytes 196608 | tf_op jit(solution)/shard_map/all_to_all | solution.py:298
  50.2 10.9 %collective-permute-start = (bf16[8,512]{1,0:T(8,128)(2,1)S(1)}, bf16[8,512]{1,0:T(8,128)(2,1)S(1)}, u32[]{:S(2)}, u32[]{:S(2)}) collective-permute-start(bf16[8,512]{1,0:T(8,128)(2,1)S(1)} %slice.7), channel_id=1, source_target_pairs={{0,16},{16,32},{32,48},{48,64},{64,80},{80,96},{96,112},{112,128},... | collective-permute-start | bytes 24584 | tf_op jit(solution)/shard_map/ppermute | solution.py:297
  61.2 0.8 collective-permute-done.rim_ref
  62.0 0.1 all-to-all-done.got_ref
  62.1 0.0 copy-done.6
  62.1 0.0 copy-done.8
  62.1 0.0 copy-start.1
  62.1 2.2 %copy-done.1 = bf16[4096,512]{1,0:T(8,128)(2,1)S(1)} copy-done((bf16[4096,512]{1,0:T(8,128)(2,1)S(1)}, bf16[4096,512]{1,0:T(8,128)(2,1)}, u32[]{:S(2)}) %copy-start.1) | copy-done | bytes 4194328
  64.3 1.0 shard_map.101
  65.3 23.4 %all_to_all.15.mix_ref = bf16[16,8,512]{2,1,0:T(8,128)(2,1)S(1)} all-to-all(bf16[16,8,512]{2,1,0:T(8,128)(2,1)S(1)} %get-tuple-element.17), channel_id=1, replica_groups=mesh['seq'=32,'tp'=16] {'tp'}, dimensions={0} | all-to-all | bytes 262144 | tf_op jit(solution)/shard_map/all_to_all | solution.py:311
  88.7 0.0 copy-done.2
  88.7 0.0 copy-done.4
  88.7 0.0 copy-done.9
  88.7 2.6 %shard_map.102 = (f32[128,512]{1,0:T(8,128)S(1)}, f32[128,32]{1,0:T(8,128)S(1)}, bf16[32,72,128]{2,1,0:T(8,128)(2,1)}) custom-call(bf16[16,8,512]{2,1,0:T(8,128)(2,1)S(1)} %all_to_all.15.mix_ref, bf16[256,512]{1,0:T(8,128)(2,1)S(1)} %copy-done.2, f32[1,512]{1,0:T(1,128)S(1)} %bitcast.9, f32[16,512]{1,0:T(8,128)S(1)} %copy-done.4, ...), custom_call_target="tpu_custom_call" | custom-call | flops 67108864 | bytes 1048576 | tf_op jit(solution)/shard_map/pallas_call | solution.py:264
  91.3 10.5 %all-to-all-start.2 = ((bf16[32,72,128]{2,1,0:T(8,128)(2,1)}), bf16[32,72,128]{2,1,0:T(8,128)(2,1)S(1)}, u32[]{:S(2)}, u32[]{:S(2)}) async-start(bf16[32,72,128]{2,1,0:T(8,128)(2,1)} %get-tuple-element.20), calls=%async_computation.2 | async-start | bytes 1179648 | tf_op jit(solution)/shard_map/all_to_all | solution.py:327
  101.8 0.0 copy-done.11
  101.9 3.8 %shard_map.103 = (f32[128,512]{1,0:T(8,128)S(1)}, bf16[8,16,16,512]{3,2,1,0:T(8,128)(2,1)S(1)}) custom-call(f32[128,32]{1,0:T(8,128)S(1)} %get-tuple-element.21.coef_ref, f32[16,512]{1,0:T(8,128)S(1)} %copy-done.4, bf16[128,512]{1,0:T(8,128)(2,1)S(1)} %get-tuple-element.18.u_ref, bf16[8,512]{1,0:T(8,128)(2,1)S(1)} %get-tuple-element.19.late_u_ref, ...), custom_call_target="tpu_custom_call" | custom-call | flops 268435456 | bytes 4194304 | tf_op jit(solution)/shard_map/pallas_call | solution.py:264
  105.7 8.4 %all-to-all-done.2.all_ref = bf16[32,72,128]{2,1,0:T(8,128)(2,1)S(1)} async-done(((bf16[32,72,128]{2,1,0:T(8,128)(2,1)}), bf16[32,72,128]{2,1,0:T(8,128)(2,1)S(1)}, u32[]{:S(2)}, u32[]{:S(2)}) %all-to-all-start.2) | async-done | bytes 589856 | tf_op jit(solution)/shard_map/all_to_all | solution.py:327
  114.1 0.0 copy-done.10
  114.1 2.3 %shard_map.104 = bf16[128,512]{1,0:T(8,128)(2,1)} custom-call(s32[1]{0:T(128)} %bitcast.mine_ref, bf16[32,72,128]{2,1,0:T(8,128)(2,1)S(1)} %all-to-all-done.2.all_ref, f32[16,512]{1,0:T(8,128)S(1)} %copy-done.4, f32[128,512]{1,0:T(8,128)S(1)} %get-tuple-element.23.y_ref, bf16[8,16,16,512]{3,2,1,0:T(8,128)(2,1)S(1)} %get-tuple-element.24.grow_ref, ...), custom_call_target="tpu_custom_call" | custom-call | flops 67108864 | bytes 1048576 | tf_op jit(solution)/shard_map/pallas_call | solution.py:264
  (1 shorter events, 0.0 us)
Async XLA Ops:
  0.0 62.1 %copy-start.6 = (f32[4,512]{1,0:T(4,128)S(1)}, f32[4,512]{1,0:T(4,128)}, u32[]{:S(2)}) copy-start(f32[4,512]{1,0:T(4,128)} %taps_ref.3) | copy-start | bytes 24580
  0.0 62.1 %copy-start.8 = (f32[512]{0:T(512)S(1)}, f32[512]{0:T(512)}, u32[]{:S(2)}) copy-start(f32[512]{0:T(512)} %param.13) | copy-start | bytes 6148
  37.5 2.2 %copy-start = (bf16[4096,512]{1,0:T(8,128)(2,1)S(1)}, bf16[4096,512]{1,0:T(8,128)(2,1)}, u32[]{:S(2)}) copy-start(bf16[4096,512]{1,0:T(8,128)(2,1)} %weight_ref.3) | copy-start | bytes 12582916
  39.7 0.8 copy-start.3
  40.5 0.7 copy-start.5
  41.2 0.7 copy-start.7
  41.9 46.8 %copy-start.2 = (bf16[256,512]{1,0:T(8,128)(2,1)S(1)}, bf16[256,512]{1,0:T(8,128)(2,1)}, u32[]{:S(2)}) copy-start(bf16[256,512]{1,0:T(8,128)(2,1)} %dtw_ref.1) | copy-start | bytes 786436
  41.9 46.8 %copy-start.4 = (f32[16,512]{1,0:T(8,128)S(1)}, f32[16,512]{1,0:T(8,128)}, u32[]{:S(2)}) copy-start(f32[16,512]{1,0:T(8,128)} %alog_ref.5) | copy-start | bytes 98308
  41.9 46.8 %copy-start.9 = (f32[512]{0:T(512)S(1)}, f32[512]{0:T(512)}, u32[]{:S(2)}) copy-start(f32[512]{0:T(512)} %param.16) | copy-start | bytes 6148
  43.7 58.2 %copy-start.11 = (f32[512]{0:T(512)S(1)}, f32[512]{0:T(512)}, u32[]{:S(2)}) copy-start(f32[512]{0:T(512)} %param.18) | copy-start | bytes 6148
  43.7 70.4 %copy-start.10 = (f32[512]{0:T(512)S(1)}, f32[512]{0:T(512)}, u32[]{:S(2)}) copy-start(f32[512]{0:T(512)} %param.19) | copy-start | bytes 6148
  43.7 18.4 %all-to-all-start = ((bf16[16,8,384]{2,1,0:T(8,128)(2,1)}), bf16[16,8,384]{2,1,0:T(8,128)(2,1)S(1)}, u32[]{:S(2)}, u32[]{:S(2)}) async-start(bf16[16,8,384]{2,1,0:T(8,128)(2,1)} %get-tuple-element.15), calls=%async_computation | async-start | bytes 196608 | tf_op jit(solution)/shard_map/all_to_all | solution.py:298
  50.2 11.7 %collective-permute-start = (bf16[8,512]{1,0:T(8,128)(2,1)S(1)}, bf16[8,512]{1,0:T(8,128)(2,1)S(1)}, u32[]{:S(2)}, u32[]{:S(2)}) collective-permute-start(bf16[8,512]{1,0:T(8,128)(2,1)S(1)} %slice.7), channel_id=1, source_target_pairs={{0,16},{16,32},{32,48},{48,64},{64,80},{80,96},{96,112},{112,128},... | collective-permute-start | bytes 24584 | tf_op jit(solution)/shard_map/ppermute | solution.py:297
  62.1 2.2 %copy-start.1 = (bf16[4096,512]{1,0:T(8,128)(2,1)S(1)}, bf16[4096,512]{1,0:T(8,128)(2,1)}, u32[]{:S(2)}) copy-start(bf16[4096,512]{1,0:T(8,128)(2,1)} %weight_ref.3) | copy-start | bytes 12582916
  91.3 22.7 %all-to-all-start.2 = ((bf16[32,72,128]{2,1,0:T(8,128)(2,1)}), bf16[32,72,128]{2,1,0:T(8,128)(2,1)S(1)}, u32[]{:S(2)}, u32[]{:S(2)}) async-start(bf16[32,72,128]{2,1,0:T(8,128)(2,1)} %get-tuple-element.20), calls=%async_computation.2 | async-start | bytes 1179648 | tf_op jit(solution)/shard_map/all_to_all | solution.py:327

commit v3 on v2

--- a/solution.py
+++ b/solution.py
@@ -12,6 +12,7 @@
 BF16 = jnp.bfloat16
 VMEM = pl.BlockSpec(memory_space=pltpu.VMEM)
 SMEM = pl.BlockSpec(memory_space=pltpu.SMEM)
+HBM = pl.BlockSpec(memory_space=pltpu.HBM)
 
 
 def struct(shape, dtype):
@@ -35,26 +36,50 @@
     return [(at, min(room, depth - at)) for at in range(0, depth, room)]
 
 
+def project_rows(u, proj_ref):
+    return lax.dot_general(u, proj_ref[...], (((1,), (1,)), ((), ())), preferred_element_type=F32)
+
+
+def fetches(pairs, sems):
+    copies = [pltpu.make_async_copy(src, dst, sems.at[i]) for i, (src, dst) in enumerate(pairs)]
+    for copy in copies:
+        copy.start()
+    return copies
+
+
+def weight_fetches(hbm_ref, buf_ref, shards, depth):
+    return [(hbm_ref.at[pl.ds(z * depth, depth)], buf_ref.at[pl.ds(z * depth, depth)]) for z in range(shards)]
+
+
 def project_kernel(
-    main_ref, tokens_ref, weight_ref, taps_ref, bias_ref, proj_ref,
-    send_ref, edge_ref, u_ref, pad_ref, wide_ref,
+    main_ref, tokens_hbm, weight_hbm, taps_hbm, bias_hbm, proj_hbm,
+    send_ref, edge_ref, u_ref,
+    pad_ref, wide_ref, weight_ref, taps_ref, bias_ref, proj_ref, tokens_ref, sems,
 ):
     shards, held, depth = main_ref.shape
     rows, width = u_ref.shape
-    sums = proj_ref.shape[1]
+    sums = proj_ref.shape[0]
+    copies = fetches(
+        weight_fetches(weight_hbm, weight_ref, shards, depth)
+        + [(taps_hbm, taps_ref), (bias_hbm, bias_ref), (proj_hbm, proj_ref),
+           (tokens_hbm.at[pl.ds(0, 8)], tokens_ref)],
+        sems,
+    )
+    pad_ref[:16, :] = jnp.zeros((16, width), F32)
     acc = jnp.zeros((held, width), F32)
     for z in range(shards):
+        copies[z].wait()
         w = weight_ref[z * depth : (z + 1) * depth, :]
         acc = acc + jnp.dot(main_ref[z], w, preferred_element_type=F32)
-    pad_ref[:16, :] = jnp.zeros((16, width), F32)
+    for copy in copies[shards:]:
+        copy.wait()
     pad_ref[8 + rows - held :, :] = acc.astype(BF16).astype(F32)
     edge_ref[:8, :] = pad_ref[rows : rows + 8, :].astype(BF16)
     edge_ref[8:, :] = pad_ref[8:16, :].astype(BF16)
     u = convolve(taps_ref, bias_ref, pad_ref, rows, width)
     u_ref[...] = u
-    part = jnp.dot(u, proj_ref[...], preferred_element_type=F32)
-    wide_ref[:, :, :sums] = part.reshape(shards, 8, sums)
-    late = tokens_ref[0:8, :].astype(F32)[0:1, :]
+    wide_ref[:, :, :sums] = project_rows(u, proj_ref).reshape(shards, 8, sums)
+    late = tokens_ref[...].astype(F32)[0:1, :]
     room = wide_ref.shape[2] - sums
     row_ids = lax.broadcasted_iota(jnp.int32, (8, room), 0)
     block = jnp.zeros((8, room), F32)
@@ -68,38 +93,47 @@
 
 
 def late_kernel(
-    got_ref, rim_ref, edge_ref, weight_ref, taps_ref, bias_ref, proj_ref,
-    mix_ref, u_ref, wide_ref, first_ref, pad_ref, pay_ref,
+    got_ref, rim_ref, edge_ref, weight_hbm, taps_hbm, bias_hbm, proj_hbm,
+    mix_ref, u_ref,
+    wide_ref, first_ref, pad_ref, pay_ref, weight_ref, taps_ref, bias_ref, proj_ref, sems,
 ):
     shards, _, lanes = got_ref.shape
     depth = weight_ref.shape[0] // shards
     width = weight_ref.shape[1]
-    sums = proj_ref.shape[1]
+    sums = proj_ref.shape[0]
+    copies = fetches(
+        weight_fetches(weight_hbm, weight_ref, shards, depth)
+        + [(taps_hbm, taps_ref), (bias_hbm, bias_ref), (proj_hbm, proj_ref)],
+        sems,
+    )
     room = lanes - sums
     wide_ref[...] = got_ref[...].astype(F32)
-    total = jnp.sum(wide_ref[:, :, :sums], axis=0)
     for p, (at, size) in enumerate(pieces(depth, room)):
         first_ref[:, at : at + size] = wide_ref[:, p, sums : sums + size]
+    total = jnp.sum(wide_ref[:, :, :sums], axis=0)
+    high = total.astype(BF16).astype(F32)
+    rank = mix_ref.shape[2] - 256
+    coefs = sums - rank
+    pay_ref[...] = jnp.zeros_like(pay_ref)
+    pay_ref[:, :sums] = high
+    pay_ref[:, sums : sums + coefs] = total[:, rank:] - high[:, rank:]
+    pad_ref[:8, :] = rim_ref[...].astype(F32)
+    pad_ref[8:, :] = edge_ref[8:, :].astype(F32)
     first = first_ref[...].astype(BF16)
     row_ids = lax.broadcasted_iota(jnp.int32, (shards, width), 0)
     acc = jnp.zeros((shards, width), F32)
     for z in range(shards):
+        copies[z].wait()
         d = jnp.dot(first, weight_ref[z * depth : (z + 1) * depth, :], preferred_element_type=F32)
         acc = acc + jnp.where(row_ids == z, d, 0.0)
-    pad_ref[:8, :] = rim_ref[...].astype(F32)
-    pad_ref[8:, :] = edge_ref[8:, :].astype(F32)
+    for copy in copies[shards:]:
+        copy.wait()
     pad_ref[8:9, :] = jnp.sum(acc, axis=0, keepdims=True).astype(BF16).astype(F32)
     u = convolve(taps_ref, bias_ref, pad_ref, 8, width)
     u_ref[...] = u
-    part = jnp.dot(u, proj_ref[...], preferred_element_type=F32)
-    high = total.astype(BF16).astype(F32)
-    rank = mix_ref.shape[2] - 256
-    coefs = sums - rank
+    part = project_rows(u, proj_ref)
     half = sums // 2
     late = taps_ref.shape[0]
-    pay_ref[...] = jnp.zeros_like(pay_ref)
-    pay_ref[:, :sums] = high
-    pay_ref[:, sums : sums + coefs] = total[:, rank:] - high[:, rank:]
     at = sums + coefs
     pay_ref[:late, at : at + half] = part[:late, :half]
     pay_ref[late : 2 * late, at : at + half] = part[:late, half:]
@@ -260,16 +294,17 @@
     out_ref[...] = y_ref[...].astype(BF16)
 
 
-def call(kernel, outs, ins, scratch=(), flops=0, specs=None):
+def call(kernel, outs, ins, scratch=(), flops=0, specs=None, vmem=12 << 20):
+    specs = specs or [VMEM] * len(ins)
     return pl.pallas_call(
         kernel,
         out_shape=outs,
-        in_specs=specs or [VMEM] * len(ins),
+        in_specs=specs,
         out_specs=jax.tree.map(lambda _: VMEM, outs),
         scratch_shapes=scratch,
         cost_estimate=pl.CostEstimate(flops=flops, bytes_accessed=flops // 64, transcendentals=0),
-        compiler_params=pltpu.CompilerParams(vmem_limit_bytes=12 << 20),
-    )(*ins)
+        compiler_params=pltpu.CompilerParams(vmem_limit_bytes=vmem),
+    )(*[pltpu.with_memory_space_constraint(x, pltpu.HBM) if spec is HBM else x for x, spec in zip(ins, specs)])
 
 
 def per_device(
@@ -285,28 +320,41 @@
     sums = rank + 2 * n
     lanes = -(-sums // 128) * 128
     bias = conv_bias[None]
+    proj = proj_weight.T
+    held = (
+        pltpu.VMEM(in_weight.shape, BF16),
+        pltpu.VMEM(conv_weight.shape, F32),
+        pltpu.VMEM(bias.shape, F32),
+        pltpu.VMEM(proj.shape, BF16),
+    )
 
     main = lax.all_gather(tokens[1:], "tp")
     send, edge, u = call(
         project_kernel,
         (struct((shards, 8, lanes), BF16), struct((16, width), BF16), struct((rows, width), BF16)),
-        (main, tokens, in_weight, conv_weight, bias, proj_weight),
-        (pltpu.VMEM((rows + 8, width), F32), pltpu.VMEM((shards, 8, lanes), F32)),
+        (main, tokens, in_weight, conv_weight, bias, proj),
+        (pltpu.VMEM((rows + 8, width), F32), pltpu.VMEM((shards, 8, lanes), F32))
+        + held
+        + (pltpu.VMEM((8, tokens.shape[1]), BF16), pltpu.SemaphoreType.DMA((shards + 4,))),
         flops=1 << 29,
+        specs=[VMEM] + [HBM] * 5,
     )
     rim = lax.ppermute(edge[:8], "seq", [(i, i + 1) for i in range(peers - 1)])
     got = lax.all_to_all(send, "tp", 0, 0)
     mix, late_u = call(
         late_kernel,
         (struct((shards, 8, rank + 256), BF16), struct((8, width), BF16)),
-        (got, rim, edge, in_weight, conv_weight, bias, proj_weight),
+        (got, rim, edge, in_weight, conv_weight, bias, proj),
         (
             pltpu.VMEM((shards, 8, lanes), F32),
             pltpu.VMEM((shards, tokens.shape[1]), F32),
             pltpu.VMEM((16, width), F32),
             pltpu.VMEM((8, rank + 256), F32),
-        ),
+        )
+        + held
+        + (pltpu.SemaphoreType.DMA((shards + 3,)),),
         flops=1 << 28,
+        specs=[VMEM] * 3 + [HBM] * 4,
     )
     mix = lax.all_to_all(mix, "tp", 0, 0)
     whole = struct((rows, width), F32)

time: 117 us -> 114 us (0.974)
  local copies, waits for them, and re-layouts: 8.68 us -> 0.88 us
  Pallas kernels: 11.5 us -> 16.3 us
    unnamed x26 -> x11, local copies, waits for them, and re-layouts: 8.68 us -> 0.88 us
    pallas_call x5, Pallas kernels: 11.5 us -> 16.3 us  [call(): pl.pallas_call(kernel, out_shape=outs, in_specs=specs, out_specs=jax.tree...]
where the time goes in v3:
time: 114 us; the launch traced here: 113 us
  blocking collectives  58.9 us (52%)
  starting transfers between devices  27.8 us (24%)
  Pallas kernels  16.3 us (14%)
  waiting for transfers between devices  9.29 us (8%)
    all_gather x1, blocking collectives, per_device(): main = lax.all_gather(tokens[1:], 'tp')  35.4 us
    all_to_all x1, blocking collectives, per_device(): mix = lax.all_to_all(mix, 'tp', 0, 0)  23.4 us
    pallas_call x5, Pallas kernels, call(): pl.pallas_call(kernel, out_shape=outs, in_specs=specs, out_specs=jax.tree...  16.3 us
    ppermute x1, starting transfers between devices, per_device(): rim = lax.ppermute(edge[:8], 'seq', [(i, i + 1) for i in range(peers - 1)])  10.9 us
    all_to_all x1, starting transfers between devices, per_device(): everyone = lax.all_to_all(pay, 'seq', 0, 0)  10.5 us
    all_to_all x1, waiting for transfers between devices, per_device(): everyone = lax.all_to_all(pay, 'seq', 0, 0)  8.4 us
    all_to_all x1, starting transfers between devices, per_device(): got = lax.all_to_all(send, 'tp', 0, 0)  6.41 us
  transfers between devices with their start and end apart: 3, of which 3 were waited for; matrix products, arithmetic and copies ran while one was open for 0% of the time, Pallas kernels for 3%

profile of v3, /device:TPU:1, one launch (start us, length us, event | category | flops | bytes accessed | tf_op | source)
XLA Modules:
  0.0 113.3 jit_solution(15930956204752477436)
XLA Ops:
  0.0 0.9 slice_bitcast_fusion
  0.9 35.4 %all-gather.1.main_ref = bf16[16,127,256]{2,1,0:T(8,128)(2,1)S(1)} all-gather(bf16[1,127,256]{2,1,0:T(8,128)(2,1)S(1)} %slice_bitcast_fusion), channel_id=2, replica_groups=mesh['seq'=32,'tp'=16] {'tp'}, dimensions={0}, use_global_device_ids=true | all-gather | bytes 1105408 | tf_op jit(solution)/shard_map/all_gather | solution.py:331
  36.3 0.0 copy-start
  36.3 0.0 copy-start.1
  36.3 0.0 copy-start.2
  36.3 3.7 %shard_map.100 = (bf16[16,8,384]{2,1,0:T(8,128)(2,1)}, bf16[16,512]{1,0:T(8,128)(2,1)S(1)}, bf16[128,512]{1,0:T(8,128)(2,1)S(1)}) custom-call(bf16[16,127,256]{2,1,0:T(8,128)(2,1)S(1)} %all-gather.1.main_ref, bf16[128,256]{1,0:T(8,128)(2,1)} %tokens_hbm.1, bf16[4096,512]{1,0:T(8,128)(2,1)} %weight_hbm.3, f32[4,512]{1,0:T(4,128)} %taps_hbm.3, ...), custom_call_target="tpu_custom_call" | custom-call | flops 536870912 | bytes 8388608 | tf_op jit(solution)/shard_map/pallas_call | solution.py:299
  40.0 0.0 copy-start.4
  40.1 0.0 copy-start.3
  40.1 6.4 %all-to-all-start = ((bf16[16,8,384]{2,1,0:T(8,128)(2,1)}), bf16[16,8,384]{2,1,0:T(8,128)(2,1)S(1)}, u32[]{:S(2)}, u32[]{:S(2)}) async-start(bf16[16,8,384]{2,1,0:T(8,128)(2,1)} %get-tuple-element.15), calls=%async_computation | async-start | bytes 196608 | tf_op jit(solution)/shard_map/all_to_all | solution.py:343
  46.5 10.9 %collective-permute-start = (bf16[8,512]{1,0:T(8,128)(2,1)S(1)}, bf16[8,512]{1,0:T(8,128)(2,1)S(1)}, u32[]{:S(2)}, u32[]{:S(2)}) collective-permute-start(bf16[8,512]{1,0:T(8,128)(2,1)S(1)} %slice.7), channel_id=1, source_target_pairs={{0,16},{16,32},{32,48},{48,64},{64,80},{80,96},{96,112},{112,128},... | collective-permute-start | bytes 24584 | tf_op jit(solution)/shard_map/ppermute | solution.py:342
  57.4 0.8 collective-permute-done.rim_ref
  58.2 0.1 all-to-all-done.got_ref
  58.3 3.8 %shard_map.101 = (bf16[16,8,512]{2,1,0:T(8,128)(2,1)S(1)}, bf16[8,512]{1,0:T(8,128)(2,1)S(1)}) custom-call(bf16[16,8,384]{2,1,0:T(8,128)(2,1)S(1)} %all-to-all-done.got_ref, bf16[8,512]{1,0:T(8,128)(2,1)S(1)} %collective-permute-done.rim_ref, bf16[16,512]{1,0:T(8,128)(2,1)S(1)} %get-tuple-element.16.edge_ref, bf16[4096,512]{1,0:T(8,128)(2,1)} %weight_hbm.3, ...), custom_call_target="tpu_custom_call" | custom-call | flops 268435456 | bytes 4194304 | tf_op jit(solution)/shard_map/pallas_call | solution.py:299
  62.1 23.4 %all_to_all.15.mix_ref = bf16[16,8,512]{2,1,0:T(8,128)(2,1)S(1)} all-to-all(bf16[16,8,512]{2,1,0:T(8,128)(2,1)S(1)} %get-tuple-element.17), channel_id=1, replica_groups=mesh['seq'=32,'tp'=16] {'tp'}, dimensions={0} | all-to-all | bytes 262144 | tf_op jit(solution)/shard_map/all_to_all | solution.py:359
  85.6 0.0 copy-done
  85.6 0.0 copy-done.1
  85.6 0.0 copy-done.2
  85.6 2.6 %shard_map.102 = (f32[128,512]{1,0:T(8,128)S(1)}, f32[128,32]{1,0:T(8,128)S(1)}, bf16[32,72,128]{2,1,0:T(8,128)(2,1)}) custom-call(bf16[16,8,512]{2,1,0:T(8,128)(2,1)S(1)} %all_to_all.15.mix_ref, bf16[256,512]{1,0:T(8,128)(2,1)S(1)} %copy-done, f32[1,512]{1,0:T(1,128)S(1)} %bitcast.8, f32[16,512]{1,0:T(8,128)S(1)} %copy-done.1, ...), custom_call_target="tpu_custom_call" | custom-call | flops 67108864 | bytes 1048576 | tf_op jit(solution)/shard_map/pallas_call | solution.py:299
  88.2 10.5 %all-to-all-start.2 = ((bf16[32,72,128]{2,1,0:T(8,128)(2,1)}), bf16[32,72,128]{2,1,0:T(8,128)(2,1)S(1)}, u32[]{:S(2)}, u32[]{:S(2)}) async-start(bf16[32,72,128]{2,1,0:T(8,128)(2,1)} %get-tuple-element.20), calls=%async_computation.2 | async-start | bytes 1179648 | tf_op jit(solution)/shard_map/all_to_all | solution.py:375
  98.7 0.0 copy-done.4
  98.7 3.8 %shard_map.103 = (f32[128,512]{1,0:T(8,128)S(1)}, bf16[8,16,16,512]{3,2,1,0:T(8,128)(2,1)S(1)}) custom-call(f32[128,32]{1,0:T(8,128)S(1)} %get-tuple-element.21.coef_ref, f32[16,512]{1,0:T(8,128)S(1)} %copy-done.1, bf16[128,512]{1,0:T(8,128)(2,1)S(1)} %get-tuple-element.18.u_ref, bf16[8,512]{1,0:T(8,128)(2,1)S(1)} %get-tuple-element.19.late_u_ref, ...), custom_call_target="tpu_custom_call" | custom-call | flops 268435456 | bytes 4194304 | tf_op jit(solution)/shard_map/pallas_call | solution.py:299
  102.5 8.4 %all-to-all-done.2.all_ref = bf16[32,72,128]{2,1,0:T(8,128)(2,1)S(1)} async-done(((bf16[32,72,128]{2,1,0:T(8,128)(2,1)}), bf16[32,72,128]{2,1,0:T(8,128)(2,1)S(1)}, u32[]{:S(2)}, u32[]{:S(2)}) %all-to-all-start.2) | async-done | bytes 589856 | tf_op jit(solution)/shard_map/all_to_all | solution.py:375
  110.9 0.0 copy-done.3
  110.9 2.3 %shard_map.104 = bf16[128,512]{1,0:T(8,128)(2,1)} custom-call(s32[1]{0:T(128)} %bitcast.mine_ref, bf16[32,72,128]{2,1,0:T(8,128)(2,1)S(1)} %all-to-all-done.2.all_ref, f32[16,512]{1,0:T(8,128)S(1)} %copy-done.1, f32[128,512]{1,0:T(8,128)S(1)} %get-tuple-element.23.y_ref, bf16[8,16,16,512]{3,2,1,0:T(8,128)(2,1)S(1)} %get-tuple-element.24.grow_ref, ...), custom_call_target="tpu_custom_call" | custom-call | flops 67108864 | bytes 1048576 | tf_op jit(solution)/shard_map/pallas_call | solution.py:299
  (1 shorter events, 0.0 us)
Async XLA Ops:
  36.3 49.3 %copy-start = (bf16[256,512]{1,0:T(8,128)(2,1)S(1)}, bf16[256,512]{1,0:T(8,128)(2,1)}, u32[]{:S(2)}) copy-start(bf16[256,512]{1,0:T(8,128)(2,1)} %dtw_ref.1) | copy-start | bytes 786436
  36.3 49.3 %copy-start.1 = (f32[16,512]{1,0:T(8,128)S(1)}, f32[16,512]{1,0:T(8,128)}, u32[]{:S(2)}) copy-start(f32[16,512]{1,0:T(8,128)} %alog_ref.5) | copy-start | bytes 98308
  36.3 49.3 %copy-start.2 = (f32[512]{0:T(512)S(1)}, f32[512]{0:T(512)}, u32[]{:S(2)}) copy-start(f32[512]{0:T(512)} %param.16) | copy-start | bytes 6148
  40.0 58.6 %copy-start.4 = (f32[512]{0:T(512)S(1)}, f32[512]{0:T(512)}, u32[]{:S(2)}) copy-start(f32[512]{0:T(512)} %param.18) | copy-start | bytes 6148
  40.1 70.9 %copy-start.3 = (f32[512]{0:T(512)S(1)}, f32[512]{0:T(512)}, u32[]{:S(2)}) copy-start(f32[512]{0:T(512)} %param.19) | copy-start | bytes 6148
  40.1 18.3 %all-to-all-start = ((bf16[16,8,384]{2,1,0:T(8,128)(2,1)}), bf16[16,8,384]{2,1,0:T(8,128)(2,1)S(1)}, u32[]{:S(2)}, u32[]{:S(2)}) async-start(bf16[16,8,384]{2,1,0:T(8,128)(2,1)} %get-tuple-element.15), calls=%async_computation | async-start | bytes 196608 | tf_op jit(solution)/shard_map/all_to_all | solution.py:343
  46.5 11.7 %collective-permute-start = (bf16[8,512]{1,0:T(8,128)(2,1)S(1)}, bf16[8,512]{1,0:T(8,128)(2,1)S(1)}, u32[]{:S(2)}, u32[]{:S(2)}) collective-permute-start(bf16[8,512]{1,0:T(8,128)(2,1)S(1)} %slice.7), channel_id=1, source_target_pairs={{0,16},{16,32},{32,48},{48,64},{64,80},{80,96},{96,112},{112,128},... | collective-permute-start | bytes 24584 | tf_op jit(solution)/shard_map/ppermute | solution.py:342
  88.2 22.7 %all-to-all-start.2 = ((bf16[32,72,128]{2,1,0:T(8,128)(2,1)}), bf16[32,72,128]{2,1,0:T(8,128)(2,1)S(1)}, u32[]{:S(2)}, u32[]{:S(2)}) async-start(bf16[32,72,128]{2,1,0:T(8,128)(2,1)} %get-tuple-element.20), calls=%async_computation.2 | async-start | bytes 1179648 | tf_op jit(solution)/shard_map/all_to_all | solution.py:375

commit v4 on v3

--- a/solution.py
+++ b/solution.py
@@ -40,36 +40,50 @@
     return lax.dot_general(u, proj_ref[...], (((1,), (1,)), ((), ())), preferred_element_type=F32)
 
 
+AHEAD = 4
+KEEP = 10
+
+
 def fetches(pairs, sems):
-    copies = [pltpu.make_async_copy(src, dst, sems.at[i]) for i, (src, dst) in enumerate(pairs)]
-    for copy in copies:
-        copy.start()
-    return copies
-
-
-def weight_fetches(hbm_ref, buf_ref, shards, depth):
-    return [(hbm_ref.at[pl.ds(z * depth, depth)], buf_ref.at[pl.ds(z * depth, depth)]) for z in range(shards)]
+    return [pltpu.make_async_copy(src, dst, sems.at[i]) for i, (src, dst) in enumerate(pairs)]
+
+
+def weight_part(keep_ref, buf_ref, z, depth):
+    if z < KEEP:
+        return keep_ref.at[pl.ds(z * depth, depth)]
+    return buf_ref.at[pl.ds((z - KEEP) * depth, depth)]
+
+
+def weight_fetches(hbm_ref, keep_ref, buf_ref, first, shards, depth):
+    return [
+        (hbm_ref.at[pl.ds(z * depth, depth)], weight_part(keep_ref, buf_ref, z, depth))
+        for z in range(first, shards)
+    ]
 
 
 def project_kernel(
     main_ref, tokens_hbm, weight_hbm, taps_hbm, bias_hbm, proj_hbm,
-    send_ref, edge_ref, u_ref,
+    send_ref, edge_ref, u_ref, keep_ref,
     pad_ref, wide_ref, weight_ref, taps_ref, bias_ref, proj_ref, tokens_ref, sems,
 ):
     shards, held, depth = main_ref.shape
     rows, width = u_ref.shape
     sums = proj_ref.shape[0]
     copies = fetches(
-        weight_fetches(weight_hbm, weight_ref, shards, depth)
-        + [(taps_hbm, taps_ref), (bias_hbm, bias_ref), (proj_hbm, proj_ref),
+        weight_fetches(weight_hbm, keep_ref, weight_ref, 0, shards, depth)
+        + [(proj_hbm, proj_ref), (taps_hbm, taps_ref), (bias_hbm, bias_ref),
            (tokens_hbm.at[pl.ds(0, 8)], tokens_ref)],
         sems,
     )
+    for copy in copies[:AHEAD]:
+        copy.start()
     pad_ref[:16, :] = jnp.zeros((16, width), F32)
     acc = jnp.zeros((held, width), F32)
     for z in range(shards):
         copies[z].wait()
-        w = weight_ref[z * depth : (z + 1) * depth, :]
+        if z + AHEAD < len(copies):
+            copies[z + AHEAD].start()
+        w = weight_part(keep_ref, weight_ref, z, depth)[...]
         acc = acc + jnp.dot(main_ref[z], w, preferred_element_type=F32)
     for copy in copies[shards:]:
         copy.wait()
@@ -93,19 +107,21 @@
 
 
 def late_kernel(
-    got_ref, rim_ref, edge_ref, weight_hbm, taps_hbm, bias_hbm, proj_hbm,
+    got_ref, rim_ref, edge_ref, keep_ref, weight_hbm, taps_hbm, bias_hbm, proj_hbm,
     mix_ref, u_ref,
     wide_ref, first_ref, pad_ref, pay_ref, weight_ref, taps_ref, bias_ref, proj_ref, sems,
 ):
     shards, _, lanes = got_ref.shape
-    depth = weight_ref.shape[0] // shards
+    depth = first_ref.shape[1]
     width = weight_ref.shape[1]
     sums = proj_ref.shape[0]
     copies = fetches(
-        weight_fetches(weight_hbm, weight_ref, shards, depth)
-        + [(taps_hbm, taps_ref), (bias_hbm, bias_ref), (proj_hbm, proj_ref)],
+        weight_fetches(weight_hbm, keep_ref, weight_ref, KEEP, shards, depth)
+        + [(proj_hbm, proj_ref), (taps_hbm, taps_ref), (bias_hbm, bias_ref)],
         sems,
     )
+    for copy in copies:
+        copy.start()
     room = lanes - sums
     wide_ref[...] = got_ref[...].astype(F32)
     for p, (at, size) in enumerate(pieces(depth, room)):
@@ -123,10 +139,12 @@
     row_ids = lax.broadcasted_iota(jnp.int32, (shards, width), 0)
     acc = jnp.zeros((shards, width), F32)
     for z in range(shards):
-        copies[z].wait()
-        d = jnp.dot(first, weight_ref[z * depth : (z + 1) * depth, :], preferred_element_type=F32)
+        if z >= KEEP:
+            copies[z - KEEP].wait()
+        w = weight_part(keep_ref, weight_ref, z, depth)[...]
+        d = jnp.dot(first, w, preferred_element_type=F32)
         acc = acc + jnp.where(row_ids == z, d, 0.0)
-    for copy in copies[shards:]:
+    for copy in copies[shards - KEEP :]:
         copy.wait()
     pad_ref[8:9, :] = jnp.sum(acc, axis=0, keepdims=True).astype(BF16).astype(F32)
     u = convolve(taps_ref, bias_ref, pad_ref, 8, width)
@@ -321,17 +339,19 @@
     lanes = -(-sums // 128) * 128
     bias = conv_bias[None]
     proj = proj_weight.T
+    kept = (KEEP * tokens.shape[1], width)
     held = (
-        pltpu.VMEM(in_weight.shape, BF16),
+        pltpu.VMEM((in_weight.shape[0] - kept[0], width), BF16),
         pltpu.VMEM(conv_weight.shape, F32),
         pltpu.VMEM(bias.shape, F32),
         pltpu.VMEM(proj.shape, BF16),
     )
 
     main = lax.all_gather(tokens[1:], "tp")
-    send, edge, u = call(
+    send, edge, u, keep = call(
         project_kernel,
-        (struct((shards, 8, lanes), BF16), struct((16, width), BF16), struct((rows, width), BF16)),
+        (struct((shards, 8, lanes), BF16), struct((16, width), BF16), struct((rows, width), BF16),
+         struct(kept, BF16)),
         (main, tokens, in_weight, conv_weight, bias, proj),
         (pltpu.VMEM((rows + 8, width), F32), pltpu.VMEM((shards, 8, lanes), F32))
         + held
@@ -344,7 +364,7 @@
     mix, late_u = call(
         late_kernel,
         (struct((shards, 8, rank + 256), BF16), struct((8, width), BF16)),
-        (got, rim, edge, in_weight, conv_weight, bias, proj),
+        (got, rim, edge, keep, in_weight, conv_weight, bias, proj),
         (
             pltpu.VMEM((shards, 8, lanes), F32),
             pltpu.VMEM((shards, tokens.shape[1]), F32),
@@ -354,7 +374,7 @@
         + held
         + (pltpu.SemaphoreType.DMA((shards + 3,)),),
         flops=1 << 28,
-        specs=[VMEM] * 3 + [HBM] * 4,
+        specs=[VMEM] * 4 + [HBM] * 4,
     )
     mix = lax.all_to_all(mix, "tp", 0, 0)
     whole = struct((rows, width), F32)

time: 114 us -> 115 us (level)
  Pallas kernels: 16.3 us -> 17.6 us
    pallas_call x5, Pallas kernels: 16.3 us -> 17.6 us  [call(): pl.pallas_call(kernel, out_shape=outs, in_specs=specs, out_specs=jax.tree...]
where the time goes in v4:
time: 115 us
  blocking collectives  58.9 us (51%)
  starting transfers between devices  27.8 us (24%)
  Pallas kernels  17.6 us (15%)
  waiting for transfers between devices  9.28 us (8%)
    all_gather x1, blocking collectives, per_device(): main = lax.all_gather(tokens[1:], 'tp')  35.4 us
    all_to_all x1, blocking collectives, per_device(): mix = lax.all_to_all(mix, 'tp', 0, 0)  23.4 us
    pallas_call x5, Pallas kernels, call(): pl.pallas_call(kernel, out_shape=outs, in_specs=specs, out_specs=jax.tree...  17.6 us
    ppermute x1, starting transfers between devices, per_device(): rim = lax.ppermute(edge[:8], 'seq', [(i, i + 1) for i in range(peers - 1)])  10.9 us
    all_to_all x1, starting transfers between devices, per_device(): everyone = lax.all_to_all(pay, 'seq', 0, 0)  10.5 us
    all_to_all x1, waiting for transfers between devices, per_device(): everyone = lax.all_to_all(pay, 'seq', 0, 0)  8.4 us
    all_to_all x1, starting transfers between devices, per_device(): got = lax.all_to_all(send, 'tp', 0, 0)  6.4 us
  transfers between devices with their start and end apart: 3, of which 3 were waited for; matrix products, arithmetic and copies ran while one was open for 0% of the time, Pallas kernels for 3%

profile of v4, /device:TPU:1, one launch (start us, length us, event | category | flops | bytes accessed | tf_op | source)
XLA Modules:
  0.0 114.6 jit_solution(15807599168751412627)
XLA Ops:
  0.0 0.9 slice_bitcast_fusion
  0.9 35.4 %all-gather.1.main_ref = bf16[16,127,256]{2,1,0:T(8,128)(2,1)S(1)} all-gather(bf16[1,127,256]{2,1,0:T(8,128)(2,1)S(1)} %slice_bitcast_fusion), channel_id=2, replica_groups=mesh['seq'=32,'tp'=16] {'tp'}, dimensions={0}, use_global_device_ids=true | all-gather | bytes 1105408 | tf_op jit(solution)/shard_map/all_gather | solution.py:350
  36.3 6.3 %shard_map.100 = (bf16[16,8,384]{2,1,0:T(8,128)(2,1)}, bf16[16,512]{1,0:T(8,128)(2,1)S(1)}, bf16[128,512]{1,0:T(8,128)(2,1)S(1)}, bf16[2560,512]{1,0:T(8,128)(2,1)S(1)}) custom-call(bf16[16,127,256]{2,1,0:T(8,128)(2,1)S(1)} %all-gather.1.main_ref, bf16[128,256]{1,0:T(8,128)(2,1)} %tokens_hbm.1, bf16[4096,512]{1,0:T(8,128)(2,1)} %weight_hbm.3, ...), custom_call_target="tpu_custom_call" | custom-call | flops 536870912 | bytes 8388608 | tf_op jit(solution)/shard_map/pallas_call | solution.py:317
  42.6 6.4 %all-to-all-start = ((bf16[16,8,384]{2,1,0:T(8,128)(2,1)}), bf16[16,8,384]{2,1,0:T(8,128)(2,1)S(1)}, u32[]{:S(2)}, u32[]{:S(2)}) async-start(bf16[16,8,384]{2,1,0:T(8,128)(2,1)} %get-tuple-element.16), calls=%async_computation | async-start | bytes 196608 | tf_op jit(solution)/shard_map/all_to_all | solution.py:363
  49.0 10.9 %collective-permute-start = (bf16[8,512]{1,0:T(8,128)(2,1)S(1)}, bf16[8,512]{1,0:T(8,128)(2,1)S(1)}, u32[]{:S(2)}, u32[]{:S(2)}) collective-permute-start(bf16[8,512]{1,0:T(8,128)(2,1)S(1)} %slice.7), channel_id=1, source_target_pairs={{0,16},{16,32},{32,48},{48,64},{64,80},{80,96},{96,112},{112,128},... | collective-permute-start | bytes 24584 | tf_op jit(solution)/shard_map/ppermute | solution.py:362
  60.0 0.8 collective-permute-done.rim_ref
  60.7 0.1 all-to-all-done.got_ref
  60.8 0.0 copy-start
  60.8 0.0 copy-start.1
  60.8 0.0 copy-start.2
  60.9 0.0 copy-start.4
  60.9 2.6 %shard_map.101 = (bf16[16,8,512]{2,1,0:T(8,128)(2,1)S(1)}, bf16[8,512]{1,0:T(8,128)(2,1)S(1)}) custom-call(bf16[16,8,384]{2,1,0:T(8,128)(2,1)S(1)} %all-to-all-done.got_ref, bf16[8,512]{1,0:T(8,128)(2,1)S(1)} %collective-permute-done.rim_ref, bf16[16,512]{1,0:T(8,128)(2,1)S(1)} %get-tuple-element.17.edge_ref, ...), custom_call_target="tpu_custom_call" | custom-call | flops 268435456 | bytes 4194304 | tf_op jit(solution)/shard_map/pallas_call | solution.py:317
  63.5 0.0 copy-start.3
  63.5 23.4 %all_to_all.15.mix_ref = bf16[16,8,512]{2,1,0:T(8,128)(2,1)S(1)} all-to-all(bf16[16,8,512]{2,1,0:T(8,128)(2,1)S(1)} %get-tuple-element.19), channel_id=1, replica_groups=mesh['seq'=32,'tp'=16] {'tp'}, dimensions={0} | all-to-all | bytes 262144 | tf_op jit(solution)/shard_map/all_to_all | solution.py:379
  86.9 0.0 copy-done
  86.9 0.0 copy-done.1
  86.9 0.0 copy-done.2
  86.9 2.6 %shard_map.102 = (f32[128,512]{1,0:T(8,128)S(1)}, f32[128,32]{1,0:T(8,128)S(1)}, bf16[32,72,128]{2,1,0:T(8,128)(2,1)}) custom-call(bf16[16,8,512]{2,1,0:T(8,128)(2,1)S(1)} %all_to_all.15.mix_ref, bf16[256,512]{1,0:T(8,128)(2,1)S(1)} %copy-done, f32[1,512]{1,0:T(1,128)S(1)} %bitcast.8, f32[16,512]{1,0:T(8,128)S(1)} %copy-done.1, ...), custom_call_target="tpu_custom_call" | custom-call | flops 67108864 | bytes 1048576 | tf_op jit(solution)/shard_map/pallas_call | solution.py:317
  89.5 10.5 %all-to-all-start.2 = ((bf16[32,72,128]{2,1,0:T(8,128)(2,1)}), bf16[32,72,128]{2,1,0:T(8,128)(2,1)S(1)}, u32[]{:S(2)}, u32[]{:S(2)}) async-start(bf16[32,72,128]{2,1,0:T(8,128)(2,1)} %get-tuple-element.22), calls=%async_computation.2 | async-start | bytes 1179648 | tf_op jit(solution)/shard_map/all_to_all | solution.py:395
  100.0 0.0 copy-done.4
  100.0 3.8 %shard_map.103 = (f32[128,512]{1,0:T(8,128)S(1)}, bf16[8,16,16,512]{3,2,1,0:T(8,128)(2,1)S(1)}) custom-call(f32[128,32]{1,0:T(8,128)S(1)} %get-tuple-element.23.coef_ref, f32[16,512]{1,0:T(8,128)S(1)} %copy-done.1, bf16[128,512]{1,0:T(8,128)(2,1)S(1)} %get-tuple-element.20.u_ref, bf16[8,512]{1,0:T(8,128)(2,1)S(1)} %get-tuple-element.21.late_u_ref, ...), custom_call_target="tpu_custom_call" | custom-call | flops 268435456 | bytes 4194304 | tf_op jit(solution)/shard_map/pallas_call | solution.py:317
  103.9 8.4 %all-to-all-done.2.all_ref = bf16[32,72,128]{2,1,0:T(8,128)(2,1)S(1)} async-done(((bf16[32,72,128]{2,1,0:T(8,128)(2,1)}), bf16[32,72,128]{2,1,0:T(8,128)(2,1)S(1)}, u32[]{:S(2)}, u32[]{:S(2)}) %all-to-all-start.2) | async-done | bytes 589856 | tf_op jit(solution)/shard_map/all_to_all | solution.py:395
  112.3 0.0 copy-done.3
  112.3 2.3 %shard_map.104 = bf16[128,512]{1,0:T(8,128)(2,1)} custom-call(s32[1]{0:T(128)} %bitcast.mine_ref, bf16[32,72,128]{2,1,0:T(8,128)(2,1)S(1)} %all-to-all-done.2.all_ref, f32[16,512]{1,0:T(8,128)S(1)} %copy-done.1, f32[128,512]{1,0:T(8,128)S(1)} %get-tuple-element.25.y_ref, bf16[8,16,16,512]{3,2,1,0:T(8,128)(2,1)S(1)} %get-tuple-element.26.grow_ref, ...), custom_call_target="tpu_custom_call" | custom-call | flops 67108864 | bytes 1048576 | tf_op jit(solution)/shard_map/pallas_call | solution.py:317
  (1 shorter events, 0.0 us)
Async XLA Ops:
  42.6 18.3 %all-to-all-start = ((bf16[16,8,384]{2,1,0:T(8,128)(2,1)}), bf16[16,8,384]{2,1,0:T(8,128)(2,1)S(1)}, u32[]{:S(2)}, u32[]{:S(2)}) async-start(bf16[16,8,384]{2,1,0:T(8,128)(2,1)} %get-tuple-element.16), calls=%async_computation | async-start | bytes 196608 | tf_op jit(solution)/shard_map/all_to_all | solution.py:363
  49.0 11.7 %collective-permute-start = (bf16[8,512]{1,0:T(8,128)(2,1)S(1)}, bf16[8,512]{1,0:T(8,128)(2,1)S(1)}, u32[]{:S(2)}, u32[]{:S(2)}) collective-permute-start(bf16[8,512]{1,0:T(8,128)(2,1)S(1)} %slice.7), channel_id=1, source_target_pairs={{0,16},{16,32},{32,48},{48,64},{64,80},{80,96},{96,112},{112,128},... | collective-permute-start | bytes 24584 | tf_op jit(solution)/shard_map/ppermute | solution.py:362
  60.8 26.1 %copy-start = (bf16[256,512]{1,0:T(8,128)(2,1)S(1)}, bf16[256,512]{1,0:T(8,128)(2,1)}, u32[]{:S(2)}) copy-start(bf16[256,512]{1,0:T(8,128)(2,1)} %dtw_ref.1) | copy-start | bytes 786436
  60.8 26.1 %copy-start.1 = (f32[16,512]{1,0:T(8,128)S(1)}, f32[16,512]{1,0:T(8,128)}, u32[]{:S(2)}) copy-start(f32[16,512]{1,0:T(8,128)} %alog_ref.5) | copy-start | bytes 98308
  60.8 26.1 %copy-start.2 = (f32[512]{0:T(512)S(1)}, f32[512]{0:T(512)}, u32[]{:S(2)}) copy-start(f32[512]{0:T(512)} %param.16) | copy-start | bytes 6148
  60.9 39.2 %copy-start.4 = (f32[512]{0:T(512)S(1)}, f32[512]{0:T(512)}, u32[]{:S(2)}) copy-start(f32[512]{0:T(512)} %param.18) | copy-start | bytes 6148
  63.5 48.8 %copy-start.3 = (f32[512]{0:T(512)S(1)}, f32[512]{0:T(512)}, u32[]{:S(2)}) copy-start(f32[512]{0:T(512)} %param.19) | copy-start | bytes 6148
  89.5 22.7 %all-to-all-start.2 = ((bf16[32,72,128]{2,1,0:T(8,128)(2,1)}), bf16[32,72,128]{2,1,0:T(8,128)(2,1)S(1)}, u32[]{:S(2)}, u32[]{:S(2)}) async-start(bf16[32,72,128]{2,1,0:T(8,128)(2,1)} %get-tuple-element.22), calls=%async_computation.2 | async-start | bytes 1179648 | tf_op jit(solution)/shard_map/all_to_all | solution.py:395

commit v5 on v4

--- a/solution.py
+++ b/solution.py
@@ -40,8 +40,7 @@
     return lax.dot_general(u, proj_ref[...], (((1,), (1,)), ((), ())), preferred_element_type=F32)
 
 
-AHEAD = 4
-KEEP = 10
+KEEP = 12
 
 
 def fetches(pairs, sems):
@@ -54,38 +53,35 @@
     return buf_ref.at[pl.ds((z - KEEP) * depth, depth)]
 
 
-def weight_fetches(hbm_ref, keep_ref, buf_ref, first, shards, depth):
-    return [
-        (hbm_ref.at[pl.ds(z * depth, depth)], weight_part(keep_ref, buf_ref, z, depth))
-        for z in range(first, shards)
-    ]
+def rows_kernel(tokens_hbm, out_ref, tokens_ref, sem):
+    copy = pltpu.make_async_copy(tokens_hbm, tokens_ref, sem)
+    copy.start()
+    copy.wait()
+    out_ref[...] = tokens_ref[...].astype(F32)[1:, :].astype(BF16)
 
 
 def project_kernel(
-    main_ref, tokens_hbm, weight_hbm, taps_hbm, bias_hbm, proj_hbm,
+    main_ref, weight_ref, tokens_hbm, taps_hbm, bias_hbm, proj_hbm,
     send_ref, edge_ref, u_ref, keep_ref,
-    pad_ref, wide_ref, weight_ref, taps_ref, bias_ref, proj_ref, tokens_ref, sems,
+    pad_ref, wide_ref, taps_ref, bias_ref, proj_ref, tokens_ref, sems,
 ):
     shards, held, depth = main_ref.shape
     rows, width = u_ref.shape
     sums = proj_ref.shape[0]
     copies = fetches(
-        weight_fetches(weight_hbm, keep_ref, weight_ref, 0, shards, depth)
-        + [(proj_hbm, proj_ref), (taps_hbm, taps_ref), (bias_hbm, bias_ref),
-           (tokens_hbm.at[pl.ds(0, 8)], tokens_ref)],
+        [(proj_hbm, proj_ref), (taps_hbm, taps_ref), (bias_hbm, bias_ref),
+         (tokens_hbm.at[pl.ds(0, 8)], tokens_ref),
+         (weight_ref.at[pl.ds(0, KEEP * depth)], keep_ref)],
         sems,
     )
-    for copy in copies[:AHEAD]:
+    for copy in copies:
         copy.start()
     pad_ref[:16, :] = jnp.zeros((16, width), F32)
     acc = jnp.zeros((held, width), F32)
     for z in range(shards):
-        copies[z].wait()
-        if z + AHEAD < len(copies):
-            copies[z + AHEAD].start()
-        w = weight_part(keep_ref, weight_ref, z, depth)[...]
+        w = weight_ref[z * depth : (z + 1) * depth, :]
         acc = acc + jnp.dot(main_ref[z], w, preferred_element_type=F32)
-    for copy in copies[shards:]:
+    for copy in copies[:4]:
         copy.wait()
     pad_ref[8 + rows - held :, :] = acc.astype(BF16).astype(F32)
     edge_ref[:8, :] = pad_ref[rows : rows + 8, :].astype(BF16)
@@ -104,6 +100,7 @@
         block = jnp.where(row_ids == p, jnp.broadcast_to(piece, (8, room)), block)
     wide_ref[:, :, sums:] = jnp.broadcast_to(block[None], (shards, 8, room))
     send_ref[...] = wide_ref[...].astype(BF16)
+    copies[4].wait()
 
 
 def late_kernel(
@@ -116,7 +113,10 @@
     width = weight_ref.shape[1]
     sums = proj_ref.shape[0]
     copies = fetches(
-        weight_fetches(weight_hbm, keep_ref, weight_ref, KEEP, shards, depth)
+        [
+            (weight_hbm.at[pl.ds(z * depth, depth)], weight_part(keep_ref, weight_ref, z, depth))
+            for z in range(KEEP, shards)
+        ]
         + [(proj_hbm, proj_ref), (taps_hbm, taps_ref), (bias_hbm, bias_ref)],
         sems,
     )
@@ -341,23 +341,30 @@
     proj = proj_weight.T
     kept = (KEEP * tokens.shape[1], width)
     held = (
-        pltpu.VMEM((in_weight.shape[0] - kept[0], width), BF16),
         pltpu.VMEM(conv_weight.shape, F32),
         pltpu.VMEM(bias.shape, F32),
         pltpu.VMEM(proj.shape, BF16),
     )
 
-    main = lax.all_gather(tokens[1:], "tp")
+    most = call(
+        rows_kernel,
+        struct((rows - 1, tokens.shape[1]), BF16),
+        (tokens,),
+        (pltpu.VMEM(tokens.shape, BF16), pltpu.SemaphoreType.DMA),
+        flops=1 << 34,
+        specs=[HBM],
+    )
+    main = lax.all_gather(most, "tp")
     send, edge, u, keep = call(
         project_kernel,
         (struct((shards, 8, lanes), BF16), struct((16, width), BF16), struct((rows, width), BF16),
          struct(kept, BF16)),
-        (main, tokens, in_weight, conv_weight, bias, proj),
+        (main, in_weight, tokens, conv_weight, bias, proj),
         (pltpu.VMEM((rows + 8, width), F32), pltpu.VMEM((shards, 8, lanes), F32))
         + held
-        + (pltpu.VMEM((8, tokens.shape[1]), BF16), pltpu.SemaphoreType.DMA((shards + 4,))),
+        + (pltpu.VMEM((8, tokens.shape[1]), BF16), pltpu.SemaphoreType.DMA((5,))),
         flops=1 << 29,
-        specs=[VMEM] + [HBM] * 5,
+        specs=[VMEM] * 2 + [HBM] * 4,
     )
     rim = lax.ppermute(edge[:8], "seq", [(i, i + 1) for i in range(peers - 1)])
     got = lax.all_to_all(send, "tp", 0, 0)
@@ -371,6 +378,7 @@
             pltpu.VMEM((16, width), F32),
             pltpu.VMEM((8, rank + 256), F32),
         )
+        + (pltpu.VMEM((in_weight.shape[0] - kept[0], width), BF16),)
         + held
         + (pltpu.SemaphoreType.DMA((shards + 3,)),),
         flops=1 << 28,

time: 115 us -> 111 us (0.965)
  Pallas kernels: 17.6 us -> 14.2 us
    pallas_call x5 -> x6, Pallas kernels: 17.6 us -> 14.2 us  [call(): pl.pallas_call(kernel, out_shape=outs, in_specs=specs, out_specs=jax.tree...]
where the time goes in v5:
time: 111 us; the launch traced here: 110 us
  blocking collectives  59 us (53%)
  starting transfers between devices  27.8 us (25%)
  Pallas kernels  14.2 us (13%)
  waiting for transfers between devices  9.31 us (8%)
    all_gather x1, blocking collectives, per_device(): main = lax.all_gather(most, 'tp')  35.6 us
    all_to_all x1, blocking collectives, per_device(): mix = lax.all_to_all(mix, 'tp', 0, 0)  23.4 us
    pallas_call x6, Pallas kernels, call(): pl.pallas_call(kernel, out_shape=outs, in_specs=specs, out_specs=jax.tree...  14.2 us
    ppermute x1, starting transfers between devices, per_device(): rim = lax.ppermute(edge[:8], 'seq', [(i, i + 1) for i in range(peers - 1)])  10.9 us
    all_to_all x1, starting transfers between devices, per_device(): everyone = lax.all_to_all(pay, 'seq', 0, 0)  10.5 us
    all_to_all x1, waiting for transfers between devices, per_device(): everyone = lax.all_to_all(pay, 'seq', 0, 0)  8.42 us
    all_to_all x1, starting transfers between devices, per_device(): got = lax.all_to_all(send, 'tp', 0, 0)  6.41 us
  transfers between devices with their start and end apart: 3, of which 3 were waited for; matrix products, arithmetic and copies ran while one was open for 0% of the time, Pallas kernels for 3%

profile of v5, /device:TPU:1, one launch (start us, length us, event | category | flops | bytes accessed | tf_op | source)
XLA Modules:
  0.0 110.5 jit_solution(13336733461462255897)
XLA Ops:
  0.0 0.0 copy-start
  0.0 1.0 shard_map.100
  1.0 35.6 %all-gather.1.main_ref = bf16[16,127,256]{2,1,0:T(8,128)(2,1)S(1)} all-gather(bf16[1,127,256]{2,1,0:T(8,128)(2,1)S(1)} %bitcast.7), channel_id=2, replica_groups=mesh['seq'=32,'tp'=16] {'tp'}, dimensions={0}, use_global_device_ids=true | all-gather | bytes 1105408 | tf_op jit(solution)/shard_map/all_gather | solution.py:357
  36.6 0.0 copy-done
  36.6 2.1 %shard_map.101 = (bf16[16,8,384]{2,1,0:T(8,128)(2,1)}, bf16[16,512]{1,0:T(8,128)(2,1)S(1)}, bf16[128,512]{1,0:T(8,128)(2,1)S(1)}, bf16[3072,512]{1,0:T(8,128)(2,1)S(1)}) custom-call(bf16[16,127,256]{2,1,0:T(8,128)(2,1)S(1)} %all-gather.1.main_ref, bf16[4096,512]{1,0:T(8,128)(2,1)S(1)} %copy-done, bf16[128,256]{1,0:T(8,128)(2,1)} %tokens_hbm.3, ...), custom_call_target="tpu_custom_call" | custom-call | flops 536870912 | bytes 8388608 | tf_op jit(solution)/shard_map/pallas_call | solution.py:317
  38.7 6.4 %all-to-all-start = ((bf16[16,8,384]{2,1,0:T(8,128)(2,1)}), bf16[16,8,384]{2,1,0:T(8,128)(2,1)S(1)}, u32[]{:S(2)}, u32[]{:S(2)}) async-start(bf16[16,8,384]{2,1,0:T(8,128)(2,1)} %get-tuple-element.16), calls=%async_computation | async-start | bytes 196608 | tf_op jit(solution)/shard_map/all_to_all | solution.py:370
  45.1 10.9 %collective-permute-start = (bf16[8,512]{1,0:T(8,128)(2,1)S(1)}, bf16[8,512]{1,0:T(8,128)(2,1)S(1)}, u32[]{:S(2)}, u32[]{:S(2)}) collective-permute-start(bf16[8,512]{1,0:T(8,128)(2,1)S(1)} %slice.3), channel_id=1, source_target_pairs={{0,16},{16,32},{32,48},{48,64},{64,80},{80,96},{96,112},{112,128},... | collective-permute-start | bytes 24584 | tf_op jit(solution)/shard_map/ppermute | solution.py:369
  56.1 0.8 collective-permute-done.rim_ref
  56.9 0.1 all-to-all-done.got_ref
  57.0 0.0 copy-start.1
  57.0 0.0 copy-start.2
  57.0 0.0 copy-start.3
  57.0 0.0 copy-start.5
  57.0 0.0 copy-start.4
  57.0 2.3 %shard_map.102 = (bf16[16,8,512]{2,1,0:T(8,128)(2,1)S(1)}, bf16[8,512]{1,0:T(8,128)(2,1)S(1)}) custom-call(bf16[16,8,384]{2,1,0:T(8,128)(2,1)S(1)} %all-to-all-done.got_ref, bf16[8,512]{1,0:T(8,128)(2,1)S(1)} %collective-permute-done.rim_ref, bf16[16,512]{1,0:T(8,128)(2,1)S(1)} %get-tuple-element.17.edge_ref, ...), custom_call_target="tpu_custom_call" | custom-call | flops 268435456 | bytes 4194304 | tf_op jit(solution)/shard_map/pallas_call | solution.py:317
  59.3 23.4 %all_to_all.15.mix_ref = bf16[16,8,512]{2,1,0:T(8,128)(2,1)S(1)} all-to-all(bf16[16,8,512]{2,1,0:T(8,128)(2,1)S(1)} %get-tuple-element.19), channel_id=1, replica_groups=mesh['seq'=32,'tp'=16] {'tp'}, dimensions={0} | all-to-all | bytes 262144 | tf_op jit(solution)/shard_map/all_to_all | solution.py:387
  82.8 0.0 copy-done.1
  82.8 0.0 copy-done.2
  82.8 0.0 copy-done.3
  82.8 2.6 %shard_map.103 = (f32[128,512]{1,0:T(8,128)S(1)}, f32[128,32]{1,0:T(8,128)S(1)}, bf16[32,72,128]{2,1,0:T(8,128)(2,1)}) custom-call(bf16[16,8,512]{2,1,0:T(8,128)(2,1)S(1)} %all_to_all.15.mix_ref, bf16[256,512]{1,0:T(8,128)(2,1)S(1)} %copy-done.1, f32[1,512]{1,0:T(1,128)S(1)} %bitcast.8, f32[16,512]{1,0:T(8,128)S(1)} %copy-done.2, ...), custom_call_target="tpu_custom_call" | custom-call | flops 67108864 | bytes 1048576 | tf_op jit(solution)/shard_map/pallas_call | solution.py:317
  85.4 10.5 %all-to-all-start.2 = ((bf16[32,72,128]{2,1,0:T(8,128)(2,1)}), bf16[32,72,128]{2,1,0:T(8,128)(2,1)S(1)}, u32[]{:S(2)}, u32[]{:S(2)}) async-start(bf16[32,72,128]{2,1,0:T(8,128)(2,1)} %get-tuple-element.22), calls=%async_computation.2 | async-start | bytes 1179648 | tf_op jit(solution)/shard_map/all_to_all | solution.py:403
  95.9 0.0 copy-done.5
  95.9 3.8 %shard_map.104 = (f32[128,512]{1,0:T(8,128)S(1)}, bf16[8,16,16,512]{3,2,1,0:T(8,128)(2,1)S(1)}) custom-call(f32[128,32]{1,0:T(8,128)S(1)} %get-tuple-element.23.coef_ref, f32[16,512]{1,0:T(8,128)S(1)} %copy-done.2, bf16[128,512]{1,0:T(8,128)(2,1)S(1)} %get-tuple-element.20.u_ref, bf16[8,512]{1,0:T(8,128)(2,1)S(1)} %get-tuple-element.21.late_u_ref, ...), custom_call_target="tpu_custom_call" | custom-call | flops 268435456 | bytes 4194304 | tf_op jit(solution)/shard_map/pallas_call | solution.py:317
  99.7 8.4 %all-to-all-done.2.all_ref = bf16[32,72,128]{2,1,0:T(8,128)(2,1)S(1)} async-done(((bf16[32,72,128]{2,1,0:T(8,128)(2,1)}), bf16[32,72,128]{2,1,0:T(8,128)(2,1)S(1)}, u32[]{:S(2)}, u32[]{:S(2)}) %all-to-all-start.2) | async-done | bytes 589856 | tf_op jit(solution)/shard_map/all_to_all | solution.py:403
  108.1 0.0 copy-done.4
  108.1 2.3 %shard_map.105 = bf16[128,512]{1,0:T(8,128)(2,1)} custom-call(s32[1]{0:T(128)} %bitcast.mine_ref, bf16[32,72,128]{2,1,0:T(8,128)(2,1)S(1)} %all-to-all-done.2.all_ref, f32[16,512]{1,0:T(8,128)S(1)} %copy-done.2, f32[128,512]{1,0:T(8,128)S(1)} %get-tuple-element.25.y_ref, bf16[8,16,16,512]{3,2,1,0:T(8,128)(2,1)S(1)} %get-tuple-element.26.grow_ref, ...), custom_call_target="tpu_custom_call" | custom-call | flops 67108864 | bytes 1048576 | tf_op jit(solution)/shard_map/pallas_call | solution.py:317
  (1 shorter events, 0.0 us)
Async XLA Ops:
  0.0 36.6 %copy-start = (bf16[4096,512]{1,0:T(8,128)(2,1)S(1)}, bf16[4096,512]{1,0:T(8,128)(2,1)}, u32[]{:S(2)}) copy-start(bf16[4096,512]{1,0:T(8,128)(2,1)} %weight_hbm.1) | copy-start | bytes 12582916
  38.7 18.3 %all-to-all-start = ((bf16[16,8,384]{2,1,0:T(8,128)(2,1)}), bf16[16,8,384]{2,1,0:T(8,128)(2,1)S(1)}, u32[]{:S(2)}, u32[]{:S(2)}) async-start(bf16[16,8,384]{2,1,0:T(8,128)(2,1)} %get-tuple-element.16), calls=%async_computation | async-start | bytes 196608 | tf_op jit(solution)/shard_map/all_to_all | solution.py:370
  45.1 11.7 %collective-permute-start = (bf16[8,512]{1,0:T(8,128)(2,1)S(1)}, bf16[8,512]{1,0:T(8,128)(2,1)S(1)}, u32[]{:S(2)}, u32[]{:S(2)}) collective-permute-start(bf16[8,512]{1,0:T(8,128)(2,1)S(1)} %slice.3), channel_id=1, source_target_pairs={{0,16},{16,32},{32,48},{48,64},{64,80},{80,96},{96,112},{112,128},... | collective-permute-start | bytes 24584 | tf_op jit(solution)/shard_map/ppermute | solution.py:369
  57.0 25.8 %copy-start.1 = (bf16[256,512]{1,0:T(8,128)(2,1)S(1)}, bf16[256,512]{1,0:T(8,128)(2,1)}, u32[]{:S(2)}) copy-start(bf16[256,512]{1,0:T(8,128)(2,1)} %dtw_ref.1) | copy-start | bytes 786436
  57.0 25.8 %copy-start.2 = (f32[16,512]{1,0:T(8,128)S(1)}, f32[16,512]{1,0:T(8,128)}, u32[]{:S(2)}) copy-start(f32[16,512]{1,0:T(8,128)} %alog_ref.5) | copy-start | bytes 98308
  57.0 25.8 %copy-start.3 = (f32[512]{0:T(512)S(1)}, f32[512]{0:T(512)}, u32[]{:S(2)}) copy-start(f32[512]{0:T(512)} %param.16) | copy-start | bytes 6148
  57.0 38.9 %copy-start.5 = (f32[512]{0:T(512)S(1)}, f32[512]{0:T(512)}, u32[]{:S(2)}) copy-start(f32[512]{0:T(512)} %param.18) | copy-start | bytes 6148
  57.0 51.2 %copy-start.4 = (f32[512]{0:T(512)S(1)}, f32[512]{0:T(512)}, u32[]{:S(2)}) copy-start(f32[512]{0:T(512)} %param.19) | copy-start | bytes 6148
  85.4 22.7 %all-to-all-start.2 = ((bf16[32,72,128]{2,1,0:T(8,128)(2,1)}), bf16[32,72,128]{2,1,0:T(8,128)(2,1)S(1)}, u32[]{:S(2)}, u32[]{:S(2)}) async-start(bf16[32,72,128]{2,1,0:T(8,128)(2,1)} %get-tuple-element.22), calls=%async_computation.2 | async-start | bytes 1179648 | tf_op jit(solution)/shard_map/all_to_all | solution.py:403

commit v6 on v5

--- a/solution.py
+++ b/solution.py
@@ -178,8 +178,8 @@
 
 def state_kernel(
     mix_ref, dtw_ref, dtb_ref, alog_ref, u_ref, late_u_ref,
-    step_ref, coef_ref, pay_ref,
-    uf_ref, flow_ref, left_ref, bx_ref, end_ref, low_ref,
+    step_ref, coef_ref, pay_hbm,
+    uf_ref, flow_ref, left_ref, bx_ref, end_ref, low_ref, pack_ref, sems,
 ):
     shards, each, _ = mix_ref.shape
     rows, width = u_ref.shape
@@ -219,14 +219,19 @@
             grow = jnp.exp2(rate_g * left_ref[i, :, lanes][None])
             return acc + grow * (flow_ref[i, :, lanes][None] * bx_ref[i])
 
-        acc = lax.fori_loop(0, tiles, turn, jnp.zeros((n, 8, 128), F32), unroll=2)
+        acc = lax.fori_loop(0, tiles, turn, jnp.zeros((n, 8, 128), F32), unroll=tiles)
         hi, lo, _ = split3(whole[:, lanes])
         end_ref[g * n : (g + 1) * n, :] = jnp.sum(acc, axis=1)
         end_ref[groups * n + g : groups * n + g + 1, :] = hi.astype(F32)
         end_ref[groups * n + groups + g : groups * n + groups + g + 1, :] = lo.astype(F32)
-    end = end_ref[...].astype(BF16)
-    for p in range(pay_ref.shape[0]):
-        pay_ref[p] = end
+    pack_ref[...] = end_ref[...].astype(BF16)
+    copies = [
+        pltpu.make_async_copy(pack_ref, pay_hbm.at[p], sems.at[p]) for p in range(pay_hbm.shape[0])
+    ]
+    for copy in copies:
+        copy.start()
+    for copy in copies:
+        copy.wait()
 
 
 def local_kernel(
@@ -305,20 +310,19 @@
         def turn(i, _):
             at = pl.ds(pl.multiple_of(i * 16, 16), 16)
             y = y_ref[at, lanes] + jnp.sum(grow_ref[i, :, :, lanes].astype(F32) * entry_g, axis=0)
-            y_ref[at, lanes] = y / (1.0 + jnp.exp(-4.0 * (y - thr)))
+            out_ref[at, lanes] = (y / (1.0 + jnp.exp(-4.0 * (y - thr)))).astype(BF16)
             return 0
 
-        lax.fori_loop(0, blocks, turn, 0)
-    out_ref[...] = y_ref[...].astype(BF16)
-
-
-def call(kernel, outs, ins, scratch=(), flops=0, specs=None, vmem=12 << 20):
+        lax.fori_loop(0, blocks, turn, 0, unroll=blocks)
+
+
+def call(kernel, outs, ins, scratch=(), flops=0, specs=None, vmem=12 << 20, outs_in=None):
     specs = specs or [VMEM] * len(ins)
     return pl.pallas_call(
         kernel,
         out_shape=outs,
         in_specs=specs,
-        out_specs=jax.tree.map(lambda _: VMEM, outs),
+        out_specs=outs_in or jax.tree.map(lambda _: VMEM, outs),
         scratch_shapes=scratch,
         cost_estimate=pl.CostEstimate(flops=flops, bytes_accessed=flops // 64, transcendentals=0),
         compiler_params=pltpu.CompilerParams(vmem_limit_bytes=vmem),
@@ -397,8 +401,11 @@
             pltpu.VMEM((rows // 8, n, 8, 128), F32),
             pltpu.VMEM(((n + 2) * width // 128, 128), F32),
             pltpu.VMEM((rows, rank), F32),
+            pltpu.VMEM(((n + 2) * width // 128, 128), BF16),
+            pltpu.SemaphoreType.DMA((peers,)),
         ),
         flops=1 << 26,
+        outs_in=(VMEM, VMEM, HBM),
     )
     everyone = lax.all_to_all(pay, "seq", 0, 0)
     y_local, grow = call(

time: 111 us -> 110 us (level)
  no operation moved by 1% of the time
where the time goes in v6:
time: 110 us
  blocking collectives  59 us (54%)
  starting transfers between devices  27.8 us (25%)
  Pallas kernels  13.4 us (12%)
  waiting for transfers between devices  9.31 us (8%)
    all_gather x1, blocking collectives, per_device(): main = lax.all_gather(most, 'tp')  35.6 us
    all_to_all x1, blocking collectives, per_device(): mix = lax.all_to_all(mix, 'tp', 0, 0)  23.4 us
    pallas_call x6, Pallas kernels, call(): pl.pallas_call(kernel, out_shape=outs, in_specs=specs, out_specs=outs_in...  13.4 us
    ppermute x1, starting transfers between devices, per_device(): rim = lax.ppermute(edge[:8], 'seq', [(i, i + 1) for i in range(peers - 1)])  10.9 us
    all_to_all x1, starting transfers between devices, per_device(): everyone = lax.all_to_all(pay, 'seq', 0, 0)  10.5 us
    all_to_all x1, waiting for transfers between devices, per_device(): everyone = lax.all_to_all(pay, 'seq', 0, 0)  8.42 us
    all_to_all x1, starting transfers between devices, per_device(): got = lax.all_to_all(send, 'tp', 0, 0)  6.41 us
  transfers between devices with their start and end apart: 3, of which 3 were waited for; matrix products, arithmetic and copies ran while one was open for 0% of the time, Pallas kernels for 3%

profile of v6, /device:TPU:1, one launch (start us, length us, event | category | flops | bytes accessed | tf_op | source)
XLA Modules:
  0.0 109.7 jit_solution(2692595949931565347)
XLA Ops:
  0.0 0.0 copy-start
  0.0 1.0 shard_map.100
  1.0 35.6 %all-gather.1.main_ref = bf16[16,127,256]{2,1,0:T(8,128)(2,1)S(1)} all-gather(bf16[1,127,256]{2,1,0:T(8,128)(2,1)S(1)} %bitcast.7), channel_id=2, replica_groups=mesh['seq'=32,'tp'=16] {'tp'}, dimensions={0}, use_global_device_ids=true | all-gather | bytes 1105408 | tf_op jit(solution)/shard_map/all_gather | solution.py:361
  36.6 0.0 copy-done
  36.6 2.1 %shard_map.101 = (bf16[16,8,384]{2,1,0:T(8,128)(2,1)}, bf16[16,512]{1,0:T(8,128)(2,1)S(1)}, bf16[128,512]{1,0:T(8,128)(2,1)S(1)}, bf16[3072,512]{1,0:T(8,128)(2,1)S(1)}) custom-call(bf16[16,127,256]{2,1,0:T(8,128)(2,1)S(1)} %all-gather.1.main_ref, bf16[4096,512]{1,0:T(8,128)(2,1)S(1)} %copy-done, bf16[128,256]{1,0:T(8,128)(2,1)} %tokens_hbm.3, ...), custom_call_target="tpu_custom_call" | custom-call | flops 536870912 | bytes 8388608 | tf_op jit(solution)/shard_map/pallas_call | solution.py:321
  38.7 6.4 %all-to-all-start = ((bf16[16,8,384]{2,1,0:T(8,128)(2,1)}), bf16[16,8,384]{2,1,0:T(8,128)(2,1)S(1)}, u32[]{:S(2)}, u32[]{:S(2)}) async-start(bf16[16,8,384]{2,1,0:T(8,128)(2,1)} %get-tuple-element.16), calls=%async_computation | async-start | bytes 196608 | tf_op jit(solution)/shard_map/all_to_all | solution.py:374
  45.1 10.9 %collective-permute-start = (bf16[8,512]{1,0:T(8,128)(2,1)S(1)}, bf16[8,512]{1,0:T(8,128)(2,1)S(1)}, u32[]{:S(2)}, u32[]{:S(2)}) collective-permute-start(bf16[8,512]{1,0:T(8,128)(2,1)S(1)} %slice.3), channel_id=1, source_target_pairs={{0,16},{16,32},{32,48},{48,64},{64,80},{80,96},{96,112},{112,128},... | collective-permute-start | bytes 24584 | tf_op jit(solution)/shard_map/ppermute | solution.py:373
  56.1 0.8 collective-permute-done.rim_ref
  56.9 0.1 all-to-all-done.got_ref
  57.0 0.0 copy-start.1
  57.0 0.0 copy-start.2
  57.0 0.0 copy-start.3
  57.0 0.0 copy-start.5
  57.0 0.0 copy-start.4
  57.0 2.3 %shard_map.102 = (bf16[16,8,512]{2,1,0:T(8,128)(2,1)S(1)}, bf16[8,512]{1,0:T(8,128)(2,1)S(1)}) custom-call(bf16[16,8,384]{2,1,0:T(8,128)(2,1)S(1)} %all-to-all-done.got_ref, bf16[8,512]{1,0:T(8,128)(2,1)S(1)} %collective-permute-done.rim_ref, bf16[16,512]{1,0:T(8,128)(2,1)S(1)} %get-tuple-element.17.edge_ref, ...), custom_call_target="tpu_custom_call" | custom-call | flops 268435456 | bytes 4194304 | tf_op jit(solution)/shard_map/pallas_call | solution.py:321
  59.3 23.4 %all_to_all.15.mix_ref = bf16[16,8,512]{2,1,0:T(8,128)(2,1)S(1)} all-to-all(bf16[16,8,512]{2,1,0:T(8,128)(2,1)S(1)} %get-tuple-element.19), channel_id=1, replica_groups=mesh['seq'=32,'tp'=16] {'tp'}, dimensions={0} | all-to-all | bytes 262144 | tf_op jit(solution)/shard_map/all_to_all | solution.py:391
  82.8 0.0 copy-done.1
  82.8 0.0 copy-done.2
  82.8 0.0 copy-done.3
  82.8 2.6 %shard_map.103 = (f32[128,512]{1,0:T(8,128)S(1)}, f32[128,32]{1,0:T(8,128)S(1)}, bf16[32,72,128]{2,1,0:T(8,128)(2,1)}) custom-call(bf16[16,8,512]{2,1,0:T(8,128)(2,1)S(1)} %all_to_all.15.mix_ref, bf16[256,512]{1,0:T(8,128)(2,1)S(1)} %copy-done.1, f32[1,512]{1,0:T(1,128)S(1)} %bitcast.8, f32[16,512]{1,0:T(8,128)S(1)} %copy-done.2, ...), custom_call_target="tpu_custom_call" | custom-call | flops 67108864 | bytes 1048576 | tf_op jit(solution)/shard_map/pallas_call | solution.py:321
  85.4 10.5 %all-to-all-start.2 = ((bf16[32,72,128]{2,1,0:T(8,128)(2,1)}), bf16[32,72,128]{2,1,0:T(8,128)(2,1)S(1)}, u32[]{:S(2)}, u32[]{:S(2)}) async-start(bf16[32,72,128]{2,1,0:T(8,128)(2,1)} %get-tuple-element.22), calls=%async_computation.2 | async-start | bytes 1179648 | tf_op jit(solution)/shard_map/all_to_all | solution.py:410
  95.9 0.0 copy-done.5
  95.9 3.8 %shard_map.104 = (f32[128,512]{1,0:T(8,128)S(1)}, bf16[8,16,16,512]{3,2,1,0:T(8,128)(2,1)S(1)}) custom-call(f32[128,32]{1,0:T(8,128)S(1)} %get-tuple-element.23.coef_ref, f32[16,512]{1,0:T(8,128)S(1)} %copy-done.2, bf16[128,512]{1,0:T(8,128)(2,1)S(1)} %get-tuple-element.20.u_ref, bf16[8,512]{1,0:T(8,128)(2,1)S(1)} %get-tuple-element.21.late_u_ref, ...), custom_call_target="tpu_custom_call" | custom-call | flops 268435456 | bytes 4194304 | tf_op jit(solution)/shard_map/pallas_call | solution.py:321
  99.7 8.4 %all-to-all-done.2.all_ref = bf16[32,72,128]{2,1,0:T(8,128)(2,1)S(1)} async-done(((bf16[32,72,128]{2,1,0:T(8,128)(2,1)}), bf16[32,72,128]{2,1,0:T(8,128)(2,1)S(1)}, u32[]{:S(2)}, u32[]{:S(2)}) %all-to-all-start.2) | async-done | bytes 589856 | tf_op jit(solution)/shard_map/all_to_all | solution.py:410
  108.1 0.0 copy-done.4
  108.1 1.6 %shard_map.105 = bf16[128,512]{1,0:T(8,128)(2,1)} custom-call(s32[1]{0:T(128)} %bitcast.mine_ref, bf16[32,72,128]{2,1,0:T(8,128)(2,1)S(1)} %all-to-all-done.2.all_ref, f32[16,512]{1,0:T(8,128)S(1)} %copy-done.2, f32[128,512]{1,0:T(8,128)S(1)} %get-tuple-element.25.y_ref, bf16[8,16,16,512]{3,2,1,0:T(8,128)(2,1)S(1)} %get-tuple-element.26.grow_ref, ...), custom_call_target="tpu_custom_call" | custom-call | flops 67108864 | bytes 1048576 | tf_op jit(solution)/shard_map/pallas_call | solution.py:321
  (1 shorter events, 0.0 us)
Async XLA Ops:
  0.0 36.6 %copy-start = (bf16[4096,512]{1,0:T(8,128)(2,1)S(1)}, bf16[4096,512]{1,0:T(8,128)(2,1)}, u32[]{:S(2)}) copy-start(bf16[4096,512]{1,0:T(8,128)(2,1)} %weight_hbm.1) | copy-start | bytes 12582916
  38.7 18.3 %all-to-all-start = ((bf16[16,8,384]{2,1,0:T(8,128)(2,1)}), bf16[16,8,384]{2,1,0:T(8,128)(2,1)S(1)}, u32[]{:S(2)}, u32[]{:S(2)}) async-start(bf16[16,8,384]{2,1,0:T(8,128)(2,1)} %get-tuple-element.16), calls=%async_computation | async-start | bytes 196608 | tf_op jit(solution)/shard_map/all_to_all | solution.py:374
  45.1 11.7 %collective-permute-start = (bf16[8,512]{1,0:T(8,128)(2,1)S(1)}, bf16[8,512]{1,0:T(8,128)(2,1)S(1)}, u32[]{:S(2)}, u32[]{:S(2)}) collective-permute-start(bf16[8,512]{1,0:T(8,128)(2,1)S(1)} %slice.3), channel_id=1, source_target_pairs={{0,16},{16,32},{32,48},{48,64},{64,80},{80,96},{96,112},{112,128},... | collective-permute-start | bytes 24584 | tf_op jit(solution)/shard_map/ppermute | solution.py:373
  57.0 25.8 %copy-start.1 = (bf16[256,512]{1,0:T(8,128)(2,1)S(1)}, bf16[256,512]{1,0:T(8,128)(2,1)}, u32[]{:S(2)}) copy-start(bf16[256,512]{1,0:T(8,128)(2,1)} %dtw_ref.1) | copy-start | bytes 786436
  57.0 25.8 %copy-start.2 = (f32[16,512]{1,0:T(8,128)S(1)}, f32[16,512]{1,0:T(8,128)}, u32[]{:S(2)}) copy-start(f32[16,512]{1,0:T(8,128)} %alog_ref.5) | copy-start | bytes 98308
  57.0 25.8 %copy-start.3 = (f32[512]{0:T(512)S(1)}, f32[512]{0:T(512)}, u32[]{:S(2)}) copy-start(f32[512]{0:T(512)} %param.16) | copy-start | bytes 6148
  57.0 38.9 %copy-start.5 = (f32[512]{0:T(512)S(1)}, f32[512]{0:T(512)}, u32[]{:S(2)}) copy-start(f32[512]{0:T(512)} %param.18) | copy-start | bytes 6148
  57.0 51.1 %copy-start.4 = (f32[512]{0:T(512)S(1)}, f32[512]{0:T(512)}, u32[]{:S(2)}) copy-start(f32[512]{0:T(512)} %param.19) | copy-start | bytes 6148
  85.4 22.7 %all-to-all-start.2 = ((bf16[32,72,128]{2,1,0:T(8,128)(2,1)}), bf16[32,72,128]{2,1,0:T(8,128)(2,1)S(1)}, u32[]{:S(2)}, u32[]{:S(2)}) async-start(bf16[32,72,128]{2,1,0:T(8,128)(2,1)} %get-tuple-element.22), calls=%async_computation.2 | async-start | bytes 1179648 | tf_op jit(solution)/shard_map/all_to_all | solution.py:410

commit v7 on v5

--- a/solution.py
+++ b/solution.py
@@ -160,12 +160,9 @@
         mix_ref[z] = pay
 
 
-def split3(x):
+def split2(x):
     a = x.astype(BF16)
-    r = x - a.astype(F32)
-    b = r.astype(BF16)
-    c = (r - b.astype(F32)).astype(BF16)
-    return a, b, c
+    return a, (x - a.astype(F32)).astype(BF16)
 
 
 def running_sum(x):
@@ -173,13 +170,13 @@
     row_ids = lax.broadcasted_iota(jnp.int32, (rows, rows), 0)
     col_ids = lax.broadcasted_iota(jnp.int32, (rows, rows), 1)
     lower = (row_ids >= col_ids).astype(F32).astype(BF16)
-    return sum(jnp.dot(lower, p, preferred_element_type=F32) for p in split3(x)[::-1])
+    return sum(jnp.dot(lower, p, preferred_element_type=F32) for p in split2(x)[::-1])
 
 
 def state_kernel(
     mix_ref, dtw_ref, dtb_ref, alog_ref, u_ref, late_u_ref,
     step_ref, coef_ref, pay_ref,
-    uf_ref, flow_ref, left_ref, bx_ref, end_ref, low_ref,
+    uf_ref, flow_ref, left_ref, bx_ref, rate_ref, low_ref, pack_ref,
 ):
     shards, each, _ = mix_ref.shape
     rows, width = u_ref.shape
@@ -197,36 +194,46 @@
     early = jnp.concatenate([pairs[:late], pairs[late:]], axis=1)
     low_ref[:late, :] = early[:, :rank]
     coef_ref[:late, :] = early[:, rank:]
-    v = jnp.dot(low_ref[...].astype(BF16), dtw_ref[...], preferred_element_type=F32) + dtb_ref[...]
-    step = jnp.maximum(v, 0.0) + jnp.log1p(jnp.exp(-jnp.abs(v)))
-    step_ref[...] = step
-    cum = running_sum(step)
-    whole = cum[rows - 1 : rows, :]
-    left_ref[...] = (whole - cum).reshape(tiles, 8, width)
+    low = low_ref[...].astype(BF16)
+    rate_ref[...] = -jnp.exp(alog_ref[...]) * LOG2E
     uf_ref[...] = u_ref[...].astype(F32)
     uf_ref[:8, :] = late_u_ref[...].astype(F32)
-    flow_ref[...] = (step * uf_ref[...]).reshape(tiles, 8, width)
     b = coef_ref[:, :n]
     for i in range(n):
         bx_ref[:, i] = jnp.broadcast_to(b[:, i : i + 1], (rows, 128)).reshape(tiles, 8, 128)
-    rate2 = -jnp.exp(alog_ref[...]) * LOG2E
     groups = width // 128
-    for g in range(groups):
-        lanes = slice(g * 128, (g + 1) * 128)
-        rate_g = jnp.broadcast_to(rate2[:, None, lanes], (n, 8, 128))
-
-        def turn(i, acc):
-            grow = jnp.exp2(rate_g * left_ref[i, :, lanes][None])
-            return acc + grow * (flow_ref[i, :, lanes][None] * bx_ref[i])
-
-        acc = lax.fori_loop(0, tiles, turn, jnp.zeros((n, 8, 128), F32), unroll=2)
-        hi, lo, _ = split3(whole[:, lanes])
-        end_ref[g * n : (g + 1) * n, :] = jnp.sum(acc, axis=1)
-        end_ref[groups * n + g : groups * n + g + 1, :] = hi.astype(F32)
-        end_ref[groups * n + groups + g : groups * n + groups + g + 1, :] = lo.astype(F32)
-    end = end_ref[...].astype(BF16)
+    span = 128
+    for h in range(width // span):
+        cols = slice(h * span, (h + 1) * span)
+        v = jnp.dot(low, dtw_ref[:, cols], preferred_element_type=F32) + dtb_ref[:, cols]
+        step = jnp.maximum(v, 0.0) + jnp.log1p(jnp.exp(-jnp.abs(v)))
+        step_ref[:, cols] = step
+        cum = running_sum(step)
+        whole = cum[rows - 1 : rows, :]
+        left_ref[:, :, cols] = (whole - cum).reshape(tiles, 8, span)
+        flow_ref[:, :, cols] = (step * uf_ref[:, cols]).reshape(tiles, 8, span)
+        for k in range(span // 128):
+            g = h * (span // 128) + k
+            lanes = slice(g * 128, (g + 1) * 128)
+            hi, lo = split2(whole[:, k * 128 : (k + 1) * 128])
+            ends = []
+            for first in range(0, n, 8):
+                rates = [jnp.broadcast_to(rate_ref[i : i + 1, lanes], (8, 128)) for i in range(first, first + 8)]
+                accs = [None] * 8
+                for t in range(tiles):
+                    left = left_ref[t, :, lanes]
+                    flow = flow_ref[t, :, lanes]
+                    for i in range(8):
+                        term = jnp.exp2(rates[i] * left) * (flow * bx_ref[t, first + i])
+                        accs[i] = term if t == 0 else accs[i] + term
+                ends += [jnp.sum(acc, axis=0, keepdims=True) for acc in accs]
+            pack_ref[g * n : (g + 1) * n, :] = jnp.concatenate(ends, axis=0).astype(BF16)
+            low_ref[g : g + 1, :128] = hi.astype(F32)
+            low_ref[groups + g : groups + g + 1, :128] = lo.astype(F32)
+    pack_ref[groups * n :, :] = low_ref[: 2 * groups, :128].astype(BF16)
+    pack = pack_ref[...]
     for p in range(pay_ref.shape[0]):
-        pay_ref[p] = end
+        pay_ref[p] = pack
 
 
 def local_kernel(
@@ -305,20 +312,19 @@
         def turn(i, _):
             at = pl.ds(pl.multiple_of(i * 16, 16), 16)
             y = y_ref[at, lanes] + jnp.sum(grow_ref[i, :, :, lanes].astype(F32) * entry_g, axis=0)
-            y_ref[at, lanes] = y / (1.0 + jnp.exp(-4.0 * (y - thr)))
+            out_ref[at, lanes] = (y / (1.0 + jnp.exp(-4.0 * (y - thr)))).astype(BF16)
             return 0
 
-        lax.fori_loop(0, blocks, turn, 0)
-    out_ref[...] = y_ref[...].astype(BF16)
-
-
-def call(kernel, outs, ins, scratch=(), flops=0, specs=None, vmem=12 << 20):
+        lax.fori_loop(0, blocks, turn, 0, unroll=blocks)
+
+
+def call(kernel, outs, ins, scratch=(), flops=0, specs=None, vmem=12 << 20, outs_in=None):
     specs = specs or [VMEM] * len(ins)
     return pl.pallas_call(
         kernel,
         out_shape=outs,
         in_specs=specs,
-        out_specs=jax.tree.map(lambda _: VMEM, outs),
+        out_specs=outs_in or jax.tree.map(lambda _: VMEM, outs),
         scratch_shapes=scratch,
         cost_estimate=pl.CostEstimate(flops=flops, bytes_accessed=flops // 64, transcendentals=0),
         compiler_params=pltpu.CompilerParams(vmem_limit_bytes=vmem),
@@ -395,8 +401,9 @@
             pltpu.VMEM((rows // 8, 8, width), F32),
             pltpu.VMEM((rows // 8, 8, width), F32),
             pltpu.VMEM((rows // 8, n, 8, 128), F32),
-            pltpu.VMEM(((n + 2) * width // 128, 128), F32),
+            pltpu.VMEM((n, width), F32),
             pltpu.VMEM((rows, rank), F32),
+            pltpu.VMEM(((n + 2) * width // 128, 128), BF16),
         ),
         flops=1 << 26,
     )

time: 111 us -> 110 us (level)
  Pallas kernels: 14.2 us -> 13 us
    pallas_call x6, Pallas kernels: 14.2 us -> 13 us  [call(): pl.pallas_call(kernel, out_shape=outs, in_specs=specs, out_specs=outs_in...]
where the time goes in v7:
time: 110 us; the launch traced here: 109 us
  blocking collectives  59 us (54%)
  starting transfers between devices  27.8 us (25%)
  Pallas kernels  13 us (12%)
  waiting for transfers between devices  9.31 us (8%)
    all_gather x1, blocking collectives, per_device(): main = lax.all_gather(most, 'tp')  35.6 us
    all_to_all x1, blocking collectives, per_device(): mix = lax.all_to_all(mix, 'tp', 0, 0)  23.4 us
    pallas_call x6, Pallas kernels, call(): pl.pallas_call(kernel, out_shape=outs, in_specs=specs, out_specs=outs_in...  13 us
    ppermute x1, starting transfers between devices, per_device(): rim = lax.ppermute(edge[:8], 'seq', [(i, i + 1) for i in range(peers - 1)])  10.9 us
    all_to_all x1, starting transfers between devices, per_device(): everyone = lax.all_to_all(pay, 'seq', 0, 0)  10.5 us
    all_to_all x1, waiting for transfers between devices, per_device(): everyone = lax.all_to_all(pay, 'seq', 0, 0)  8.42 us
    all_to_all x1, starting transfers between devices, per_device(): got = lax.all_to_all(send, 'tp', 0, 0)  6.41 us
  transfers between devices with their start and end apart: 3, of which 3 were waited for; matrix products, arithmetic and copies ran while one was open for 0% of the time, Pallas kernels for 3%

profile of v7, /device:TPU:1, one launch (start us, length us, event | category | flops | bytes accessed | tf_op | source)
XLA Modules:
  0.0 109.3 jit_solution(982697442941745214)
XLA Ops:
  0.0 0.0 copy-start
  0.0 1.0 shard_map.100
  1.0 35.6 %all-gather.1.main_ref = bf16[16,127,256]{2,1,0:T(8,128)(2,1)S(1)} all-gather(bf16[1,127,256]{2,1,0:T(8,128)(2,1)S(1)} %bitcast.7), channel_id=2, replica_groups=mesh['seq'=32,'tp'=16] {'tp'}, dimensions={0}, use_global_device_ids=true | all-gather | bytes 1105408 | tf_op jit(solution)/shard_map/all_gather | solution.py:363
  36.6 0.0 copy-done
  36.6 2.1 %shard_map.101 = (bf16[16,8,384]{2,1,0:T(8,128)(2,1)}, bf16[16,512]{1,0:T(8,128)(2,1)S(1)}, bf16[128,512]{1,0:T(8,128)(2,1)S(1)}, bf16[3072,512]{1,0:T(8,128)(2,1)S(1)}) custom-call(bf16[16,127,256]{2,1,0:T(8,128)(2,1)S(1)} %all-gather.1.main_ref, bf16[4096,512]{1,0:T(8,128)(2,1)S(1)} %copy-done, bf16[128,256]{1,0:T(8,128)(2,1)} %tokens_hbm.3, ...), custom_call_target="tpu_custom_call" | custom-call | flops 536870912 | bytes 8388608 | tf_op jit(solution)/shard_map/pallas_call | solution.py:323
  38.7 6.4 %all-to-all-start = ((bf16[16,8,384]{2,1,0:T(8,128)(2,1)}), bf16[16,8,384]{2,1,0:T(8,128)(2,1)S(1)}, u32[]{:S(2)}, u32[]{:S(2)}) async-start(bf16[16,8,384]{2,1,0:T(8,128)(2,1)} %get-tuple-element.16), calls=%async_computation | async-start | bytes 196608 | tf_op jit(solution)/shard_map/all_to_all | solution.py:376
  45.1 10.9 %collective-permute-start = (bf16[8,512]{1,0:T(8,128)(2,1)S(1)}, bf16[8,512]{1,0:T(8,128)(2,1)S(1)}, u32[]{:S(2)}, u32[]{:S(2)}) collective-permute-start(bf16[8,512]{1,0:T(8,128)(2,1)S(1)} %slice.3), channel_id=1, source_target_pairs={{0,16},{16,32},{32,48},{48,64},{64,80},{80,96},{96,112},{112,128},... | collective-permute-start | bytes 24584 | tf_op jit(solution)/shard_map/ppermute | solution.py:375
  56.1 0.8 collective-permute-done.rim_ref
  56.9 0.1 all-to-all-done.got_ref
  57.0 0.0 copy-start.1
  57.0 0.0 copy-start.2
  57.0 0.0 copy-start.3
  57.0 0.0 copy-start.5
  57.0 0.0 copy-start.4
  57.0 2.3 %shard_map.102 = (bf16[16,8,512]{2,1,0:T(8,128)(2,1)S(1)}, bf16[8,512]{1,0:T(8,128)(2,1)S(1)}) custom-call(bf16[16,8,384]{2,1,0:T(8,128)(2,1)S(1)} %all-to-all-done.got_ref, bf16[8,512]{1,0:T(8,128)(2,1)S(1)} %collective-permute-done.rim_ref, bf16[16,512]{1,0:T(8,128)(2,1)S(1)} %get-tuple-element.17.edge_ref, ...), custom_call_target="tpu_custom_call" | custom-call | flops 268435456 | bytes 4194304 | tf_op jit(solution)/shard_map/pallas_call | solution.py:323
  59.3 23.4 %all_to_all.15.mix_ref = bf16[16,8,512]{2,1,0:T(8,128)(2,1)S(1)} all-to-all(bf16[16,8,512]{2,1,0:T(8,128)(2,1)S(1)} %get-tuple-element.19), channel_id=1, replica_groups=mesh['seq'=32,'tp'=16] {'tp'}, dimensions={0} | all-to-all | bytes 262144 | tf_op jit(solution)/shard_map/all_to_all | solution.py:393
  82.8 0.0 copy-done.1
  82.8 0.0 copy-done.2
  82.8 0.0 copy-done.3
  82.8 2.2 %shard_map.103 = (f32[128,512]{1,0:T(8,128)S(1)}, f32[128,32]{1,0:T(8,128)S(1)}, bf16[32,72,128]{2,1,0:T(8,128)(2,1)}) custom-call(bf16[16,8,512]{2,1,0:T(8,128)(2,1)S(1)} %all_to_all.15.mix_ref, bf16[256,512]{1,0:T(8,128)(2,1)S(1)} %copy-done.1, f32[1,512]{1,0:T(1,128)S(1)} %bitcast.8, f32[16,512]{1,0:T(8,128)S(1)} %copy-done.2, ...), custom_call_target="tpu_custom_call" | custom-call | flops 67108864 | bytes 1048576 | tf_op jit(solution)/shard_map/pallas_call | solution.py:323
  85.0 10.5 %all-to-all-start.2 = ((bf16[32,72,128]{2,1,0:T(8,128)(2,1)}), bf16[32,72,128]{2,1,0:T(8,128)(2,1)S(1)}, u32[]{:S(2)}, u32[]{:S(2)}) async-start(bf16[32,72,128]{2,1,0:T(8,128)(2,1)} %get-tuple-element.22), calls=%async_computation.2 | async-start | bytes 1179648 | tf_op jit(solution)/shard_map/all_to_all | solution.py:410
  95.5 0.0 copy-done.5
  95.5 3.8 %shard_map.104 = (f32[128,512]{1,0:T(8,128)S(1)}, bf16[8,16,16,512]{3,2,1,0:T(8,128)(2,1)S(1)}) custom-call(f32[128,32]{1,0:T(8,128)S(1)} %get-tuple-element.23.coef_ref, f32[16,512]{1,0:T(8,128)S(1)} %copy-done.2, bf16[128,512]{1,0:T(8,128)(2,1)S(1)} %get-tuple-element.20.u_ref, bf16[8,512]{1,0:T(8,128)(2,1)S(1)} %get-tuple-element.21.late_u_ref, ...), custom_call_target="tpu_custom_call" | custom-call | flops 268435456 | bytes 4194304 | tf_op jit(solution)/shard_map/pallas_call | solution.py:323
  99.3 8.4 %all-to-all-done.2.all_ref = bf16[32,72,128]{2,1,0:T(8,128)(2,1)S(1)} async-done(((bf16[32,72,128]{2,1,0:T(8,128)(2,1)}), bf16[32,72,128]{2,1,0:T(8,128)(2,1)S(1)}, u32[]{:S(2)}, u32[]{:S(2)}) %all-to-all-start.2) | async-done | bytes 589856 | tf_op jit(solution)/shard_map/all_to_all | solution.py:410
  107.7 0.0 copy-done.4
  107.7 1.6 %shard_map.105 = bf16[128,512]{1,0:T(8,128)(2,1)} custom-call(s32[1]{0:T(128)} %bitcast.mine_ref, bf16[32,72,128]{2,1,0:T(8,128)(2,1)S(1)} %all-to-all-done.2.all_ref, f32[16,512]{1,0:T(8,128)S(1)} %copy-done.2, f32[128,512]{1,0:T(8,128)S(1)} %get-tuple-element.25.y_ref, bf16[8,16,16,512]{3,2,1,0:T(8,128)(2,1)S(1)} %get-tuple-element.26.grow_ref, ...), custom_call_target="tpu_custom_call" | custom-call | flops 67108864 | bytes 1048576 | tf_op jit(solution)/shard_map/pallas_call | solution.py:323
  (1 shorter events, 0.0 us)
Async XLA Ops:
  0.0 36.6 %copy-start = (bf16[4096,512]{1,0:T(8,128)(2,1)S(1)}, bf16[4096,512]{1,0:T(8,128)(2,1)}, u32[]{:S(2)}) copy-start(bf16[4096,512]{1,0:T(8,128)(2,1)} %weight_hbm.1) | copy-start | bytes 12582916
  38.7 18.3 %all-to-all-start = ((bf16[16,8,384]{2,1,0:T(8,128)(2,1)}), bf16[16,8,384]{2,1,0:T(8,128)(2,1)S(1)}, u32[]{:S(2)}, u32[]{:S(2)}) async-start(bf16[16,8,384]{2,1,0:T(8,128)(2,1)} %get-tuple-element.16), calls=%async_computation | async-start | bytes 196608 | tf_op jit(solution)/shard_map/all_to_all | solution.py:376
  45.1 11.7 %collective-permute-start = (bf16[8,512]{1,0:T(8,128)(2,1)S(1)}, bf16[8,512]{1,0:T(8,128)(2,1)S(1)}, u32[]{:S(2)}, u32[]{:S(2)}) collective-permute-start(bf16[8,512]{1,0:T(8,128)(2,1)S(1)} %slice.3), channel_id=1, source_target_pairs={{0,16},{16,32},{32,48},{48,64},{64,80},{80,96},{96,112},{112,128},... | collective-permute-start | bytes 24584 | tf_op jit(solution)/shard_map/ppermute | solution.py:375
  57.0 25.8 %copy-start.1 = (bf16[256,512]{1,0:T(8,128)(2,1)S(1)}, bf16[256,512]{1,0:T(8,128)(2,1)}, u32[]{:S(2)}) copy-start(bf16[256,512]{1,0:T(8,128)(2,1)} %dtw_ref.1) | copy-start | bytes 786436
  57.0 25.8 %copy-start.2 = (f32[16,512]{1,0:T(8,128)S(1)}, f32[16,512]{1,0:T(8,128)}, u32[]{:S(2)}) copy-start(f32[16,512]{1,0:T(8,128)} %alog_ref.5) | copy-start | bytes 98308
  57.0 25.8 %copy-start.3 = (f32[512]{0:T(512)S(1)}, f32[512]{0:T(512)}, u32[]{:S(2)}) copy-start(f32[512]{0:T(512)} %param.16) | copy-start | bytes 6148
  57.0 38.5 %copy-start.5 = (f32[512]{0:T(512)S(1)}, f32[512]{0:T(512)}, u32[]{:S(2)}) copy-start(f32[512]{0:T(512)} %param.18) | copy-start | bytes 6148
  57.0 50.8 %copy-start.4 = (f32[512]{0:T(512)S(1)}, f32[512]{0:T(512)}, u32[]{:S(2)}) copy-start(f32[512]{0:T(512)} %param.19) | copy-start | bytes 6148
  85.0 22.7 %all-to-all-start.2 = ((bf16[32,72,128]{2,1,0:T(8,128)(2,1)}), bf16[32,72,128]{2,1,0:T(8,128)(2,1)S(1)}, u32[]{:S(2)}, u32[]{:S(2)}) async-start(bf16[32,72,128]{2,1,0:T(8,128)(2,1)} %get-tuple-element.22), calls=%async_computation.2 | async-start | bytes 1179648 | tf_op jit(solution)/shard_map/all_to_all | solution.py:410

commit v8 on v7

--- a/solution.py
+++ b/solution.py
@@ -175,8 +175,8 @@
 
 def state_kernel(
     mix_ref, dtw_ref, dtb_ref, alog_ref, u_ref, late_u_ref,
-    step_ref, coef_ref, pay_ref,
-    uf_ref, flow_ref, left_ref, bx_ref, rate_ref, low_ref, pack_ref,
+    step_ref, coef_ref, pack_ref,
+    uf_ref, flow_ref, left_ref, bx_ref, rate_ref, low_ref,
 ):
     shards, each, _ = mix_ref.shape
     rows, width = u_ref.shape
@@ -231,7 +231,40 @@
             low_ref[g : g + 1, :128] = hi.astype(F32)
             low_ref[groups + g : groups + g + 1, :128] = lo.astype(F32)
     pack_ref[groups * n :, :] = low_ref[: 2 * groups, :128].astype(BF16)
-    pack = pack_ref[...]
+
+
+def merge_kernel(mine_ref, own_ref, other_ref, alog_ref, pay_ref, pack_ref):
+    n, width = alog_ref.shape
+    groups = width // 128
+    near = groups // 2
+    second_core = lax.rem(mine_ref[0], 2) == 1
+    own = own_ref[...].astype(F32)
+    other = other_ref[...].astype(F32)
+    early = jnp.where(second_core, other, own)
+    later = jnp.where(second_core, own, other)
+    rate2 = -jnp.exp(alog_ref[...]) * LOG2E
+
+    def rows(block, g, first, size):
+        low = block[first + g * size : first + (g + 1) * size, :]
+        high = block[first + (near + g) * size : first + (near + g + 1) * size, :]
+        return jnp.where(second_core, high, low)
+
+    for g in range(near):
+        at = groups * n
+        sum_early = rows(early, g, at, 1) + rows(early, g, at + groups, 1)
+        sum_later = rows(later, g, at, 1) + rows(later, g, at + groups, 1)
+        rate_g = jnp.where(
+            second_core,
+            rate2[:, (near + g) * 128 : (near + g + 1) * 128],
+            rate2[:, g * 128 : (g + 1) * 128],
+        )
+        pack_ref[g * n : (g + 1) * n, :] = (
+            jnp.exp2(rate_g * sum_later) * rows(early, g, 0, n) + rows(later, g, 0, n)
+        )
+        hi, lo = split2(sum_early + sum_later)
+        pack_ref[near * n + g : near * n + g + 1, :] = hi.astype(F32)
+        pack_ref[near * n + near + g : near * n + near + g + 1, :] = lo.astype(F32)
+    pack = pack_ref[...].astype(BF16)
     for p in range(pay_ref.shape[0]):
         pay_ref[p] = pack
 
@@ -283,29 +316,32 @@
         lax.fori_loop(0, blocks, fill, 0)
 
 
-def final_kernel(mine_ref, all_ref, alog_ref, y_ref, grow_ref, thr_ref, out_ref):
+def final_kernel(mine_ref, all_ref, other_ref, alog_ref, y_ref, grow_ref, thr_ref, out_ref):
     rows, width = y_ref.shape
     n = alog_ref.shape[0]
     blocks = rows // 16
-    peers = all_ref.shape[0]
+    chips = all_ref.shape[0] // 2
     mine = mine_ref[0]
+    second_core = lax.rem(mine, 2) == 1
     rate2 = -jnp.exp(alog_ref[...]) * LOG2E
-
     groups = width // 128
+    near = groups // 2
+    other = other_ref[...].astype(F32)
     for g in range(groups):
         lanes = slice(g * 128, (g + 1) * 128)
         rate_g = rate2[:, lanes]
-
-        def join(p, state):
-            block = all_ref[p].astype(F32)
-            at = groups * n + g
-            whole = block[at : at + 1, :] + block[at + groups : at + groups + 1, :]
-            longer = jnp.exp2(rate_g * whole) * state + block[g * n : (g + 1) * n, :]
-            return jnp.where(p < mine, longer, state)
-
+        half, place = g // near, g % near
         entry = jnp.zeros((n, 128), F32)
-        for p in range(peers - 1):
-            entry = join(p, entry)
+        for p in range(chips - 1):
+            block = all_ref[2 * p + half].astype(F32)
+            at = near * n + place
+            whole = block[at : at + 1, :] + block[at + near : at + near + 1, :]
+            longer = jnp.exp2(rate_g * whole) * entry + block[place * n : (place + 1) * n, :]
+            entry = jnp.where(2 * p + 1 < mine, longer, entry)
+        at = groups * n + g
+        whole = other[at : at + 1, :] + other[at + groups : at + groups + 1, :]
+        longer = jnp.exp2(rate_g * whole) * entry + other[g * n : (g + 1) * n, :]
+        entry = jnp.where(second_core, longer, entry)
         entry_g = jnp.broadcast_to(entry[:, None, :], (n, 16, 128))
         thr = thr_ref[:, lanes]
 
@@ -392,9 +428,9 @@
     )
     mix = lax.all_to_all(mix, "tp", 0, 0)
     whole = struct((rows, width), F32)
-    step, coef, pay = call(
+    step, coef, own = call(
         state_kernel,
-        (whole, struct((rows, 2 * n), F32), struct((peers, (n + 2) * width // 128, 128), BF16)),
+        (whole, struct((rows, 2 * n), F32), struct(((n + 2) * width // 128, 128), BF16)),
         (mix, dt_weight, dt_bias[None], a_log, u, late_u),
         (
             pltpu.VMEM((rows, width), F32),
@@ -403,10 +439,21 @@
             pltpu.VMEM((rows // 8, n, 8, 128), F32),
             pltpu.VMEM((n, width), F32),
             pltpu.VMEM((rows, rank), F32),
-            pltpu.VMEM(((n + 2) * width // 128, 128), BF16),
         ),
         flops=1 << 26,
     )
+    mine = lax.axis_index("seq").astype(jnp.int32)[None]
+    other = lax.ppermute(own, "seq", [(i, i ^ 1) for i in range(peers)])
+    half = (n + 2) * width // 256
+    pay = call(
+        merge_kernel,
+        struct((peers, half, 128), BF16),
+        (mine, own, other, a_log),
+        (pltpu.VMEM((half, 128), F32),),
+        flops=1 << 20,
+        specs=[SMEM] + [VMEM] * 3,
+    )
+    pay, coef = lax.optimization_barrier((pay, coef))
     everyone = lax.all_to_all(pay, "seq", 0, 0)
     y_local, grow = call(
         local_kernel,
@@ -422,13 +469,12 @@
         ),
         flops=1 << 28,
     )
-    mine = lax.axis_index("seq").astype(jnp.int32)[None]
     return call(
         final_kernel,
         struct((rows, width), BF16),
-        (mine, everyone, a_log, y_local, grow, threshold[None]),
+        (mine, everyone, other, a_log, y_local, grow, threshold[None]),
         flops=1 << 26,
-        specs=[SMEM] + [VMEM] * 5,
+        specs=[SMEM] + [VMEM] * 6,
     )
 
 

time: 110 us -> 110 us (level)
  starting transfers between devices: 27.8 us -> 30.1 us
  waiting for transfers between devices: 9.31 us -> 7.38 us
    ppermute x0 -> x1, starting transfers between devices: none -> 5.6 us  [per_device(): other = lax.ppermute(own, 'seq', [(i, i ^ 1) for i in range(peers)])]
    all_to_all x1, starting transfers between devices: 10.5 us -> 7.13 us  [per_device(): everyone = lax.all_to_all(pay, 'seq', 0, 0)]
    all_to_all x1, waiting for transfers between devices: 8.42 us -> 5.68 us  [per_device(): everyone = lax.all_to_all(pay, 'seq', 0, 0)]
    pallas_call x6 -> x7, Pallas kernels: 13 us -> 12.8 us  [call(): pl.pallas_call(kernel, out_shape=outs, in_specs=specs, out_specs=outs_in...]
  transfers between devices with their start and end apart: 3 -> 4, of which waited for: 3 -> 4; matrix products, arithmetic and copies ran while one was open for 0% -> 0% of each run, Pallas kernels for 3% -> 4%
where the time goes in v8:
time: 110 us; the launch traced here: 109 us
  blocking collectives  59 us (54%)
  starting transfers between devices  30.1 us (27%)
  Pallas kernels  12.8 us (12%)
  waiting for transfers between devices  7.38 us (7%)
    all_gather x1, blocking collectives, per_device(): main = lax.all_gather(most, 'tp')  35.6 us
    all_to_all x1, blocking collectives, per_device(): mix = lax.all_to_all(mix, 'tp', 0, 0)  23.4 us
    pallas_call x7, Pallas kernels, call(): pl.pallas_call(kernel, out_shape=outs, in_specs=specs, out_specs=outs_in...  12.8 us
    ppermute x1, starting transfers between devices, per_device(): rim = lax.ppermute(edge[:8], 'seq', [(i, i + 1) for i in range(peers - 1)])  10.9 us
    all_to_all x1, starting transfers between devices, per_device(): everyone = lax.all_to_all(pay, 'seq', 0, 0)  7.13 us
    all_to_all x1, starting transfers between devices, per_device(): got = lax.all_to_all(send, 'tp', 0, 0)  6.41 us
    all_to_all x1, waiting for transfers between devices, per_device(): everyone = lax.all_to_all(pay, 'seq', 0, 0)  5.68 us
    ppermute x1, starting transfers between devices, per_device(): other = lax.ppermute(own, 'seq', [(i, i ^ 1) for i in range(peers)])  5.6 us
  transfers between devices with their start and end apart: 4, of which 4 were waited for; matrix products, arithmetic and copies ran while one was open for 0% of the time, Pallas kernels for 4%

profile of v8, /device:TPU:1, one launch (start us, length us, event | category | flops | bytes accessed | tf_op | source)
XLA Modules:
  0.0 109.4 jit_solution(3119275063438223096)
XLA Ops:
  0.0 0.0 copy-start
  0.0 1.0 shard_map.100
  1.0 35.6 %all-gather.1.main_ref = bf16[16,127,256]{2,1,0:T(8,128)(2,1)S(1)} all-gather(bf16[1,127,256]{2,1,0:T(8,128)(2,1)S(1)} %bitcast.7), channel_id=2, replica_groups=mesh['seq'=32,'tp'=16] {'tp'}, dimensions={0}, use_global_device_ids=true | all-gather | bytes 1105408 | tf_op jit(solution)/shard_map/all_gather | solution.py:399
  36.6 0.0 copy-done
  36.6 2.1 %shard_map.101 = (bf16[16,8,384]{2,1,0:T(8,128)(2,1)}, bf16[16,512]{1,0:T(8,128)(2,1)S(1)}, bf16[128,512]{1,0:T(8,128)(2,1)S(1)}, bf16[3072,512]{1,0:T(8,128)(2,1)S(1)}) custom-call(bf16[16,127,256]{2,1,0:T(8,128)(2,1)S(1)} %all-gather.1.main_ref, bf16[4096,512]{1,0:T(8,128)(2,1)S(1)} %copy-done, bf16[128,256]{1,0:T(8,128)(2,1)} %tokens_hbm.3, ...), custom_call_target="tpu_custom_call" | custom-call | flops 536870912 | bytes 8388608 | tf_op jit(solution)/shard_map/pallas_call | solution.py:359
  38.7 6.4 %all-to-all-start = ((bf16[16,8,384]{2,1,0:T(8,128)(2,1)}), bf16[16,8,384]{2,1,0:T(8,128)(2,1)S(1)}, u32[]{:S(2)}, u32[]{:S(2)}) async-start(bf16[16,8,384]{2,1,0:T(8,128)(2,1)} %get-tuple-element.18), calls=%async_computation | async-start | bytes 196608 | tf_op jit(solution)/shard_map/all_to_all | solution.py:412
  45.1 10.9 %collective-permute-start = (bf16[8,512]{1,0:T(8,128)(2,1)S(1)}, bf16[8,512]{1,0:T(8,128)(2,1)S(1)}, u32[]{:S(2)}, u32[]{:S(2)}) collective-permute-start(bf16[8,512]{1,0:T(8,128)(2,1)S(1)} %slice.3), channel_id=1, source_target_pairs={{0,16},{16,32},{32,48},{48,64},{64,80},{80,96},{96,112},{112,128},... | collective-permute-start | bytes 24584 | tf_op jit(solution)/shard_map/ppermute | solution.py:411
  56.1 0.8 collective-permute-done.rim_ref
  56.9 0.1 all-to-all-done.got_ref
  57.0 0.0 copy-start.1
  57.0 0.0 copy-start.2
  57.0 0.0 copy-start.3
  57.0 0.0 copy-start.5
  57.0 0.0 copy-start.4
  57.0 2.3 %shard_map.102 = (bf16[16,8,512]{2,1,0:T(8,128)(2,1)S(1)}, bf16[8,512]{1,0:T(8,128)(2,1)S(1)}) custom-call(bf16[16,8,384]{2,1,0:T(8,128)(2,1)S(1)} %all-to-all-done.got_ref, bf16[8,512]{1,0:T(8,128)(2,1)S(1)} %collective-permute-done.rim_ref, bf16[16,512]{1,0:T(8,128)(2,1)S(1)} %get-tuple-element.19.edge_ref, ...), custom_call_target="tpu_custom_call" | custom-call | flops 268435456 | bytes 4194304 | tf_op jit(solution)/shard_map/pallas_call | solution.py:359
  59.3 23.4 %all_to_all.15.mix_ref = bf16[16,8,512]{2,1,0:T(8,128)(2,1)S(1)} all-to-all(bf16[16,8,512]{2,1,0:T(8,128)(2,1)S(1)} %get-tuple-element.21), channel_id=1, replica_groups=mesh['seq'=32,'tp'=16] {'tp'}, dimensions={0} | all-to-all | bytes 262144 | tf_op jit(solution)/shard_map/all_to_all | solution.py:429
  82.8 0.0 copy-done.1
  82.8 0.0 copy-done.2
  82.8 0.0 copy-done.3
  82.8 1.3 %shard_map.103 = (f32[128,512]{1,0:T(8,128)S(1)}, f32[128,32]{1,0:T(8,128)S(1)}, bf16[72,128]{1,0:T(8,128)(2,1)S(1)}) custom-call(bf16[16,8,512]{2,1,0:T(8,128)(2,1)S(1)} %all_to_all.15.mix_ref, bf16[256,512]{1,0:T(8,128)(2,1)S(1)} %copy-done.2, f32[1,512]{1,0:T(1,128)S(1)} %bitcast.8, f32[16,512]{1,0:T(8,128)S(1)} %copy-done.1, ...), custom_call_target="tpu_custom_call" | custom-call | flops 67108864 | bytes 1048576 | tf_op jit(solution)/shard_map/pallas_call | solution.py:359
  84.1 5.6 %collective-permute-start.1 = (bf16[72,128]{1,0:T(8,128)(2,1)S(1)}, bf16[72,128]{1,0:T(8,128)(2,1)S(1)}, u32[]{:S(2)}, u32[]{:S(2)}) collective-permute-start(bf16[72,128]{1,0:T(8,128)(2,1)S(1)} %get-tuple-element.24.own_ref), channel_id=1, source_target_pairs={{0,16},{16,0},{32,48},{48,32},{64,80},{80,64},{96,112},{112,96},{1... | collective-permute-start | bytes 55304 | tf_op jit(solution)/shard_map/ppermute | solution.py:446
  89.7 0.8 collective-permute-done.1.other_ref
  90.5 0.8 shard_map.104
  91.3 7.1 %all-to-all-start.2 = ((bf16[32,36,128]{2,1,0:T(8,128)(2,1)}), bf16[32,36,128]{2,1,0:T(8,128)(2,1)S(1)}, u32[]{:S(2)}, u32[]{:S(2)}) async-start(bf16[32,36,128]{2,1,0:T(8,128)(2,1)} %shard_map.104), calls=%async_computation.2 | async-start | bytes 655360 | tf_op jit(solution)/shard_map/all_to_all | solution.py:457
  98.4 0.0 copy-done.5
  98.4 3.8 %shard_map.105 = (f32[128,512]{1,0:T(8,128)S(1)}, bf16[8,16,16,512]{3,2,1,0:T(8,128)(2,1)S(1)}) custom-call(f32[128,32]{1,0:T(8,128)S(1)} %get-tuple-element.27.coef_ref, f32[16,512]{1,0:T(8,128)S(1)} %copy-done.1, bf16[128,512]{1,0:T(8,128)(2,1)S(1)} %get-tuple-element.22.u_ref, bf16[8,512]{1,0:T(8,128)(2,1)S(1)} %get-tuple-element.23.late_u_ref, ...), custom_call_target="tpu_custom_call" | custom-call | flops 268435456 | bytes 4194304 | tf_op jit(solution)/shard_map/pallas_call | solution.py:359
  102.3 5.7 %all-to-all-done.2.all_ref = bf16[32,36,128]{2,1,0:T(8,128)(2,1)S(1)} async-done(((bf16[32,36,128]{2,1,0:T(8,128)(2,1)}), bf16[32,36,128]{2,1,0:T(8,128)(2,1)S(1)}, u32[]{:S(2)}, u32[]{:S(2)}) %all-to-all-start.2) | async-done | bytes 294944 | tf_op jit(solution)/shard_map/all_to_all | solution.py:457
  108.0 0.0 copy-done.4
  108.0 1.4 %shard_map.106 = bf16[128,512]{1,0:T(8,128)(2,1)} custom-call(s32[1]{0:T(128)} %bitcast.mine_ref, bf16[32,36,128]{2,1,0:T(8,128)(2,1)S(1)} %all-to-all-done.2.all_ref, bf16[72,128]{1,0:T(8,128)(2,1)S(1)} %collective-permute-done.1.other_ref, f32[16,512]{1,0:T(8,128)S(1)} %copy-done.1, f32[128,512]{1,0:T(8,128)S(1)} %get-tuple-element.29.y_ref, ...), custom_call_target="tpu_custom_call" | custom-call | flops 67108864 | bytes 1048576 | tf_op jit(solution)/shard_map/pallas_call | solution.py:359
  (1 shorter events, 0.0 us)
Async XLA Ops:
  0.0 36.6 %copy-start = (bf16[4096,512]{1,0:T(8,128)(2,1)S(1)}, bf16[4096,512]{1,0:T(8,128)(2,1)}, u32[]{:S(2)}) copy-start(bf16[4096,512]{1,0:T(8,128)(2,1)} %weight_hbm.1) | copy-start | bytes 12582916
  38.7 18.3 %all-to-all-start = ((bf16[16,8,384]{2,1,0:T(8,128)(2,1)}), bf16[16,8,384]{2,1,0:T(8,128)(2,1)S(1)}, u32[]{:S(2)}, u32[]{:S(2)}) async-start(bf16[16,8,384]{2,1,0:T(8,128)(2,1)} %get-tuple-element.18), calls=%async_computation | async-start | bytes 196608 | tf_op jit(solution)/shard_map/all_to_all | solution.py:412
  45.1 11.7 %collective-permute-start = (bf16[8,512]{1,0:T(8,128)(2,1)S(1)}, bf16[8,512]{1,0:T(8,128)(2,1)S(1)}, u32[]{:S(2)}, u32[]{:S(2)}) collective-permute-start(bf16[8,512]{1,0:T(8,128)(2,1)S(1)} %slice.3), channel_id=1, source_target_pairs={{0,16},{16,32},{32,48},{48,64},{64,80},{80,96},{96,112},{112,128},... | collective-permute-start | bytes 24584 | tf_op jit(solution)/shard_map/ppermute | solution.py:411
  57.0 25.8 %copy-start.1 = (f32[16,512]{1,0:T(8,128)S(1)}, f32[16,512]{1,0:T(8,128)}, u32[]{:S(2)}) copy-start(f32[16,512]{1,0:T(8,128)} %alog_ref.7) | copy-start | bytes 98308
  57.0 25.8 %copy-start.2 = (bf16[256,512]{1,0:T(8,128)(2,1)S(1)}, bf16[256,512]{1,0:T(8,128)(2,1)}, u32[]{:S(2)}) copy-start(bf16[256,512]{1,0:T(8,128)(2,1)} %dtw_ref.1) | copy-start | bytes 786436
  57.0 25.8 %copy-start.3 = (f32[512]{0:T(512)S(1)}, f32[512]{0:T(512)}, u32[]{:S(2)}) copy-start(f32[512]{0:T(512)} %param.16) | copy-start | bytes 6148
  57.0 41.5 %copy-start.5 = (f32[512]{0:T(512)S(1)}, f32[512]{0:T(512)}, u32[]{:S(2)}) copy-start(f32[512]{0:T(512)} %param.18) | copy-start | bytes 6148
  57.0 51.0 %copy-start.4 = (f32[512]{0:T(512)S(1)}, f32[512]{0:T(512)}, u32[]{:S(2)}) copy-start(f32[512]{0:T(512)} %param.19) | copy-start | bytes 6148
  84.1 6.4 %collective-permute-start.1 = (bf16[72,128]{1,0:T(8,128)(2,1)S(1)}, bf16[72,128]{1,0:T(8,128)(2,1)S(1)}, u32[]{:S(2)}, u32[]{:S(2)}) collective-permute-start(bf16[72,128]{1,0:T(8,128)(2,1)S(1)} %get-tuple-element.24.own_ref), channel_id=1, source_target_pairs={{0,16},{16,0},{32,48},{48,32},{64,80},{80,64},{96,112},{112,96},{1... | collective-permute-start | bytes 55304 | tf_op jit(solution)/shard_map/ppermute | solution.py:446
  91.3 16.7 %all-to-all-start.2 = ((bf16[32,36,128]{2,1,0:T(8,128)(2,1)}), bf16[32,36,128]{2,1,0:T(8,128)(2,1)S(1)}, u32[]{:S(2)}, u32[]{:S(2)}) async-start(bf16[32,36,128]{2,1,0:T(8,128)(2,1)} %shard_map.104), calls=%async_computation.2 | async-start | bytes 655360 | tf_op jit(solution)/shard_map/all_to_all | solution.py:457

commit v9 on v8

--- a/solution.py
+++ b/solution.py
@@ -70,8 +70,7 @@
     sums = proj_ref.shape[0]
     copies = fetches(
         [(proj_hbm, proj_ref), (taps_hbm, taps_ref), (bias_hbm, bias_ref),
-         (tokens_hbm.at[pl.ds(0, 8)], tokens_ref),
-         (weight_ref.at[pl.ds(0, KEEP * depth)], keep_ref)],
+         (tokens_hbm.at[pl.ds(0, 8)], tokens_ref)],
         sems,
     )
     for copy in copies:
@@ -80,8 +79,10 @@
     acc = jnp.zeros((held, width), F32)
     for z in range(shards):
         w = weight_ref[z * depth : (z + 1) * depth, :]
+        if z < KEEP:
+            keep_ref[z * depth : (z + 1) * depth, :] = w
         acc = acc + jnp.dot(main_ref[z], w, preferred_element_type=F32)
-    for copy in copies[:4]:
+    for copy in copies:
         copy.wait()
     pad_ref[8 + rows - held :, :] = acc.astype(BF16).astype(F32)
     edge_ref[:8, :] = pad_ref[rows : rows + 8, :].astype(BF16)
@@ -100,7 +101,6 @@
         block = jnp.where(row_ids == p, jnp.broadcast_to(piece, (8, room)), block)
     wide_ref[:, :, sums:] = jnp.broadcast_to(block[None], (shards, 8, room))
     send_ref[...] = wide_ref[...].astype(BF16)
-    copies[4].wait()
 
 
 def late_kernel(
@@ -404,7 +404,7 @@
         (main, in_weight, tokens, conv_weight, bias, proj),
         (pltpu.VMEM((rows + 8, width), F32), pltpu.VMEM((shards, 8, lanes), F32))
         + held
-        + (pltpu.VMEM((8, tokens.shape[1]), BF16), pltpu.SemaphoreType.DMA((5,))),
+        + (pltpu.VMEM((8, tokens.shape[1]), BF16), pltpu.SemaphoreType.DMA((4,))),
         flops=1 << 29,
         specs=[VMEM] * 2 + [HBM] * 4,
     )

time: 110 us -> 110 us (level)
  transfers between devices with their start and end apart: 4 -> 4, of which waited for: 4 -> 4; matrix products, arithmetic and copies ran while one was open for 0% -> 0% of each run, Pallas kernels for 4% -> 3%
where the time goes in v9:
time: 110 us
  blocking collectives  59 us (54%)
  starting transfers between devices  30.1 us (27%)
  Pallas kernels  13.4 us (12%)
  waiting for transfers between devices  7.38 us (7%)
    all_gather x1, blocking collectives, per_device(): main = lax.all_gather(most, 'tp')  35.6 us
    all_to_all x1, blocking collectives, per_device(): mix = lax.all_to_all(mix, 'tp', 0, 0)  23.4 us
    pallas_call x7, Pallas kernels, call(): pl.pallas_call(kernel, out_shape=outs, in_specs=specs, out_specs=outs_in...  13.4 us
    ppermute x1, starting transfers between devices, per_device(): rim = lax.ppermute(edge[:8], 'seq', [(i, i + 1) for i in range(peers - 1)])  10.9 us
    all_to_all x1, starting transfers between devices, per_device(): everyone = lax.all_to_all(pay, 'seq', 0, 0)  7.13 us
    all_to_all x1, starting transfers between devices, per_device(): got = lax.all_to_all(send, 'tp', 0, 0)  6.41 us
    all_to_all x1, waiting for transfers between devices, per_device(): everyone = lax.all_to_all(pay, 'seq', 0, 0)  5.68 us
    ppermute x1, starting transfers between devices, per_device(): other = lax.ppermute(own, 'seq', [(i, i ^ 1) for i in range(peers)])  5.6 us
  transfers between devices with their start and end apart: 4, of which 4 were waited for; matrix products, arithmetic and copies ran while one was open for 0% of the time, Pallas kernels for 3%

profile of v9, /device:TPU:1, one launch (start us, length us, event | category | flops | bytes accessed | tf_op | source)
XLA Modules:
  0.0 110.0 jit_solution(8505398346055984878)
XLA Ops:
  0.0 0.0 copy-start
  0.0 1.0 shard_map.100
  1.0 35.6 %all-gather.1.main_ref = bf16[16,127,256]{2,1,0:T(8,128)(2,1)S(1)} all-gather(bf16[1,127,256]{2,1,0:T(8,128)(2,1)S(1)} %bitcast.7), channel_id=2, replica_groups=mesh['seq'=32,'tp'=16] {'tp'}, dimensions={0}, use_global_device_ids=true | all-gather | bytes 1105408 | tf_op jit(solution)/shard_map/all_gather | solution.py:399
  36.6 0.0 copy-done
  36.6 2.7 %shard_map.101 = (bf16[16,8,384]{2,1,0:T(8,128)(2,1)}, bf16[16,512]{1,0:T(8,128)(2,1)S(1)}, bf16[128,512]{1,0:T(8,128)(2,1)S(1)}, bf16[3072,512]{1,0:T(8,128)(2,1)S(1)}) custom-call(bf16[16,127,256]{2,1,0:T(8,128)(2,1)S(1)} %all-gather.1.main_ref, bf16[4096,512]{1,0:T(8,128)(2,1)S(1)} %copy-done, bf16[128,256]{1,0:T(8,128)(2,1)} %tokens_hbm.3, ...), custom_call_target="tpu_custom_call" | custom-call | flops 536870912 | bytes 8388608 | tf_op jit(solution)/shard_map/pallas_call | solution.py:359
  39.3 6.4 %all-to-all-start = ((bf16[16,8,384]{2,1,0:T(8,128)(2,1)}), bf16[16,8,384]{2,1,0:T(8,128)(2,1)S(1)}, u32[]{:S(2)}, u32[]{:S(2)}) async-start(bf16[16,8,384]{2,1,0:T(8,128)(2,1)} %get-tuple-element.18), calls=%async_computation | async-start | bytes 196608 | tf_op jit(solution)/shard_map/all_to_all | solution.py:412
  45.8 10.9 %collective-permute-start = (bf16[8,512]{1,0:T(8,128)(2,1)S(1)}, bf16[8,512]{1,0:T(8,128)(2,1)S(1)}, u32[]{:S(2)}, u32[]{:S(2)}) collective-permute-start(bf16[8,512]{1,0:T(8,128)(2,1)S(1)} %slice.3), channel_id=1, source_target_pairs={{0,16},{16,32},{32,48},{48,64},{64,80},{80,96},{96,112},{112,128},... | collective-permute-start | bytes 24584 | tf_op jit(solution)/shard_map/ppermute | solution.py:411
  56.7 0.8 collective-permute-done.rim_ref
  57.5 0.1 all-to-all-done.got_ref
  57.6 0.0 copy-start.1
  57.6 0.0 copy-start.2
  57.6 0.0 copy-start.3
  57.6 0.0 copy-start.5
  57.6 0.0 copy-start.4
  57.6 2.3 %shard_map.102 = (bf16[16,8,512]{2,1,0:T(8,128)(2,1)S(1)}, bf16[8,512]{1,0:T(8,128)(2,1)S(1)}) custom-call(bf16[16,8,384]{2,1,0:T(8,128)(2,1)S(1)} %all-to-all-done.got_ref, bf16[8,512]{1,0:T(8,128)(2,1)S(1)} %collective-permute-done.rim_ref, bf16[16,512]{1,0:T(8,128)(2,1)S(1)} %get-tuple-element.19.edge_ref, ...), custom_call_target="tpu_custom_call" | custom-call | flops 268435456 | bytes 4194304 | tf_op jit(solution)/shard_map/pallas_call | solution.py:359
  59.9 23.4 %all_to_all.15.mix_ref = bf16[16,8,512]{2,1,0:T(8,128)(2,1)S(1)} all-to-all(bf16[16,8,512]{2,1,0:T(8,128)(2,1)S(1)} %get-tuple-element.21), channel_id=1, replica_groups=mesh['seq'=32,'tp'=16] {'tp'}, dimensions={0} | all-to-all | bytes 262144 | tf_op jit(solution)/shard_map/all_to_all | solution.py:429
  83.4 0.0 copy-done.1
  83.4 0.0 copy-done.2
  83.4 0.0 copy-done.3
  83.4 1.3 %shard_map.103 = (f32[128,512]{1,0:T(8,128)S(1)}, f32[128,32]{1,0:T(8,128)S(1)}, bf16[72,128]{1,0:T(8,128)(2,1)S(1)}) custom-call(bf16[16,8,512]{2,1,0:T(8,128)(2,1)S(1)} %all_to_all.15.mix_ref, bf16[256,512]{1,0:T(8,128)(2,1)S(1)} %copy-done.2, f32[1,512]{1,0:T(1,128)S(1)} %bitcast.8, f32[16,512]{1,0:T(8,128)S(1)} %copy-done.1, ...), custom_call_target="tpu_custom_call" | custom-call | flops 67108864 | bytes 1048576 | tf_op jit(solution)/shard_map/pallas_call | solution.py:359
  84.7 5.6 %collective-permute-start.1 = (bf16[72,128]{1,0:T(8,128)(2,1)S(1)}, bf16[72,128]{1,0:T(8,128)(2,1)S(1)}, u32[]{:S(2)}, u32[]{:S(2)}) collective-permute-start(bf16[72,128]{1,0:T(8,128)(2,1)S(1)} %get-tuple-element.24.own_ref), channel_id=1, source_target_pairs={{0,16},{16,0},{32,48},{48,32},{64,80},{80,64},{96,112},{112,96},{1... | collective-permute-start | bytes 55304 | tf_op jit(solution)/shard_map/ppermute | solution.py:446
  90.3 0.8 collective-permute-done.1.other_ref
  91.2 0.8 shard_map.104
  91.9 7.1 %all-to-all-start.2 = ((bf16[32,36,128]{2,1,0:T(8,128)(2,1)}), bf16[32,36,128]{2,1,0:T(8,128)(2,1)S(1)}, u32[]{:S(2)}, u32[]{:S(2)}) async-start(bf16[32,36,128]{2,1,0:T(8,128)(2,1)} %shard_map.104), calls=%async_computation.2 | async-start | bytes 655360 | tf_op jit(solution)/shard_map/all_to_all | solution.py:457
  99.1 0.0 copy-done.5
  99.1 3.8 %shard_map.105 = (f32[128,512]{1,0:T(8,128)S(1)}, bf16[8,16,16,512]{3,2,1,0:T(8,128)(2,1)S(1)}) custom-call(f32[128,32]{1,0:T(8,128)S(1)} %get-tuple-element.27.coef_ref, f32[16,512]{1,0:T(8,128)S(1)} %copy-done.1, bf16[128,512]{1,0:T(8,128)(2,1)S(1)} %get-tuple-element.22.u_ref, bf16[8,512]{1,0:T(8,128)(2,1)S(1)} %get-tuple-element.23.late_u_ref, ...), custom_call_target="tpu_custom_call" | custom-call | flops 268435456 | bytes 4194304 | tf_op jit(solution)/shard_map/pallas_call | solution.py:359
  102.9 5.7 %all-to-all-done.2.all_ref = bf16[32,36,128]{2,1,0:T(8,128)(2,1)S(1)} async-done(((bf16[32,36,128]{2,1,0:T(8,128)(2,1)}), bf16[32,36,128]{2,1,0:T(8,128)(2,1)S(1)}, u32[]{:S(2)}, u32[]{:S(2)}) %all-to-all-start.2) | async-done | bytes 294944 | tf_op jit(solution)/shard_map/all_to_all | solution.py:457
  108.6 0.0 copy-done.4
  108.6 1.4 %shard_map.106 = bf16[128,512]{1,0:T(8,128)(2,1)} custom-call(s32[1]{0:T(128)} %bitcast.mine_ref, bf16[32,36,128]{2,1,0:T(8,128)(2,1)S(1)} %all-to-all-done.2.all_ref, bf16[72,128]{1,0:T(8,128)(2,1)S(1)} %collective-permute-done.1.other_ref, f32[16,512]{1,0:T(8,128)S(1)} %copy-done.1, f32[128,512]{1,0:T(8,128)S(1)} %get-tuple-element.29.y_ref, ...), custom_call_target="tpu_custom_call" | custom-call | flops 67108864 | bytes 1048576 | tf_op jit(solution)/shard_map/pallas_call | solution.py:359
  (1 shorter events, 0.0 us)
Async XLA Ops:
  0.0 36.6 %copy-start = (bf16[4096,512]{1,0:T(8,128)(2,1)S(1)}, bf16[4096,512]{1,0:T(8,128)(2,1)}, u32[]{:S(2)}) copy-start(bf16[4096,512]{1,0:T(8,128)(2,1)} %weight_hbm.1) | copy-start | bytes 12582916
  39.3 18.3 %all-to-all-start = ((bf16[16,8,384]{2,1,0:T(8,128)(2,1)}), bf16[16,8,384]{2,1,0:T(8,128)(2,1)S(1)}, u32[]{:S(2)}, u32[]{:S(2)}) async-start(bf16[16,8,384]{2,1,0:T(8,128)(2,1)} %get-tuple-element.18), calls=%async_computation | async-start | bytes 196608 | tf_op jit(solution)/shard_map/all_to_all | solution.py:412
  45.8 11.7 %collective-permute-start = (bf16[8,512]{1,0:T(8,128)(2,1)S(1)}, bf16[8,512]{1,0:T(8,128)(2,1)S(1)}, u32[]{:S(2)}, u32[]{:S(2)}) collective-permute-start(bf16[8,512]{1,0:T(8,128)(2,1)S(1)} %slice.3), channel_id=1, source_target_pairs={{0,16},{16,32},{32,48},{48,64},{64,80},{80,96},{96,112},{112,128},... | collective-permute-start | bytes 24584 | tf_op jit(solution)/shard_map/ppermute | solution.py:411
  57.6 25.8 %copy-start.1 = (f32[16,512]{1,0:T(8,128)S(1)}, f32[16,512]{1,0:T(8,128)}, u32[]{:S(2)}) copy-start(f32[16,512]{1,0:T(8,128)} %alog_ref.7) | copy-start | bytes 98308
  57.6 25.8 %copy-start.2 = (bf16[256,512]{1,0:T(8,128)(2,1)S(1)}, bf16[256,512]{1,0:T(8,128)(2,1)}, u32[]{:S(2)}) copy-start(bf16[256,512]{1,0:T(8,128)(2,1)} %dtw_ref.1) | copy-start | bytes 786436
  57.6 25.8 %copy-start.3 = (f32[512]{0:T(512)S(1)}, f32[512]{0:T(512)}, u32[]{:S(2)}) copy-start(f32[512]{0:T(512)} %param.16) | copy-start | bytes 6148
  57.6 41.5 %copy-start.5 = (f32[512]{0:T(512)S(1)}, f32[512]{0:T(512)}, u32[]{:S(2)}) copy-start(f32[512]{0:T(512)} %param.18) | copy-start | bytes 6148
  57.6 51.0 %copy-start.4 = (f32[512]{0:T(512)S(1)}, f32[512]{0:T(512)}, u32[]{:S(2)}) copy-start(f32[512]{0:T(512)} %param.19) | copy-start | bytes 6148
  84.7 6.4 %collective-permute-start.1 = (bf16[72,128]{1,0:T(8,128)(2,1)S(1)}, bf16[72,128]{1,0:T(8,128)(2,1)S(1)}, u32[]{:S(2)}, u32[]{:S(2)}) collective-permute-start(bf16[72,128]{1,0:T(8,128)(2,1)S(1)} %get-tuple-element.24.own_ref), channel_id=1, source_target_pairs={{0,16},{16,0},{32,48},{48,32},{64,80},{80,64},{96,112},{112,96},{1... | collective-permute-start | bytes 55304 | tf_op jit(solution)/shard_map/ppermute | solution.py:446
  91.9 16.7 %all-to-all-start.2 = ((bf16[32,36,128]{2,1,0:T(8,128)(2,1)}), bf16[32,36,128]{2,1,0:T(8,128)(2,1)S(1)}, u32[]{:S(2)}, u32[]{:S(2)}) async-start(bf16[32,36,128]{2,1,0:T(8,128)(2,1)} %shard_map.104), calls=%async_computation.2 | async-start | bytes 655360 | tf_op jit(solution)/shard_map/all_to_all | solution.py:457

commit v10 on v8

--- a/solution.py
+++ b/solution.py
@@ -70,8 +70,8 @@
     sums = proj_ref.shape[0]
     copies = fetches(
         [(proj_hbm, proj_ref), (taps_hbm, taps_ref), (bias_hbm, bias_ref),
-         (tokens_hbm.at[pl.ds(0, 8)], tokens_ref),
-         (weight_ref.at[pl.ds(0, KEEP * depth)], keep_ref)],
+         (tokens_hbm.at[pl.ds(0, 8)], tokens_ref)]
+        + [(weight_ref.at[pl.ds(z * depth, depth)], keep_ref.at[pl.ds(z * depth, depth)]) for z in range(KEEP)],
         sems,
     )
     for copy in copies:
@@ -100,7 +100,8 @@
         block = jnp.where(row_ids == p, jnp.broadcast_to(piece, (8, room)), block)
     wide_ref[:, :, sums:] = jnp.broadcast_to(block[None], (shards, 8, room))
     send_ref[...] = wide_ref[...].astype(BF16)
-    copies[4].wait()
+    for copy in copies[4:]:
+        copy.wait()
 
 
 def late_kernel(
@@ -135,15 +136,15 @@
     pay_ref[:, sums : sums + coefs] = total[:, rank:] - high[:, rank:]
     pad_ref[:8, :] = rim_ref[...].astype(F32)
     pad_ref[8:, :] = edge_ref[8:, :].astype(F32)
-    first = first_ref[...].astype(BF16)
-    row_ids = lax.broadcasted_iota(jnp.int32, (shards, width), 0)
+    first = first_ref[...]
+    row_ids = lax.broadcasted_iota(jnp.int32, (shards, depth), 0)
     acc = jnp.zeros((shards, width), F32)
     for z in range(shards):
         if z >= KEEP:
             copies[z - KEEP].wait()
         w = weight_part(keep_ref, weight_ref, z, depth)[...]
-        d = jnp.dot(first, w, preferred_element_type=F32)
-        acc = acc + jnp.where(row_ids == z, d, 0.0)
+        only = jnp.where(row_ids == z, first, 0.0).astype(BF16)
+        acc = acc + jnp.dot(only, w, preferred_element_type=F32)
     for copy in copies[shards - KEEP :]:
         copy.wait()
     pad_ref[8:9, :] = jnp.sum(acc, axis=0, keepdims=True).astype(BF16).astype(F32)
@@ -404,7 +405,7 @@
         (main, in_weight, tokens, conv_weight, bias, proj),
         (pltpu.VMEM((rows + 8, width), F32), pltpu.VMEM((shards, 8, lanes), F32))
         + held
-        + (pltpu.VMEM((8, tokens.shape[1]), BF16), pltpu.SemaphoreType.DMA((5,))),
+        + (pltpu.VMEM((8, tokens.shape[1]), BF16), pltpu.SemaphoreType.DMA((4 + KEEP,))),
         flops=1 << 29,
         specs=[VMEM] * 2 + [HBM] * 4,
     )

time: 110 us -> 110 us (level)
  no operation moved by 1% of the time
where the time goes in v10:
time: 110 us; the launch traced here: 109 us
  blocking collectives  59 us (54%)
  starting transfers between devices  30.1 us (27%)
  Pallas kernels  12.7 us (12%)
  waiting for transfers between devices  7.37 us (7%)
    all_gather x1, blocking collectives, per_device(): main = lax.all_gather(most, 'tp')  35.6 us
    all_to_all x1, blocking collectives, per_device(): mix = lax.all_to_all(mix, 'tp', 0, 0)  23.4 us
    pallas_call x7, Pallas kernels, call(): pl.pallas_call(kernel, out_shape=outs, in_specs=specs, out_specs=outs_in...  12.7 us
    ppermute x1, starting transfers between devices, per_device(): rim = lax.ppermute(edge[:8], 'seq', [(i, i + 1) for i in range(peers - 1)])  10.9 us
    all_to_all x1, starting transfers between devices, per_device(): everyone = lax.all_to_all(pay, 'seq', 0, 0)  7.13 us
    all_to_all x1, starting transfers between devices, per_device(): got = lax.all_to_all(send, 'tp', 0, 0)  6.41 us
    all_to_all x1, waiting for transfers between devices, per_device(): everyone = lax.all_to_all(pay, 'seq', 0, 0)  5.67 us
    ppermute x1, starting transfers between devices, per_device(): other = lax.ppermute(own, 'seq', [(i, i ^ 1) for i in range(peers)])  5.59 us
  transfers between devices with their start and end apart: 4, of which 4 were waited for; matrix products, arithmetic and copies ran while one was open for 0% of the time, Pallas kernels for 4%

profile of v10, /device:TPU:1, one launch (start us, length us, event | category | flops | bytes accessed | tf_op | source)
XLA Modules:
  0.0 109.3 jit_solution(7268223873029151601)
XLA Ops:
  0.0 0.0 copy-start
  0.0 1.0 shard_map.100
  1.0 35.6 %all-gather.1.main_ref = bf16[16,127,256]{2,1,0:T(8,128)(2,1)S(1)} all-gather(bf16[1,127,256]{2,1,0:T(8,128)(2,1)S(1)} %bitcast.7), channel_id=2, replica_groups=mesh['seq'=32,'tp'=16] {'tp'}, dimensions={0}, use_global_device_ids=true | all-gather | bytes 1105408 | tf_op jit(solution)/shard_map/all_gather | solution.py:400
  36.6 0.0 copy-done
  36.6 2.2 %shard_map.101 = (bf16[16,8,384]{2,1,0:T(8,128)(2,1)}, bf16[16,512]{1,0:T(8,128)(2,1)S(1)}, bf16[128,512]{1,0:T(8,128)(2,1)S(1)}, bf16[3072,512]{1,0:T(8,128)(2,1)S(1)}) custom-call(bf16[16,127,256]{2,1,0:T(8,128)(2,1)S(1)} %all-gather.1.main_ref, bf16[4096,512]{1,0:T(8,128)(2,1)S(1)} %copy-done, bf16[128,256]{1,0:T(8,128)(2,1)} %tokens_hbm.3, ...), custom_call_target="tpu_custom_call" | custom-call | flops 536870912 | bytes 8388608 | tf_op jit(solution)/shard_map/pallas_call | solution.py:360
  38.8 6.4 %all-to-all-start = ((bf16[16,8,384]{2,1,0:T(8,128)(2,1)}), bf16[16,8,384]{2,1,0:T(8,128)(2,1)S(1)}, u32[]{:S(2)}, u32[]{:S(2)}) async-start(bf16[16,8,384]{2,1,0:T(8,128)(2,1)} %get-tuple-element.18), calls=%async_computation | async-start | bytes 196608 | tf_op jit(solution)/shard_map/all_to_all | solution.py:413
  45.3 10.9 %collective-permute-start = (bf16[8,512]{1,0:T(8,128)(2,1)S(1)}, bf16[8,512]{1,0:T(8,128)(2,1)S(1)}, u32[]{:S(2)}, u32[]{:S(2)}) collective-permute-start(bf16[8,512]{1,0:T(8,128)(2,1)S(1)} %slice.3), channel_id=1, source_target_pairs={{0,16},{16,32},{32,48},{48,64},{64,80},{80,96},{96,112},{112,128},... | collective-permute-start | bytes 24584 | tf_op jit(solution)/shard_map/ppermute | solution.py:412
  56.2 0.8 collective-permute-done.rim_ref
  57.0 0.1 all-to-all-done.got_ref
  57.1 0.0 copy-start.1
  57.1 0.0 copy-start.2
  57.1 0.0 copy-start.3
  57.1 0.0 copy-start.5
  57.1 0.0 copy-start.4
  57.1 2.1 %shard_map.102 = (bf16[16,8,512]{2,1,0:T(8,128)(2,1)S(1)}, bf16[8,512]{1,0:T(8,128)(2,1)S(1)}) custom-call(bf16[16,8,384]{2,1,0:T(8,128)(2,1)S(1)} %all-to-all-done.got_ref, bf16[8,512]{1,0:T(8,128)(2,1)S(1)} %collective-permute-done.rim_ref, bf16[16,512]{1,0:T(8,128)(2,1)S(1)} %get-tuple-element.19.edge_ref, ...), custom_call_target="tpu_custom_call" | custom-call | flops 268435456 | bytes 4194304 | tf_op jit(solution)/shard_map/pallas_call | solution.py:360
  59.2 23.4 %all_to_all.15.mix_ref = bf16[16,8,512]{2,1,0:T(8,128)(2,1)S(1)} all-to-all(bf16[16,8,512]{2,1,0:T(8,128)(2,1)S(1)} %get-tuple-element.21), channel_id=1, replica_groups=mesh['seq'=32,'tp'=16] {'tp'}, dimensions={0} | all-to-all | bytes 262144 | tf_op jit(solution)/shard_map/all_to_all | solution.py:430
  82.7 0.0 copy-done.1
  82.7 0.0 copy-done.2
  82.7 0.0 copy-done.3
  82.7 1.3 %shard_map.103 = (f32[128,512]{1,0:T(8,128)S(1)}, f32[128,32]{1,0:T(8,128)S(1)}, bf16[72,128]{1,0:T(8,128)(2,1)S(1)}) custom-call(bf16[16,8,512]{2,1,0:T(8,128)(2,1)S(1)} %all_to_all.15.mix_ref, bf16[256,512]{1,0:T(8,128)(2,1)S(1)} %copy-done.2, f32[1,512]{1,0:T(1,128)S(1)} %bitcast.8, f32[16,512]{1,0:T(8,128)S(1)} %copy-done.1, ...), custom_call_target="tpu_custom_call" | custom-call | flops 67108864 | bytes 1048576 | tf_op jit(solution)/shard_map/pallas_call | solution.py:360
  84.0 5.6 %collective-permute-start.1 = (bf16[72,128]{1,0:T(8,128)(2,1)S(1)}, bf16[72,128]{1,0:T(8,128)(2,1)S(1)}, u32[]{:S(2)}, u32[]{:S(2)}) collective-permute-start(bf16[72,128]{1,0:T(8,128)(2,1)S(1)} %get-tuple-element.24.own_ref), channel_id=1, source_target_pairs={{0,16},{16,0},{32,48},{48,32},{64,80},{80,64},{96,112},{112,96},{1... | collective-permute-start | bytes 55304 | tf_op jit(solution)/shard_map/ppermute | solution.py:447
  89.6 0.8 collective-permute-done.1.other_ref
  90.4 0.8 shard_map.104
  91.2 7.1 %all-to-all-start.2 = ((bf16[32,36,128]{2,1,0:T(8,128)(2,1)}), bf16[32,36,128]{2,1,0:T(8,128)(2,1)S(1)}, u32[]{:S(2)}, u32[]{:S(2)}) async-start(bf16[32,36,128]{2,1,0:T(8,128)(2,1)} %shard_map.104), calls=%async_computation.2 | async-start | bytes 655360 | tf_op jit(solution)/shard_map/all_to_all | solution.py:458
  98.3 0.0 copy-done.5
  98.4 3.8 %shard_map.105 = (f32[128,512]{1,0:T(8,128)S(1)}, bf16[8,16,16,512]{3,2,1,0:T(8,128)(2,1)S(1)}) custom-call(f32[128,32]{1,0:T(8,128)S(1)} %get-tuple-element.27.coef_ref, f32[16,512]{1,0:T(8,128)S(1)} %copy-done.1, bf16[128,512]{1,0:T(8,128)(2,1)S(1)} %get-tuple-element.22.u_ref, bf16[8,512]{1,0:T(8,128)(2,1)S(1)} %get-tuple-element.23.late_u_ref, ...), custom_call_target="tpu_custom_call" | custom-call | flops 268435456 | bytes 4194304 | tf_op jit(solution)/shard_map/pallas_call | solution.py:360
  102.2 5.7 %all-to-all-done.2.all_ref = bf16[32,36,128]{2,1,0:T(8,128)(2,1)S(1)} async-done(((bf16[32,36,128]{2,1,0:T(8,128)(2,1)}), bf16[32,36,128]{2,1,0:T(8,128)(2,1)S(1)}, u32[]{:S(2)}, u32[]{:S(2)}) %all-to-all-start.2) | async-done | bytes 294944 | tf_op jit(solution)/shard_map/all_to_all | solution.py:458
  107.9 0.0 copy-done.4
  107.9 1.4 %shard_map.106 = bf16[128,512]{1,0:T(8,128)(2,1)} custom-call(s32[1]{0:T(128)} %bitcast.mine_ref, bf16[32,36,128]{2,1,0:T(8,128)(2,1)S(1)} %all-to-all-done.2.all_ref, bf16[72,128]{1,0:T(8,128)(2,1)S(1)} %collective-permute-done.1.other_ref, f32[16,512]{1,0:T(8,128)S(1)} %copy-done.1, f32[128,512]{1,0:T(8,128)S(1)} %get-tuple-element.29.y_ref, ...), custom_call_target="tpu_custom_call" | custom-call | flops 67108864 | bytes 1048576 | tf_op jit(solution)/shard_map/pallas_call | solution.py:360
  (1 shorter events, 0.0 us)
Async XLA Ops:
  0.0 36.6 %copy-start = (bf16[4096,512]{1,0:T(8,128)(2,1)S(1)}, bf16[4096,512]{1,0:T(8,128)(2,1)}, u32[]{:S(2)}) copy-start(bf16[4096,512]{1,0:T(8,128)(2,1)} %weight_hbm.1) | copy-start | bytes 12582916
  38.8 18.3 %all-to-all-start = ((bf16[16,8,384]{2,1,0:T(8,128)(2,1)}), bf16[16,8,384]{2,1,0:T(8,128)(2,1)S(1)}, u32[]{:S(2)}, u32[]{:S(2)}) async-start(bf16[16,8,384]{2,1,0:T(8,128)(2,1)} %get-tuple-element.18), calls=%async_computation | async-start | bytes 196608 | tf_op jit(solution)/shard_map/all_to_all | solution.py:413
  45.3 11.7 %collective-permute-start = (bf16[8,512]{1,0:T(8,128)(2,1)S(1)}, bf16[8,512]{1,0:T(8,128)(2,1)S(1)}, u32[]{:S(2)}, u32[]{:S(2)}) collective-permute-start(bf16[8,512]{1,0:T(8,128)(2,1)S(1)} %slice.3), channel_id=1, source_target_pairs={{0,16},{16,32},{32,48},{48,64},{64,80},{80,96},{96,112},{112,128},... | collective-permute-start | bytes 24584 | tf_op jit(solution)/shard_map/ppermute | solution.py:412
  57.1 25.6 %copy-start.1 = (f32[16,512]{1,0:T(8,128)S(1)}, f32[16,512]{1,0:T(8,128)}, u32[]{:S(2)}) copy-start(f32[16,512]{1,0:T(8,128)} %alog_ref.7) | copy-start | bytes 98308
  57.1 25.6 %copy-start.2 = (bf16[256,512]{1,0:T(8,128)(2,1)S(1)}, bf16[256,512]{1,0:T(8,128)(2,1)}, u32[]{:S(2)}) copy-start(bf16[256,512]{1,0:T(8,128)(2,1)} %dtw_ref.1) | copy-start | bytes 786436
  57.1 25.6 %copy-start.3 = (f32[512]{0:T(512)S(1)}, f32[512]{0:T(512)}, u32[]{:S(2)}) copy-start(f32[512]{0:T(512)} %param.16) | copy-start | bytes 6148
  57.1 41.3 %copy-start.5 = (f32[512]{0:T(512)S(1)}, f32[512]{0:T(512)}, u32[]{:S(2)}) copy-start(f32[512]{0:T(512)} %param.18) | copy-start | bytes 6148
  57.1 50.8 %copy-start.4 = (f32[512]{0:T(512)S(1)}, f32[512]{0:T(512)}, u32[]{:S(2)}) copy-start(f32[512]{0:T(512)} %param.19) | copy-start | bytes 6148
  84.0 6.4 %collective-permute-start.1 = (bf16[72,128]{1,0:T(8,128)(2,1)S(1)}, bf16[72,128]{1,0:T(8,128)(2,1)S(1)}, u32[]{:S(2)}, u32[]{:S(2)}) collective-permute-start(bf16[72,128]{1,0:T(8,128)(2,1)S(1)} %get-tuple-element.24.own_ref), channel_id=1, source_target_pairs={{0,16},{16,0},{32,48},{48,32},{64,80},{80,64},{96,112},{112,96},{1... | collective-permute-start | bytes 55304 | tf_op jit(solution)/shard_map/ppermute | solution.py:447
  91.2 16.7 %all-to-all-start.2 = ((bf16[32,36,128]{2,1,0:T(8,128)(2,1)}), bf16[32,36,128]{2,1,0:T(8,128)(2,1)S(1)}, u32[]{:S(2)}, u32[]{:S(2)}) async-start(bf16[32,36,128]{2,1,0:T(8,128)(2,1)} %shard_map.104), calls=%async_computation.2 | async-start | bytes 655360 | tf_op jit(solution)/shard_map/all_to_all | solution.py:458

commit v11 on v10

--- a/solution.py
+++ b/solution.py
@@ -71,7 +71,7 @@
     copies = fetches(
         [(proj_hbm, proj_ref), (taps_hbm, taps_ref), (bias_hbm, bias_ref),
          (tokens_hbm.at[pl.ds(0, 8)], tokens_ref)]
-        + [(weight_ref.at[pl.ds(z * depth, depth)], keep_ref.at[pl.ds(z * depth, depth)]) for z in range(KEEP)],
+        + [(weight_ref.at[pl.ds(0, KEEP * depth)], keep_ref)],
         sems,
     )
     for copy in copies:
@@ -100,8 +100,7 @@
         block = jnp.where(row_ids == p, jnp.broadcast_to(piece, (8, room)), block)
     wide_ref[:, :, sums:] = jnp.broadcast_to(block[None], (shards, 8, room))
     send_ref[...] = wide_ref[...].astype(BF16)
-    for copy in copies[4:]:
-        copy.wait()
+    copies[4].wait()
 
 
 def late_kernel(
@@ -405,7 +404,7 @@
         (main, in_weight, tokens, conv_weight, bias, proj),
         (pltpu.VMEM((rows + 8, width), F32), pltpu.VMEM((shards, 8, lanes), F32))
         + held
-        + (pltpu.VMEM((8, tokens.shape[1]), BF16), pltpu.SemaphoreType.DMA((4 + KEEP,))),
+        + (pltpu.VMEM((8, tokens.shape[1]), BF16), pltpu.SemaphoreType.DMA((5,))),
         flops=1 << 29,
         specs=[VMEM] * 2 + [HBM] * 4,
     )

time: 110 us -> 110 us (level)
  no operation moved by 1% of the time
where the time goes in v11:
time: 110 us; the launch traced here: 109 us
  blocking collectives  59 us (54%)
  starting transfers between devices  30.1 us (27%)
  Pallas kernels  12.6 us (11%)
  waiting for transfers between devices  7.38 us (7%)
    all_gather x1, blocking collectives, per_device(): main = lax.all_gather(most, 'tp')  35.6 us
    all_to_all x1, blocking collectives, per_device(): mix = lax.all_to_all(mix, 'tp', 0, 0)  23.4 us
    pallas_call x7, Pallas kernels, call(): pl.pallas_call(kernel, out_shape=outs, in_specs=specs, out_specs=outs_in...  12.6 us
    ppermute x1, starting transfers between devices, per_device(): rim = lax.ppermute(edge[:8], 'seq', [(i, i + 1) for i in range(peers - 1)])  10.9 us
    all_to_all x1, starting transfers between devices, per_device(): everyone = lax.all_to_all(pay, 'seq', 0, 0)  7.13 us
    all_to_all x1, starting transfers between devices, per_device(): got = lax.all_to_all(send, 'tp', 0, 0)  6.41 us
    all_to_all x1, waiting for transfers between devices, per_device(): everyone = lax.all_to_all(pay, 'seq', 0, 0)  5.68 us
    ppermute x1, starting transfers between devices, per_device(): other = lax.ppermute(own, 'seq', [(i, i ^ 1) for i in range(peers)])  5.6 us
  transfers between devices with their start and end apart: 4, of which 4 were waited for; matrix products, arithmetic and copies ran while one was open for 0% of the time, Pallas kernels for 4%

profile of v11, /device:TPU:1, one launch (start us, length us, event | category | flops | bytes accessed | tf_op | source)
XLA Modules:
  0.0 109.2 jit_solution(11033736313870883706)
XLA Ops:
  0.0 0.0 copy-start
  0.0 1.0 shard_map.100
  1.0 35.6 %all-gather.1.main_ref = bf16[16,127,256]{2,1,0:T(8,128)(2,1)S(1)} all-gather(bf16[1,127,256]{2,1,0:T(8,128)(2,1)S(1)} %bitcast.7), channel_id=2, replica_groups=mesh['seq'=32,'tp'=16] {'tp'}, dimensions={0}, use_global_device_ids=true | all-gather | bytes 1105408 | tf_op jit(solution)/shard_map/all_gather | solution.py:399
  36.6 0.0 copy-done
  36.6 2.1 %shard_map.101 = (bf16[16,8,384]{2,1,0:T(8,128)(2,1)}, bf16[16,512]{1,0:T(8,128)(2,1)S(1)}, bf16[128,512]{1,0:T(8,128)(2,1)S(1)}, bf16[3072,512]{1,0:T(8,128)(2,1)S(1)}) custom-call(bf16[16,127,256]{2,1,0:T(8,128)(2,1)S(1)} %all-gather.1.main_ref, bf16[4096,512]{1,0:T(8,128)(2,1)S(1)} %copy-done, bf16[128,256]{1,0:T(8,128)(2,1)} %tokens_hbm.3, ...), custom_call_target="tpu_custom_call" | custom-call | flops 536870912 | bytes 8388608 | tf_op jit(solution)/shard_map/pallas_call | solution.py:359
  38.7 6.4 %all-to-all-start = ((bf16[16,8,384]{2,1,0:T(8,128)(2,1)}), bf16[16,8,384]{2,1,0:T(8,128)(2,1)S(1)}, u32[]{:S(2)}, u32[]{:S(2)}) async-start(bf16[16,8,384]{2,1,0:T(8,128)(2,1)} %get-tuple-element.18), calls=%async_computation | async-start | bytes 196608 | tf_op jit(solution)/shard_map/all_to_all | solution.py:412
  45.1 10.9 %collective-permute-start = (bf16[8,512]{1,0:T(8,128)(2,1)S(1)}, bf16[8,512]{1,0:T(8,128)(2,1)S(1)}, u32[]{:S(2)}, u32[]{:S(2)}) collective-permute-start(bf16[8,512]{1,0:T(8,128)(2,1)S(1)} %slice.3), channel_id=1, source_target_pairs={{0,16},{16,32},{32,48},{48,64},{64,80},{80,96},{96,112},{112,128},... | collective-permute-start | bytes 24584 | tf_op jit(solution)/shard_map/ppermute | solution.py:411
  56.1 0.8 collective-permute-done.rim_ref
  56.9 0.1 all-to-all-done.got_ref
  57.0 0.0 copy-start.1
  57.0 0.0 copy-start.2
  57.0 0.0 copy-start.3
  57.0 0.0 copy-start.5
  57.0 0.0 copy-start.4
  57.0 2.1 %shard_map.102 = (bf16[16,8,512]{2,1,0:T(8,128)(2,1)S(1)}, bf16[8,512]{1,0:T(8,128)(2,1)S(1)}) custom-call(bf16[16,8,384]{2,1,0:T(8,128)(2,1)S(1)} %all-to-all-done.got_ref, bf16[8,512]{1,0:T(8,128)(2,1)S(1)} %collective-permute-done.rim_ref, bf16[16,512]{1,0:T(8,128)(2,1)S(1)} %get-tuple-element.19.edge_ref, ...), custom_call_target="tpu_custom_call" | custom-call | flops 268435456 | bytes 4194304 | tf_op jit(solution)/shard_map/pallas_call | solution.py:359
  59.1 23.4 %all_to_all.15.mix_ref = bf16[16,8,512]{2,1,0:T(8,128)(2,1)S(1)} all-to-all(bf16[16,8,512]{2,1,0:T(8,128)(2,1)S(1)} %get-tuple-element.21), channel_id=1, replica_groups=mesh['seq'=32,'tp'=16] {'tp'}, dimensions={0} | all-to-all | bytes 262144 | tf_op jit(solution)/shard_map/all_to_all | solution.py:429
  82.6 0.0 copy-done.1
  82.6 0.0 copy-done.2
  82.6 0.0 copy-done.3
  82.6 1.3 %shard_map.103 = (f32[128,512]{1,0:T(8,128)S(1)}, f32[128,32]{1,0:T(8,128)S(1)}, bf16[72,128]{1,0:T(8,128)(2,1)S(1)}) custom-call(bf16[16,8,512]{2,1,0:T(8,128)(2,1)S(1)} %all_to_all.15.mix_ref, bf16[256,512]{1,0:T(8,128)(2,1)S(1)} %copy-done.2, f32[1,512]{1,0:T(1,128)S(1)} %bitcast.8, f32[16,512]{1,0:T(8,128)S(1)} %copy-done.1, ...), custom_call_target="tpu_custom_call" | custom-call | flops 67108864 | bytes 1048576 | tf_op jit(solution)/shard_map/pallas_call | solution.py:359
  83.9 5.6 %collective-permute-start.1 = (bf16[72,128]{1,0:T(8,128)(2,1)S(1)}, bf16[72,128]{1,0:T(8,128)(2,1)S(1)}, u32[]{:S(2)}, u32[]{:S(2)}) collective-permute-start(bf16[72,128]{1,0:T(8,128)(2,1)S(1)} %get-tuple-element.24.own_ref), channel_id=1, source_target_pairs={{0,16},{16,0},{32,48},{48,32},{64,80},{80,64},{96,112},{112,96},{1... | collective-permute-start | bytes 55304 | tf_op jit(solution)/shard_map/ppermute | solution.py:446
  89.5 0.8 collective-permute-done.1.other_ref
  90.3 0.8 shard_map.104
  91.1 7.1 %all-to-all-start.2 = ((bf16[32,36,128]{2,1,0:T(8,128)(2,1)}), bf16[32,36,128]{2,1,0:T(8,128)(2,1)S(1)}, u32[]{:S(2)}, u32[]{:S(2)}) async-start(bf16[32,36,128]{2,1,0:T(8,128)(2,1)} %shard_map.104), calls=%async_computation.2 | async-start | bytes 655360 | tf_op jit(solution)/shard_map/all_to_all | solution.py:457
  98.2 0.0 copy-done.5
  98.2 3.8 %shard_map.105 = (f32[128,512]{1,0:T(8,128)S(1)}, bf16[8,16,16,512]{3,2,1,0:T(8,128)(2,1)S(1)}) custom-call(f32[128,32]{1,0:T(8,128)S(1)} %get-tuple-element.27.coef_ref, f32[16,512]{1,0:T(8,128)S(1)} %copy-done.1, bf16[128,512]{1,0:T(8,128)(2,1)S(1)} %get-tuple-element.22.u_ref, bf16[8,512]{1,0:T(8,128)(2,1)S(1)} %get-tuple-element.23.late_u_ref, ...), custom_call_target="tpu_custom_call" | custom-call | flops 268435456 | bytes 4194304 | tf_op jit(solution)/shard_map/pallas_call | solution.py:359
  102.1 5.7 %all-to-all-done.2.all_ref = bf16[32,36,128]{2,1,0:T(8,128)(2,1)S(1)} async-done(((bf16[32,36,128]{2,1,0:T(8,128)(2,1)}), bf16[32,36,128]{2,1,0:T(8,128)(2,1)S(1)}, u32[]{:S(2)}, u32[]{:S(2)}) %all-to-all-start.2) | async-done | bytes 294944 | tf_op jit(solution)/shard_map/all_to_all | solution.py:457
  107.8 0.0 copy-done.4
  107.8 1.4 %shard_map.106 = bf16[128,512]{1,0:T(8,128)(2,1)} custom-call(s32[1]{0:T(128)} %bitcast.mine_ref, bf16[32,36,128]{2,1,0:T(8,128)(2,1)S(1)} %all-to-all-done.2.all_ref, bf16[72,128]{1,0:T(8,128)(2,1)S(1)} %collective-permute-done.1.other_ref, f32[16,512]{1,0:T(8,128)S(1)} %copy-done.1, f32[128,512]{1,0:T(8,128)S(1)} %get-tuple-element.29.y_ref, ...), custom_call_target="tpu_custom_call" | custom-call | flops 67108864 | bytes 1048576 | tf_op jit(solution)/shard_map/pallas_call | solution.py:359
  (1 shorter events, 0.0 us)
Async XLA Ops:
  0.0 36.6 %copy-start = (bf16[4096,512]{1,0:T(8,128)(2,1)S(1)}, bf16[4096,512]{1,0:T(8,128)(2,1)}, u32[]{:S(2)}) copy-start(bf16[4096,512]{1,0:T(8,128)(2,1)} %weight_hbm.1) | copy-start | bytes 12582916
  38.7 18.3 %all-to-all-start = ((bf16[16,8,384]{2,1,0:T(8,128)(2,1)}), bf16[16,8,384]{2,1,0:T(8,128)(2,1)S(1)}, u32[]{:S(2)}, u32[]{:S(2)}) async-start(bf16[16,8,384]{2,1,0:T(8,128)(2,1)} %get-tuple-element.18), calls=%async_computation | async-start | bytes 196608 | tf_op jit(solution)/shard_map/all_to_all | solution.py:412
  45.1 11.7 %collective-permute-start = (bf16[8,512]{1,0:T(8,128)(2,1)S(1)}, bf16[8,512]{1,0:T(8,128)(2,1)S(1)}, u32[]{:S(2)}, u32[]{:S(2)}) collective-permute-start(bf16[8,512]{1,0:T(8,128)(2,1)S(1)} %slice.3), channel_id=1, source_target_pairs={{0,16},{16,32},{32,48},{48,64},{64,80},{80,96},{96,112},{112,128},... | collective-permute-start | bytes 24584 | tf_op jit(solution)/shard_map/ppermute | solution.py:411
  57.0 25.6 %copy-start.1 = (f32[16,512]{1,0:T(8,128)S(1)}, f32[16,512]{1,0:T(8,128)}, u32[]{:S(2)}) copy-start(f32[16,512]{1,0:T(8,128)} %alog_ref.7) | copy-start | bytes 98308
  57.0 25.6 %copy-start.2 = (bf16[256,512]{1,0:T(8,128)(2,1)S(1)}, bf16[256,512]{1,0:T(8,128)(2,1)}, u32[]{:S(2)}) copy-start(bf16[256,512]{1,0:T(8,128)(2,1)} %dtw_ref.1) | copy-start | bytes 786436
  57.0 25.6 %copy-start.3 = (f32[512]{0:T(512)S(1)}, f32[512]{0:T(512)}, u32[]{:S(2)}) copy-start(f32[512]{0:T(512)} %param.16) | copy-start | bytes 6148
  57.0 41.3 %copy-start.5 = (f32[512]{0:T(512)S(1)}, f32[512]{0:T(512)}, u32[]{:S(2)}) copy-start(f32[512]{0:T(512)} %param.18) | copy-start | bytes 6148
  57.0 50.8 %copy-start.4 = (f32[512]{0:T(512)S(1)}, f32[512]{0:T(512)}, u32[]{:S(2)}) copy-start(f32[512]{0:T(512)} %param.19) | copy-start | bytes 6148
  83.9 6.4 %collective-permute-start.1 = (bf16[72,128]{1,0:T(8,128)(2,1)S(1)}, bf16[72,128]{1,0:T(8,128)(2,1)S(1)}, u32[]{:S(2)}, u32[]{:S(2)}) collective-permute-start(bf16[72,128]{1,0:T(8,128)(2,1)S(1)} %get-tuple-element.24.own_ref), channel_id=1, source_target_pairs={{0,16},{16,0},{32,48},{48,32},{64,80},{80,64},{96,112},{112,96},{1... | collective-permute-start | bytes 55304 | tf_op jit(solution)/shard_map/ppermute | solution.py:446
  91.1 16.7 %all-to-all-start.2 = ((bf16[32,36,128]{2,1,0:T(8,128)(2,1)}), bf16[32,36,128]{2,1,0:T(8,128)(2,1)S(1)}, u32[]{:S(2)}, u32[]{:S(2)}) async-start(bf16[32,36,128]{2,1,0:T(8,128)(2,1)} %shard_map.104), calls=%async_computation.2 | async-start | bytes 655360 | tf_op jit(solution)/shard_map/all_to_all | solution.py:457

commit v12 on v7

--- a/solution.py
+++ b/solution.py
@@ -135,15 +135,15 @@
     pay_ref[:, sums : sums + coefs] = total[:, rank:] - high[:, rank:]
     pad_ref[:8, :] = rim_ref[...].astype(F32)
     pad_ref[8:, :] = edge_ref[8:, :].astype(F32)
-    first = first_ref[...].astype(BF16)
-    row_ids = lax.broadcasted_iota(jnp.int32, (shards, width), 0)
+    first = first_ref[...]
+    row_ids = lax.broadcasted_iota(jnp.int32, (shards, depth), 0)
     acc = jnp.zeros((shards, width), F32)
     for z in range(shards):
         if z >= KEEP:
             copies[z - KEEP].wait()
         w = weight_part(keep_ref, weight_ref, z, depth)[...]
-        d = jnp.dot(first, w, preferred_element_type=F32)
-        acc = acc + jnp.where(row_ids == z, d, 0.0)
+        only = jnp.where(row_ids == z, first, 0.0).astype(BF16)
+        acc = acc + jnp.dot(only, w, preferred_element_type=F32)
     for copy in copies[shards - KEEP :]:
         copy.wait()
     pad_ref[8:9, :] = jnp.sum(acc, axis=0, keepdims=True).astype(BF16).astype(F32)

time: 110 us -> 109 us (level)
  no operation moved by 1% of the time
where the time goes in v12:
time: 109 us
  blocking collectives  59 us (54%)
  starting transfers between devices  27.8 us (26%)
  Pallas kernels  12.8 us (12%)
  waiting for transfers between devices  9.31 us (9%)
    all_gather x1, blocking collectives, per_device(): main = lax.all_gather(most, 'tp')  35.6 us
    all_to_all x1, blocking collectives, per_device(): mix = lax.all_to_all(mix, 'tp', 0, 0)  23.4 us
    pallas_call x6, Pallas kernels, call(): pl.pallas_call(kernel, out_shape=outs, in_specs=specs, out_specs=outs_in...  12.8 us
    ppermute x1, starting transfers between devices, per_device(): rim = lax.ppermute(edge[:8], 'seq', [(i, i + 1) for i in range(peers - 1)])  10.9 us
    all_to_all x1, starting transfers between devices, per_device(): everyone = lax.all_to_all(pay, 'seq', 0, 0)  10.5 us
    all_to_all x1, waiting for transfers between devices, per_device(): everyone = lax.all_to_all(pay, 'seq', 0, 0)  8.42 us
    all_to_all x1, starting transfers between devices, per_device(): got = lax.all_to_all(send, 'tp', 0, 0)  6.41 us
  transfers between devices with their start and end apart: 3, of which 3 were waited for; matrix products, arithmetic and copies ran while one was open for 0% of the time, Pallas kernels for 3%

profile of v12, /device:TPU:1, one launch (start us, length us, event | category | flops | bytes accessed | tf_op | source)
XLA Modules:
  0.0 109.1 jit_solution(10892029184981173618)
XLA Ops:
  0.0 0.0 copy-start
  0.0 1.0 shard_map.100
  1.0 35.6 %all-gather.1.main_ref = bf16[16,127,256]{2,1,0:T(8,128)(2,1)S(1)} all-gather(bf16[1,127,256]{2,1,0:T(8,128)(2,1)S(1)} %bitcast.7), channel_id=2, replica_groups=mesh['seq'=32,'tp'=16] {'tp'}, dimensions={0}, use_global_device_ids=true | all-gather | bytes 1105408 | tf_op jit(solution)/shard_map/all_gather | solution.py:363
  36.6 0.0 copy-done
  36.6 2.1 %shard_map.101 = (bf16[16,8,384]{2,1,0:T(8,128)(2,1)}, bf16[16,512]{1,0:T(8,128)(2,1)S(1)}, bf16[128,512]{1,0:T(8,128)(2,1)S(1)}, bf16[3072,512]{1,0:T(8,128)(2,1)S(1)}) custom-call(bf16[16,127,256]{2,1,0:T(8,128)(2,1)S(1)} %all-gather.1.main_ref, bf16[4096,512]{1,0:T(8,128)(2,1)S(1)} %copy-done, bf16[128,256]{1,0:T(8,128)(2,1)} %tokens_hbm.3, ...), custom_call_target="tpu_custom_call" | custom-call | flops 536870912 | bytes 8388608 | tf_op jit(solution)/shard_map/pallas_call | solution.py:323
  38.7 6.4 %all-to-all-start = ((bf16[16,8,384]{2,1,0:T(8,128)(2,1)}), bf16[16,8,384]{2,1,0:T(8,128)(2,1)S(1)}, u32[]{:S(2)}, u32[]{:S(2)}) async-start(bf16[16,8,384]{2,1,0:T(8,128)(2,1)} %get-tuple-element.16), calls=%async_computation | async-start | bytes 196608 | tf_op jit(solution)/shard_map/all_to_all | solution.py:376
  45.1 10.9 %collective-permute-start = (bf16[8,512]{1,0:T(8,128)(2,1)S(1)}, bf16[8,512]{1,0:T(8,128)(2,1)S(1)}, u32[]{:S(2)}, u32[]{:S(2)}) collective-permute-start(bf16[8,512]{1,0:T(8,128)(2,1)S(1)} %slice.3), channel_id=1, source_target_pairs={{0,16},{16,32},{32,48},{48,64},{64,80},{80,96},{96,112},{112,128},... | collective-permute-start | bytes 24584 | tf_op jit(solution)/shard_map/ppermute | solution.py:375
  56.1 0.8 collective-permute-done.rim_ref
  56.9 0.1 all-to-all-done.got_ref
  57.0 0.0 copy-start.1
  57.0 0.0 copy-start.2
  57.0 0.0 copy-start.3
  57.0 0.0 copy-start.5
  57.0 0.0 copy-start.4
  57.0 2.1 %shard_map.102 = (bf16[16,8,512]{2,1,0:T(8,128)(2,1)S(1)}, bf16[8,512]{1,0:T(8,128)(2,1)S(1)}) custom-call(bf16[16,8,384]{2,1,0:T(8,128)(2,1)S(1)} %all-to-all-done.got_ref, bf16[8,512]{1,0:T(8,128)(2,1)S(1)} %collective-permute-done.rim_ref, bf16[16,512]{1,0:T(8,128)(2,1)S(1)} %get-tuple-element.17.edge_ref, ...), custom_call_target="tpu_custom_call" | custom-call | flops 268435456 | bytes 4194304 | tf_op jit(solution)/shard_map/pallas_call | solution.py:323
  59.1 23.4 %all_to_all.15.mix_ref = bf16[16,8,512]{2,1,0:T(8,128)(2,1)S(1)} all-to-all(bf16[16,8,512]{2,1,0:T(8,128)(2,1)S(1)} %get-tuple-element.19), channel_id=1, replica_groups=mesh['seq'=32,'tp'=16] {'tp'}, dimensions={0} | all-to-all | bytes 262144 | tf_op jit(solution)/shard_map/all_to_all | solution.py:393
  82.6 0.0 copy-done.1
  82.6 0.0 copy-done.2
  82.6 0.0 copy-done.3
  82.6 2.2 %shard_map.103 = (f32[128,512]{1,0:T(8,128)S(1)}, f32[128,32]{1,0:T(8,128)S(1)}, bf16[32,72,128]{2,1,0:T(8,128)(2,1)}) custom-call(bf16[16,8,512]{2,1,0:T(8,128)(2,1)S(1)} %all_to_all.15.mix_ref, bf16[256,512]{1,0:T(8,128)(2,1)S(1)} %copy-done.1, f32[1,512]{1,0:T(1,128)S(1)} %bitcast.8, f32[16,512]{1,0:T(8,128)S(1)} %copy-done.2, ...), custom_call_target="tpu_custom_call" | custom-call | flops 67108864 | bytes 1048576 | tf_op jit(solution)/shard_map/pallas_call | solution.py:323
  84.8 10.5 %all-to-all-start.2 = ((bf16[32,72,128]{2,1,0:T(8,128)(2,1)}), bf16[32,72,128]{2,1,0:T(8,128)(2,1)S(1)}, u32[]{:S(2)}, u32[]{:S(2)}) async-start(bf16[32,72,128]{2,1,0:T(8,128)(2,1)} %get-tuple-element.22), calls=%async_computation.2 | async-start | bytes 1179648 | tf_op jit(solution)/shard_map/all_to_all | solution.py:410
  95.3 0.0 copy-done.5
  95.3 3.8 %shard_map.104 = (f32[128,512]{1,0:T(8,128)S(1)}, bf16[8,16,16,512]{3,2,1,0:T(8,128)(2,1)S(1)}) custom-call(f32[128,32]{1,0:T(8,128)S(1)} %get-tuple-element.23.coef_ref, f32[16,512]{1,0:T(8,128)S(1)} %copy-done.2, bf16[128,512]{1,0:T(8,128)(2,1)S(1)} %get-tuple-element.20.u_ref, bf16[8,512]{1,0:T(8,128)(2,1)S(1)} %get-tuple-element.21.late_u_ref, ...), custom_call_target="tpu_custom_call" | custom-call | flops 268435456 | bytes 4194304 | tf_op jit(solution)/shard_map/pallas_call | solution.py:323
  99.1 8.4 %all-to-all-done.2.all_ref = bf16[32,72,128]{2,1,0:T(8,128)(2,1)S(1)} async-done(((bf16[32,72,128]{2,1,0:T(8,128)(2,1)}), bf16[32,72,128]{2,1,0:T(8,128)(2,1)S(1)}, u32[]{:S(2)}, u32[]{:S(2)}) %all-to-all-start.2) | async-done | bytes 589856 | tf_op jit(solution)/shard_map/all_to_all | solution.py:410
  107.5 0.0 copy-done.4
  107.5 1.6 %shard_map.105 = bf16[128,512]{1,0:T(8,128)(2,1)} custom-call(s32[1]{0:T(128)} %bitcast.mine_ref, bf16[32,72,128]{2,1,0:T(8,128)(2,1)S(1)} %all-to-all-done.2.all_ref, f32[16,512]{1,0:T(8,128)S(1)} %copy-done.2, f32[128,512]{1,0:T(8,128)S(1)} %get-tuple-element.25.y_ref, bf16[8,16,16,512]{3,2,1,0:T(8,128)(2,1)S(1)} %get-tuple-element.26.grow_ref, ...), custom_call_target="tpu_custom_call" | custom-call | flops 67108864 | bytes 1048576 | tf_op jit(solution)/shard_map/pallas_call | solution.py:323
  (1 shorter events, 0.0 us)
Async XLA Ops:
  0.0 36.6 %copy-start = (bf16[4096,512]{1,0:T(8,128)(2,1)S(1)}, bf16[4096,512]{1,0:T(8,128)(2,1)}, u32[]{:S(2)}) copy-start(bf16[4096,512]{1,0:T(8,128)(2,1)} %weight_hbm.1) | copy-start | bytes 12582916
  38.7 18.3 %all-to-all-start = ((bf16[16,8,384]{2,1,0:T(8,128)(2,1)}), bf16[16,8,384]{2,1,0:T(8,128)(2,1)S(1)}, u32[]{:S(2)}, u32[]{:S(2)}) async-start(bf16[16,8,384]{2,1,0:T(8,128)(2,1)} %get-tuple-element.16), calls=%async_computation | async-start | bytes 196608 | tf_op jit(solution)/shard_map/all_to_all | solution.py:376
  45.1 11.7 %collective-permute-start = (bf16[8,512]{1,0:T(8,128)(2,1)S(1)}, bf16[8,512]{1,0:T(8,128)(2,1)S(1)}, u32[]{:S(2)}, u32[]{:S(2)}) collective-permute-start(bf16[8,512]{1,0:T(8,128)(2,1)S(1)} %slice.3), channel_id=1, source_target_pairs={{0,16},{16,32},{32,48},{48,64},{64,80},{80,96},{96,112},{112,128},... | collective-permute-start | bytes 24584 | tf_op jit(solution)/shard_map/ppermute | solution.py:375
  57.0 25.6 %copy-start.1 = (bf16[256,512]{1,0:T(8,128)(2,1)S(1)}, bf16[256,512]{1,0:T(8,128)(2,1)}, u32[]{:S(2)}) copy-start(bf16[256,512]{1,0:T(8,128)(2,1)} %dtw_ref.1) | copy-start | bytes 786436
  57.0 25.6 %copy-start.2 = (f32[16,512]{1,0:T(8,128)S(1)}, f32[16,512]{1,0:T(8,128)}, u32[]{:S(2)}) copy-start(f32[16,512]{1,0:T(8,128)} %alog_ref.5) | copy-start | bytes 98308
  57.0 25.6 %copy-start.3 = (f32[512]{0:T(512)S(1)}, f32[512]{0:T(512)}, u32[]{:S(2)}) copy-start(f32[512]{0:T(512)} %param.16) | copy-start | bytes 6148
  57.0 38.3 %copy-start.5 = (f32[512]{0:T(512)S(1)}, f32[512]{0:T(512)}, u32[]{:S(2)}) copy-start(f32[512]{0:T(512)} %param.18) | copy-start | bytes 6148
  57.0 50.5 %copy-start.4 = (f32[512]{0:T(512)S(1)}, f32[512]{0:T(512)}, u32[]{:S(2)}) copy-start(f32[512]{0:T(512)} %param.19) | copy-start | bytes 6148
  84.8 22.7 %all-to-all-start.2 = ((bf16[32,72,128]{2,1,0:T(8,128)(2,1)}), bf16[32,72,128]{2,1,0:T(8,128)(2,1)S(1)}, u32[]{:S(2)}, u32[]{:S(2)}) async-start(bf16[32,72,128]{2,1,0:T(8,128)(2,1)} %get-tuple-element.22), calls=%async_computation.2 | async-start | bytes 1179648 | tf_op jit(solution)/shard_map/all_to_all | solution.py:410

commit v13 on v11

--- a/solution.py
+++ b/solution.py
@@ -342,12 +342,12 @@
         whole = other[at : at + 1, :] + other[at + groups : at + groups + 1, :]
         longer = jnp.exp2(rate_g * whole) * entry + other[g * n : (g + 1) * n, :]
         entry = jnp.where(second_core, longer, entry)
-        entry_g = jnp.broadcast_to(entry[:, None, :], (n, 16, 128))
+        entry_g = jnp.broadcast_to(entry[:, None, :], (n, 16, 128)).astype(BF16)
         thr = thr_ref[:, lanes]
 
         def turn(i, _):
             at = pl.ds(pl.multiple_of(i * 16, 16), 16)
-            y = y_ref[at, lanes] + jnp.sum(grow_ref[i, :, :, lanes].astype(F32) * entry_g, axis=0)
+            y = y_ref[at, lanes] + jnp.sum((grow_ref[i, :, :, lanes] * entry_g).astype(F32), axis=0)
             out_ref[at, lanes] = (y / (1.0 + jnp.exp(-4.0 * (y - thr)))).astype(BF16)
             return 0
 

time: 110 us -> 110 us (level)
  no operation moved by 1% of the time
where the time goes in v13:
time: 110 us; the launch traced here: 109 us
  blocking collectives  59 us (54%)
  starting transfers between devices  30.1 us (27%)
  Pallas kernels  12.5 us (11%)
  waiting for transfers between devices  7.38 us (7%)
    all_gather x1, blocking collectives, per_device(): main = lax.all_gather(most, 'tp')  35.6 us
    all_to_all x1, blocking collectives, per_device(): mix = lax.all_to_all(mix, 'tp', 0, 0)  23.4 us
    pallas_call x7, Pallas kernels, call(): pl.pallas_call(kernel, out_shape=outs, in_specs=specs, out_specs=outs_in...  12.5 us
    ppermute x1, starting transfers between devices, per_device(): rim = lax.ppermute(edge[:8], 'seq', [(i, i + 1) for i in range(peers - 1)])  10.9 us
    all_to_all x1, starting transfers between devices, per_device(): everyone = lax.all_to_all(pay, 'seq', 0, 0)  7.13 us
    all_to_all x1, starting transfers between devices, per_device(): got = lax.all_to_all(send, 'tp', 0, 0)  6.41 us
    all_to_all x1, waiting for transfers between devices, per_device(): everyone = lax.all_to_all(pay, 'seq', 0, 0)  5.68 us
    ppermute x1, starting transfers between devices, per_device(): other = lax.ppermute(own, 'seq', [(i, i ^ 1) for i in range(peers)])  5.6 us
  transfers between devices with their start and end apart: 4, of which 4 were waited for; matrix products, arithmetic and copies ran while one was open for 0% of the time, Pallas kernels for 4%

profile of v13, /device:TPU:1, one launch (start us, length us, event | category | flops | bytes accessed | tf_op | source)
XLA Modules:
  0.0 109.1 jit_solution(7273673927602567459)
XLA Ops:
  0.0 0.0 copy-start
  0.0 1.0 shard_map.100
  1.0 35.6 %all-gather.1.main_ref = bf16[16,127,256]{2,1,0:T(8,128)(2,1)S(1)} all-gather(bf16[1,127,256]{2,1,0:T(8,128)(2,1)S(1)} %bitcast.7), channel_id=2, replica_groups=mesh['seq'=32,'tp'=16] {'tp'}, dimensions={0}, use_global_device_ids=true | all-gather | bytes 1105408 | tf_op jit(solution)/shard_map/all_gather | solution.py:399
  36.6 0.0 copy-done
  36.6 2.1 %shard_map.101 = (bf16[16,8,384]{2,1,0:T(8,128)(2,1)}, bf16[16,512]{1,0:T(8,128)(2,1)S(1)}, bf16[128,512]{1,0:T(8,128)(2,1)S(1)}, bf16[3072,512]{1,0:T(8,128)(2,1)S(1)}) custom-call(bf16[16,127,256]{2,1,0:T(8,128)(2,1)S(1)} %all-gather.1.main_ref, bf16[4096,512]{1,0:T(8,128)(2,1)S(1)} %copy-done, bf16[128,256]{1,0:T(8,128)(2,1)} %tokens_hbm.3, ...), custom_call_target="tpu_custom_call" | custom-call | flops 536870912 | bytes 8388608 | tf_op jit(solution)/shard_map/pallas_call | solution.py:359
  38.7 6.4 %all-to-all-start = ((bf16[16,8,384]{2,1,0:T(8,128)(2,1)}), bf16[16,8,384]{2,1,0:T(8,128)(2,1)S(1)}, u32[]{:S(2)}, u32[]{:S(2)}) async-start(bf16[16,8,384]{2,1,0:T(8,128)(2,1)} %get-tuple-element.18), calls=%async_computation | async-start | bytes 196608 | tf_op jit(solution)/shard_map/all_to_all | solution.py:412
  45.1 10.9 %collective-permute-start = (bf16[8,512]{1,0:T(8,128)(2,1)S(1)}, bf16[8,512]{1,0:T(8,128)(2,1)S(1)}, u32[]{:S(2)}, u32[]{:S(2)}) collective-permute-start(bf16[8,512]{1,0:T(8,128)(2,1)S(1)} %slice.3), channel_id=1, source_target_pairs={{0,16},{16,32},{32,48},{48,64},{64,80},{80,96},{96,112},{112,128},... | collective-permute-start | bytes 24584 | tf_op jit(solution)/shard_map/ppermute | solution.py:411
  56.1 0.8 collective-permute-done.rim_ref
  56.9 0.1 all-to-all-done.got_ref
  57.0 0.0 copy-start.1
  57.0 0.0 copy-start.2
  57.0 0.0 copy-start.3
  57.0 0.0 copy-start.5
  57.0 0.0 copy-start.4
  57.0 2.1 %shard_map.102 = (bf16[16,8,512]{2,1,0:T(8,128)(2,1)S(1)}, bf16[8,512]{1,0:T(8,128)(2,1)S(1)}) custom-call(bf16[16,8,384]{2,1,0:T(8,128)(2,1)S(1)} %all-to-all-done.got_ref, bf16[8,512]{1,0:T(8,128)(2,1)S(1)} %collective-permute-done.rim_ref, bf16[16,512]{1,0:T(8,128)(2,1)S(1)} %get-tuple-element.19.edge_ref, ...), custom_call_target="tpu_custom_call" | custom-call | flops 268435456 | bytes 4194304 | tf_op jit(solution)/shard_map/pallas_call | solution.py:359
  59.1 23.4 %all_to_all.15.mix_ref = bf16[16,8,512]{2,1,0:T(8,128)(2,1)S(1)} all-to-all(bf16[16,8,512]{2,1,0:T(8,128)(2,1)S(1)} %get-tuple-element.21), channel_id=1, replica_groups=mesh['seq'=32,'tp'=16] {'tp'}, dimensions={0} | all-to-all | bytes 262144 | tf_op jit(solution)/shard_map/all_to_all | solution.py:429
  82.6 0.0 copy-done.1
  82.6 0.0 copy-done.2
  82.6 0.0 copy-done.3
  82.6 1.3 %shard_map.103 = (f32[128,512]{1,0:T(8,128)S(1)}, f32[128,32]{1,0:T(8,128)S(1)}, bf16[72,128]{1,0:T(8,128)(2,1)S(1)}) custom-call(bf16[16,8,512]{2,1,0:T(8,128)(2,1)S(1)} %all_to_all.15.mix_ref, bf16[256,512]{1,0:T(8,128)(2,1)S(1)} %copy-done.2, f32[1,512]{1,0:T(1,128)S(1)} %bitcast.8, f32[16,512]{1,0:T(8,128)S(1)} %copy-done.1, ...), custom_call_target="tpu_custom_call" | custom-call | flops 67108864 | bytes 1048576 | tf_op jit(solution)/shard_map/pallas_call | solution.py:359
  83.9 5.6 %collective-permute-start.1 = (bf16[72,128]{1,0:T(8,128)(2,1)S(1)}, bf16[72,128]{1,0:T(8,128)(2,1)S(1)}, u32[]{:S(2)}, u32[]{:S(2)}) collective-permute-start(bf16[72,128]{1,0:T(8,128)(2,1)S(1)} %get-tuple-element.24.own_ref), channel_id=1, source_target_pairs={{0,16},{16,0},{32,48},{48,32},{64,80},{80,64},{96,112},{112,96},{1... | collective-permute-start | bytes 55304 | tf_op jit(solution)/shard_map/ppermute | solution.py:446
  89.5 0.8 collective-permute-done.1.other_ref
  90.3 0.8 shard_map.104
  91.1 7.1 %all-to-all-start.2 = ((bf16[32,36,128]{2,1,0:T(8,128)(2,1)}), bf16[32,36,128]{2,1,0:T(8,128)(2,1)S(1)}, u32[]{:S(2)}, u32[]{:S(2)}) async-start(bf16[32,36,128]{2,1,0:T(8,128)(2,1)} %shard_map.104), calls=%async_computation.2 | async-start | bytes 655360 | tf_op jit(solution)/shard_map/all_to_all | solution.py:457
  98.2 0.0 copy-done.5
  98.2 3.8 %shard_map.105 = (f32[128,512]{1,0:T(8,128)S(1)}, bf16[8,16,16,512]{3,2,1,0:T(8,128)(2,1)S(1)}) custom-call(f32[128,32]{1,0:T(8,128)S(1)} %get-tuple-element.27.coef_ref, f32[16,512]{1,0:T(8,128)S(1)} %copy-done.1, bf16[128,512]{1,0:T(8,128)(2,1)S(1)} %get-tuple-element.22.u_ref, bf16[8,512]{1,0:T(8,128)(2,1)S(1)} %get-tuple-element.23.late_u_ref, ...), custom_call_target="tpu_custom_call" | custom-call | flops 268435456 | bytes 4194304 | tf_op jit(solution)/shard_map/pallas_call | solution.py:359
  102.1 5.7 %all-to-all-done.2.all_ref = bf16[32,36,128]{2,1,0:T(8,128)(2,1)S(1)} async-done(((bf16[32,36,128]{2,1,0:T(8,128)(2,1)}), bf16[32,36,128]{2,1,0:T(8,128)(2,1)S(1)}, u32[]{:S(2)}, u32[]{:S(2)}) %all-to-all-start.2) | async-done | bytes 294944 | tf_op jit(solution)/shard_map/all_to_all | solution.py:457
  107.8 0.0 copy-done.4
  107.8 1.4 %shard_map.106 = bf16[128,512]{1,0:T(8,128)(2,1)} custom-call(s32[1]{0:T(128)} %bitcast.mine_ref, bf16[32,36,128]{2,1,0:T(8,128)(2,1)S(1)} %all-to-all-done.2.all_ref, bf16[72,128]{1,0:T(8,128)(2,1)S(1)} %collective-permute-done.1.other_ref, f32[16,512]{1,0:T(8,128)S(1)} %copy-done.1, f32[128,512]{1,0:T(8,128)S(1)} %get-tuple-element.29.y_ref, ...), custom_call_target="tpu_custom_call" | custom-call | flops 67108864 | bytes 1048576 | tf_op jit(solution)/shard_map/pallas_call | solution.py:359
  (1 shorter events, 0.0 us)
Async XLA Ops:
  0.0 36.6 %copy-start = (bf16[4096,512]{1,0:T(8,128)(2,1)S(1)}, bf16[4096,512]{1,0:T(8,128)(2,1)}, u32[]{:S(2)}) copy-start(bf16[4096,512]{1,0:T(8,128)(2,1)} %weight_hbm.1) | copy-start | bytes 12582916
  38.7 18.3 %all-to-all-start = ((bf16[16,8,384]{2,1,0:T(8,128)(2,1)}), bf16[16,8,384]{2,1,0:T(8,128)(2,1)S(1)}, u32[]{:S(2)}, u32[]{:S(2)}) async-start(bf16[16,8,384]{2,1,0:T(8,128)(2,1)} %get-tuple-element.18), calls=%async_computation | async-start | bytes 196608 | tf_op jit(solution)/shard_map/all_to_all | solution.py:412
  45.1 11.7 %collective-permute-start = (bf16[8,512]{1,0:T(8,128)(2,1)S(1)}, bf16[8,512]{1,0:T(8,128)(2,1)S(1)}, u32[]{:S(2)}, u32[]{:S(2)}) collective-permute-start(bf16[8,512]{1,0:T(8,128)(2,1)S(1)} %slice.3), channel_id=1, source_target_pairs={{0,16},{16,32},{32,48},{48,64},{64,80},{80,96},{96,112},{112,128},... | collective-permute-start | bytes 24584 | tf_op jit(solution)/shard_map/ppermute | solution.py:411
  57.0 25.6 %copy-start.1 = (f32[16,512]{1,0:T(8,128)S(1)}, f32[16,512]{1,0:T(8,128)}, u32[]{:S(2)}) copy-start(f32[16,512]{1,0:T(8,128)} %alog_ref.7) | copy-start | bytes 98308
  57.0 25.6 %copy-start.2 = (bf16[256,512]{1,0:T(8,128)(2,1)S(1)}, bf16[256,512]{1,0:T(8,128)(2,1)}, u32[]{:S(2)}) copy-start(bf16[256,512]{1,0:T(8,128)(2,1)} %dtw_ref.1) | copy-start | bytes 786436
  57.0 25.6 %copy-start.3 = (f32[512]{0:T(512)S(1)}, f32[512]{0:T(512)}, u32[]{:S(2)}) copy-start(f32[512]{0:T(512)} %param.16) | copy-start | bytes 6148
  57.0 41.3 %copy-start.5 = (f32[512]{0:T(512)S(1)}, f32[512]{0:T(512)}, u32[]{:S(2)}) copy-start(f32[512]{0:T(512)} %param.18) | copy-start | bytes 6148
  57.0 50.8 %copy-start.4 = (f32[512]{0:T(512)S(1)}, f32[512]{0:T(512)}, u32[]{:S(2)}) copy-start(f32[512]{0:T(512)} %param.19) | copy-start | bytes 6148
  83.9 6.4 %collective-permute-start.1 = (bf16[72,128]{1,0:T(8,128)(2,1)S(1)}, bf16[72,128]{1,0:T(8,128)(2,1)S(1)}, u32[]{:S(2)}, u32[]{:S(2)}) collective-permute-start(bf16[72,128]{1,0:T(8,128)(2,1)S(1)} %get-tuple-element.24.own_ref), channel_id=1, source_target_pairs={{0,16},{16,0},{32,48},{48,32},{64,80},{80,64},{96,112},{112,96},{1... | collective-permute-start | bytes 55304 | tf_op jit(solution)/shard_map/ppermute | solution.py:446
  91.1 16.7 %all-to-all-start.2 = ((bf16[32,36,128]{2,1,0:T(8,128)(2,1)}), bf16[32,36,128]{2,1,0:T(8,128)(2,1)S(1)}, u32[]{:S(2)}, u32[]{:S(2)}) async-start(bf16[32,36,128]{2,1,0:T(8,128)(2,1)} %shard_map.104), calls=%async_computation.2 | async-start | bytes 655360 | tf_op jit(solution)/shard_map/all_to_all | solution.py:457

commit v14 on v11

--- a/solution.py
+++ b/solution.py
@@ -40,7 +40,7 @@
     return lax.dot_general(u, proj_ref[...], (((1,), (1,)), ((), ())), preferred_element_type=F32)
 
 
-KEEP = 12
+KEEP = 11
 
 
 def fetches(pairs, sems):

time: 110 us -> 109 us (level)
  no operation moved by 1% of the time
where the time goes in v14:
time: 109 us
  blocking collectives  59 us (54%)
  starting transfers between devices  30.1 us (28%)
  Pallas kernels  12.5 us (11%)
  waiting for transfers between devices  7.37 us (7%)
    all_gather x1, blocking collectives, per_device(): main = lax.all_gather(most, 'tp')  35.6 us
    all_to_all x1, blocking collectives, per_device(): mix = lax.all_to_all(mix, 'tp', 0, 0)  23.4 us
    pallas_call x7, Pallas kernels, call(): pl.pallas_call(kernel, out_shape=outs, in_specs=specs, out_specs=outs_in...  12.5 us
    ppermute x1, starting transfers between devices, per_device(): rim = lax.ppermute(edge[:8], 'seq', [(i, i + 1) for i in range(peers - 1)])  10.9 us
    all_to_all x1, starting transfers between devices, per_device(): everyone = lax.all_to_all(pay, 'seq', 0, 0)  7.14 us
    all_to_all x1, starting transfers between devices, per_device(): got = lax.all_to_all(send, 'tp', 0, 0)  6.41 us
    all_to_all x1, waiting for transfers between devices, per_device(): everyone = lax.all_to_all(pay, 'seq', 0, 0)  5.67 us
    ppermute x1, starting transfers between devices, per_device(): other = lax.ppermute(own, 'seq', [(i, i ^ 1) for i in range(peers)])  5.58 us
  transfers between devices with their start and end apart: 4, of which 4 were waited for; matrix products, arithmetic and copies ran while one was open for 0% of the time, Pallas kernels for 4%

profile of v14, /device:TPU:1, one launch (start us, length us, event | category | flops | bytes accessed | tf_op | source)
XLA Modules:
  0.0 109.1 jit_solution(13100786472904499556)
XLA Ops:
  0.0 0.0 copy-start
  0.0 1.0 shard_map.100
  1.0 35.6 %all-gather.1.main_ref = bf16[16,127,256]{2,1,0:T(8,128)(2,1)S(1)} all-gather(bf16[1,127,256]{2,1,0:T(8,128)(2,1)S(1)} %bitcast.7), channel_id=2, replica_groups=mesh['seq'=32,'tp'=16] {'tp'}, dimensions={0}, use_global_device_ids=true | all-gather | bytes 1105408 | tf_op jit(solution)/shard_map/all_gather | solution.py:399
  36.6 0.0 copy-done
  36.6 2.1 %shard_map.101 = (bf16[16,8,384]{2,1,0:T(8,128)(2,1)}, bf16[16,512]{1,0:T(8,128)(2,1)S(1)}, bf16[128,512]{1,0:T(8,128)(2,1)S(1)}, bf16[2816,512]{1,0:T(8,128)(2,1)S(1)}) custom-call(bf16[16,127,256]{2,1,0:T(8,128)(2,1)S(1)} %all-gather.1.main_ref, bf16[4096,512]{1,0:T(8,128)(2,1)S(1)} %copy-done, bf16[128,256]{1,0:T(8,128)(2,1)} %tokens_hbm.3, ...), custom_call_target="tpu_custom_call" | custom-call | flops 536870912 | bytes 8388608 | tf_op jit(solution)/shard_map/pallas_call | solution.py:359
  38.7 6.4 %all-to-all-start = ((bf16[16,8,384]{2,1,0:T(8,128)(2,1)}), bf16[16,8,384]{2,1,0:T(8,128)(2,1)S(1)}, u32[]{:S(2)}, u32[]{:S(2)}) async-start(bf16[16,8,384]{2,1,0:T(8,128)(2,1)} %get-tuple-element.18), calls=%async_computation | async-start | bytes 196608 | tf_op jit(solution)/shard_map/all_to_all | solution.py:412
  45.1 10.9 %collective-permute-start = (bf16[8,512]{1,0:T(8,128)(2,1)S(1)}, bf16[8,512]{1,0:T(8,128)(2,1)S(1)}, u32[]{:S(2)}, u32[]{:S(2)}) collective-permute-start(bf16[8,512]{1,0:T(8,128)(2,1)S(1)} %slice.3), channel_id=1, source_target_pairs={{0,16},{16,32},{32,48},{48,64},{64,80},{80,96},{96,112},{112,128},... | collective-permute-start | bytes 24584 | tf_op jit(solution)/shard_map/ppermute | solution.py:411
  56.1 0.8 collective-permute-done.rim_ref
  56.9 0.1 all-to-all-done.got_ref
  57.0 0.0 copy-start.1
  57.0 0.0 copy-start.2
  57.0 0.0 copy-start.3
  57.0 0.0 copy-start.5
  57.0 2.0 %shard_map.102 = (bf16[16,8,512]{2,1,0:T(8,128)(2,1)S(1)}, bf16[8,512]{1,0:T(8,128)(2,1)S(1)}) custom-call(bf16[16,8,384]{2,1,0:T(8,128)(2,1)S(1)} %all-to-all-done.got_ref, bf16[8,512]{1,0:T(8,128)(2,1)S(1)} %collective-permute-done.rim_ref, bf16[16,512]{1,0:T(8,128)(2,1)S(1)} %get-tuple-element.19.edge_ref, ...), custom_call_target="tpu_custom_call" | custom-call | flops 268435456 | bytes 4194304 | tf_op jit(solution)/shard_map/pallas_call | solution.py:359
  59.0 0.0 copy-start.4
  59.0 23.4 %all_to_all.15.mix_ref = bf16[16,8,512]{2,1,0:T(8,128)(2,1)S(1)} all-to-all(bf16[16,8,512]{2,1,0:T(8,128)(2,1)S(1)} %get-tuple-element.21), channel_id=1, replica_groups=mesh['seq'=32,'tp'=16] {'tp'}, dimensions={0} | all-to-all | bytes 262144 | tf_op jit(solution)/shard_map/all_to_all | solution.py:429
  82.5 0.0 copy-done.1
  82.5 0.0 copy-done.2
  82.5 0.0 copy-done.3
  82.5 1.3 %shard_map.103 = (f32[128,512]{1,0:T(8,128)S(1)}, f32[128,32]{1,0:T(8,128)S(1)}, bf16[72,128]{1,0:T(8,128)(2,1)S(1)}) custom-call(bf16[16,8,512]{2,1,0:T(8,128)(2,1)S(1)} %all_to_all.15.mix_ref, bf16[256,512]{1,0:T(8,128)(2,1)S(1)} %copy-done.2, f32[1,512]{1,0:T(1,128)S(1)} %bitcast.8, f32[16,512]{1,0:T(8,128)S(1)} %copy-done.1, ...), custom_call_target="tpu_custom_call" | custom-call | flops 67108864 | bytes 1048576 | tf_op jit(solution)/shard_map/pallas_call | solution.py:359
  83.8 5.6 %collective-permute-start.1 = (bf16[72,128]{1,0:T(8,128)(2,1)S(1)}, bf16[72,128]{1,0:T(8,128)(2,1)S(1)}, u32[]{:S(2)}, u32[]{:S(2)}) collective-permute-start(bf16[72,128]{1,0:T(8,128)(2,1)S(1)} %get-tuple-element.24.own_ref), channel_id=1, source_target_pairs={{0,16},{16,0},{32,48},{48,32},{64,80},{80,64},{96,112},{112,96},{1... | collective-permute-start | bytes 55304 | tf_op jit(solution)/shard_map/ppermute | solution.py:446
  89.4 0.8 collective-permute-done.1.other_ref
  90.2 0.8 shard_map.104
  91.0 7.1 %all-to-all-start.2 = ((bf16[32,36,128]{2,1,0:T(8,128)(2,1)}), bf16[32,36,128]{2,1,0:T(8,128)(2,1)S(1)}, u32[]{:S(2)}, u32[]{:S(2)}) async-start(bf16[32,36,128]{2,1,0:T(8,128)(2,1)} %shard_map.104), calls=%async_computation.2 | async-start | bytes 655360 | tf_op jit(solution)/shard_map/all_to_all | solution.py:457
  98.1 0.0 copy-done.5
  98.1 3.8 %shard_map.105 = (f32[128,512]{1,0:T(8,128)S(1)}, bf16[8,16,16,512]{3,2,1,0:T(8,128)(2,1)S(1)}) custom-call(f32[128,32]{1,0:T(8,128)S(1)} %get-tuple-element.27.coef_ref, f32[16,512]{1,0:T(8,128)S(1)} %copy-done.1, bf16[128,512]{1,0:T(8,128)(2,1)S(1)} %get-tuple-element.22.u_ref, bf16[8,512]{1,0:T(8,128)(2,1)S(1)} %get-tuple-element.23.late_u_ref, ...), custom_call_target="tpu_custom_call" | custom-call | flops 268435456 | bytes 4194304 | tf_op jit(solution)/shard_map/pallas_call | solution.py:359
  102.0 5.7 %all-to-all-done.2.all_ref = bf16[32,36,128]{2,1,0:T(8,128)(2,1)S(1)} async-done(((bf16[32,36,128]{2,1,0:T(8,128)(2,1)}), bf16[32,36,128]{2,1,0:T(8,128)(2,1)S(1)}, u32[]{:S(2)}, u32[]{:S(2)}) %all-to-all-start.2) | async-done | bytes 294944 | tf_op jit(solution)/shard_map/all_to_all | solution.py:457
  107.7 0.0 copy-done.4
  107.7 1.4 %shard_map.106 = bf16[128,512]{1,0:T(8,128)(2,1)} custom-call(s32[1]{0:T(128)} %bitcast.mine_ref, bf16[32,36,128]{2,1,0:T(8,128)(2,1)S(1)} %all-to-all-done.2.all_ref, bf16[72,128]{1,0:T(8,128)(2,1)S(1)} %collective-permute-done.1.other_ref, f32[16,512]{1,0:T(8,128)S(1)} %copy-done.1, f32[128,512]{1,0:T(8,128)S(1)} %get-tuple-element.29.y_ref, ...), custom_call_target="tpu_custom_call" | custom-call | flops 67108864 | bytes 1048576 | tf_op jit(solution)/shard_map/pallas_call | solution.py:359
  (1 shorter events, 0.0 us)
Async XLA Ops:
  0.0 36.6 %copy-start = (bf16[4096,512]{1,0:T(8,128)(2,1)S(1)}, bf16[4096,512]{1,0:T(8,128)(2,1)}, u32[]{:S(2)}) copy-start(bf16[4096,512]{1,0:T(8,128)(2,1)} %weight_hbm.1) | copy-start | bytes 12582916
  38.7 18.3 %all-to-all-start = ((bf16[16,8,384]{2,1,0:T(8,128)(2,1)}), bf16[16,8,384]{2,1,0:T(8,128)(2,1)S(1)}, u32[]{:S(2)}, u32[]{:S(2)}) async-start(bf16[16,8,384]{2,1,0:T(8,128)(2,1)} %get-tuple-element.18), calls=%async_computation | async-start | bytes 196608 | tf_op jit(solution)/shard_map/all_to_all | solution.py:412
  45.1 11.7 %collective-permute-start = (bf16[8,512]{1,0:T(8,128)(2,1)S(1)}, bf16[8,512]{1,0:T(8,128)(2,1)S(1)}, u32[]{:S(2)}, u32[]{:S(2)}) collective-permute-start(bf16[8,512]{1,0:T(8,128)(2,1)S(1)} %slice.3), channel_id=1, source_target_pairs={{0,16},{16,32},{32,48},{48,64},{64,80},{80,96},{96,112},{112,128},... | collective-permute-start | bytes 24584 | tf_op jit(solution)/shard_map/ppermute | solution.py:411
  57.0 25.5 %copy-start.1 = (f32[16,512]{1,0:T(8,128)S(1)}, f32[16,512]{1,0:T(8,128)}, u32[]{:S(2)}) copy-start(f32[16,512]{1,0:T(8,128)} %alog_ref.7) | copy-start | bytes 98308
  57.0 25.5 %copy-start.2 = (bf16[256,512]{1,0:T(8,128)(2,1)S(1)}, bf16[256,512]{1,0:T(8,128)(2,1)}, u32[]{:S(2)}) copy-start(bf16[256,512]{1,0:T(8,128)(2,1)} %dtw_ref.1) | copy-start | bytes 786436
  57.0 25.5 %copy-start.3 = (f32[512]{0:T(512)S(1)}, f32[512]{0:T(512)}, u32[]{:S(2)}) copy-start(f32[512]{0:T(512)} %param.16) | copy-start | bytes 6148
  57.0 41.2 %copy-start.5 = (f32[512]{0:T(512)S(1)}, f32[512]{0:T(512)}, u32[]{:S(2)}) copy-start(f32[512]{0:T(512)} %param.18) | copy-start | bytes 6148
  59.0 48.6 %copy-start.4 = (f32[512]{0:T(512)S(1)}, f32[512]{0:T(512)}, u32[]{:S(2)}) copy-start(f32[512]{0:T(512)} %param.19) | copy-start | bytes 6148
  83.8 6.4 %collective-permute-start.1 = (bf16[72,128]{1,0:T(8,128)(2,1)S(1)}, bf16[72,128]{1,0:T(8,128)(2,1)S(1)}, u32[]{:S(2)}, u32[]{:S(2)}) collective-permute-start(bf16[72,128]{1,0:T(8,128)(2,1)S(1)} %get-tuple-element.24.own_ref), channel_id=1, source_target_pairs={{0,16},{16,0},{32,48},{48,32},{64,80},{80,64},{96,112},{112,96},{1... | collective-permute-start | bytes 55304 | tf_op jit(solution)/shard_map/ppermute | solution.py:446
  91.0 16.7 %all-to-all-start.2 = ((bf16[32,36,128]{2,1,0:T(8,128)(2,1)}), bf16[32,36,128]{2,1,0:T(8,128)(2,1)S(1)}, u32[]{:S(2)}, u32[]{:S(2)}) async-start(bf16[32,36,128]{2,1,0:T(8,128)(2,1)} %shard_map.104), calls=%async_computation.2 | async-start | bytes 655360 | tf_op jit(solution)/shard_map/all_to_all | solution.py:457
